TPU v7x, 512 devices: a whole 4x8x8 slice. The times are simulated.
512 devices in a mesh: group: 2 (over y_lo), seq: 32 (over x, y_hi, core), mp: 8 (over z).
Axes of the slice: x: 4, y: 8 (y_hi: 4, y_lo: 2; y = y_hi * 2 + y_lo), z: 8, core: 2. Of those that a mesh axis runs over, the one named last changes fastest.
Arguments:
- student_hidden: bfloat16 [2, 4096, 3072], P('group', 'seq', 'mp'), may hold values from -6 to 6
- student_cond: float32 [2, 3072], P(None, 'seq'), may hold values from -6 to 6
- student_mod: bfloat16 [3072, 2, 3072], P('seq', 'group', 'mp'), may hold values from -0.109375 to 0.109375
- student_out: bfloat16 [3072, 64], P('mp'), may hold values from -0.109375 to 0.109375
- timestep: int32 [2], P('group'), may hold values from 0 to 999
- noise: bfloat16 [2, 4096, 64], P('group', 'seq'), may hold values from -6 to 6
- teacher_embed: bfloat16 [64, 3072], P(None, 'mp'), may hold values from -0.75 to 0.75
- teacher_mod: bfloat16 [256, 2, 3072], P(None, None, 'mp'), may hold values from -0.375 to 0.375
- up_weight: bfloat16 [3072, 6144], P('seq', 'mp'), may hold values from -0.109375 to 0.109375
- down_weight: bfloat16 [6144, 3072], P('mp', 'seq'), may hold values from -0.078125 to 0.078125
- head_proj: bfloat16 [4, 3072, 128], P(None, 'mp'), may hold values from -0.109375 to 0.109375
- head_kernel: float32 [4, 3, 3, 128], replicated, may hold values from -3 to 3
- head_out: float32 [4, 128], replicated, may hold values from -2 to 2
- disc_layer: int32 [2, 4], P('group'), may hold values from 0 to 1, as said below
Outputs:
- latents: bfloat16 [2, 4096, 64], P('group', 'seq')
- logits: float32 [2, 4, 4096], P('group', None, 'seq')
- latent_grad: float32 [2, 4096, 64], P('group', 'seq')
Inputs may be any that keep to these rules, and one draw needn't show every extreme that they name: `disc_layer`: for every sample, exactly half of the 4 heads read layer 0 and the other half layer 1, in an order drawn afresh.
All inputs are finite; a program needn't handle non-finite values.
Results may differ from a plain program's by a relative error of at most 0.029.
Values may be sent and summed in bfloat16 or wider, within the bound.
No kernel may reach another device: no remote copies, remote signals or barrier semaphores. Data moves between devices by JAX's collectives and lax.ppermute only.
A program may use at most 64 MiB of HBM per device.

v0:
```python
import functools
import math

import jax
import jax.numpy as jnp
from jax import lax
from jax.experimental import pallas as pl
from jax.experimental.pallas import tpu as pltpu
from jax.sharding import PartitionSpec as P


GRID_W = 64
EPSILON = 1e-06
GELU_COEF = 0.7978845608028654
INTERPRET = False

F32 = jnp.float32
BF16 = jnp.bfloat16
HIGHEST = lax.Precision.HIGHEST


def contract(left, right, left_dim, right_dim, precision=None):
    return lax.dot_general(
        left,
        right,
        (((left_dim,), (right_dim,)), ((), ())),
        precision=precision,
        preferred_element_type=F32,
    )


def gelu_tanh(values):
    inner = GELU_COEF * (values + 0.044715 * values * values * values)
    return 0.5 * values * (1.0 + jnp.tanh(inner))


def gelu_slope(values):
    inner = GELU_COEF * (values + 0.044715 * values * values * values)
    tangent = jnp.tanh(inner)
    return 0.5 * (1.0 + tangent) + 0.5 * values * (1.0 - tangent * tangent) * GELU_COEF * (
        1.0 + 3.0 * 0.044715 * values * values
    )


def time_features(timestep, width):
    half_width = width // 2
    index = jnp.arange(half_width, dtype=F32)
    freqs = jnp.exp(-math.log(10000.0) * index / half_width)
    angles = timestep.astype(F32)[:, None] * freqs[None, :]
    return jnp.concatenate([jnp.cos(angles), jnp.sin(angles)], axis=-1)


def exchange(value, axes):
    return lax.all_to_all(value, axes, 0, 0, tiled=False)


def call(body, outs, scalars, arrays, scratch=(), loose=()):
    smem = pl.BlockSpec(memory_space=pltpu.SMEM)
    vmem = pl.BlockSpec(memory_space=pltpu.VMEM)
    if INTERPRET:
        shapes = [jax.ShapeDtypeStruct(shape, dtype) for shape, dtype in outs]
    else:
        shapes = [
            jax.ShapeDtypeStruct(*out) if place in loose else pltpu.VMEM(*out)
            for place, out in enumerate(outs)
        ]
        arrays = [pltpu.with_memory_space_constraint(value, pltpu.VMEM) for value in arrays]
    return pl.pallas_call(
        body,
        in_specs=[smem] * len(scalars) + [vmem] * len(arrays),
        out_specs=[vmem] * len(outs),
        out_shape=shapes,
        scratch_shapes=[pltpu.VMEM(shape, dtype) for shape, dtype in scratch],
        interpret=INTERPRET,
    )(*scalars, *arrays)


def pick_heads(disc_ref):
    picks = [disc_ref[0, k] for k in range(4)]
    pairs = []
    for layer in (1, 0):
        first = jnp.where(picks[0] == layer, 0, jnp.where(picks[1] == layer, 1, 2))
        last = jnp.where(picks[3] == layer, 3, jnp.where(picks[2] == layer, 2, 1))
        pairs.append((first, last))
    return pairs


def level_of(time_ref):
    return time_ref[0].astype(F32) / 1000.0


def smod_body(cond_ref, mod_ref, out_ref):
    groups = cond_ref.shape[0]
    copies, pieces, lanes = out_ref.shape
    seqs = copies // groups
    half = contract(cond_ref[...], mod_ref[...].astype(F32), 1, 0, HIGHEST)
    for group in range(groups):
        row = half[group : group + 1]
        block = jnp.concatenate(
            [row[:, lanes * p : lanes * (p + 1)] for p in range(pieces)], axis=0
        )
        out_ref[seqs * group : seqs * (group + 1)] = jnp.broadcast_to(block[None], (seqs, pieces, lanes))


def prep_body(disc_ref, tmod_ref, embed_ref, proj_ref, out_ref, turned_ref):
    rows = out_ref.shape[0]
    channels = proj_ref.shape[2]
    width = embed_ref.shape[1]
    latent = embed_ref.shape[0]
    start = (lax.axis_index("seq") % (width // rows)) * rows
    gain = 1.0 + tmod_ref[1:2]
    queries = jnp.concatenate(
        [
            embed_ref[...].astype(F32) * gain,
            gain,
            tmod_ref[0:1],
            jnp.zeros((128 - latent - 2, width), F32),
        ],
        axis=0,
    )
    turned_ref[...] = queries.T
    out_ref[:, 2 * channels :] = turned_ref[pl.ds(start, rows), :].astype(BF16)
    for place, head in enumerate(pick_heads(disc_ref)[0]):
        out_ref[:, channels * place : channels * (place + 1)] = proj_ref[head, pl.ds(start, rows), :]


def weight_body(got_ref, down_ref, up_ref, order_ref, out_ref):
    del order_ref
    copies, rows, lanes = out_ref.shape
    split = lanes - 128
    terms = jnp.concatenate(
        [
            contract(down_ref[...], got_ref[:, :split], 0, 0),
            contract(up_ref[...], got_ref[:, split:], 0, 0),
        ],
        axis=1,
    )
    out_ref[...] = terms.astype(BF16).reshape(copies, rows, lanes)


def gather_body(parts_ref, order_ref, out_ref):
    del order_ref
    total = jnp.sum(parts_ref[...].astype(F32), axis=0).astype(BF16)
    out_ref[...] = jnp.broadcast_to(total[None], out_ref.shape)


def cross_body(disc_ref, proj_ref, embed_ref, table_ref, cross_ref, taps_ref, turned_ref):
    _, share, lanes = cross_ref.shape
    channels = proj_ref.shape[2]
    per_head = channels // share
    begin = lax.axis_index("mp") * share
    slot = begin // channels
    offset = pl.multiple_of(begin % channels, 8)
    embed = embed_ref[...]
    block, other = pick_heads(disc_ref)
    for place in range(2):
        both = jnp.concatenate(
            [contract(proj_ref[head], embed, 0, 1) for head in (block[place], other[place])], axis=1
        )
        cross_ref[per_head * place : per_head * (place + 1)] = (
            both.astype(BF16).reshape(per_head, share, lanes)
        )
    for place, pair in enumerate((block, other)):
        turned_ref[...] = table_ref[jnp.where(slot == 0, pair[0], pair[1])].T
        taps_ref[share * place : share * (place + 1)] = turned_ref[pl.ds(offset, share), :]


def sums_body(hidden_ref, out_w_ref, embed_ref, mod_ref, sums_ref):
    copies, pieces, _ = mod_ref.shape
    latent, width = out_w_ref.shape
    tokens = hidden_ref.shape[0]
    halves = []
    for half in range(2):
        total = jnp.sum(mod_ref[copies // 2 * half : copies // 2 * (half + 1)], axis=0)
        halves.append(jnp.concatenate([total[p : p + 1] for p in range(pieces)], axis=1))
    shift, scale = halves
    hidden = hidden_ref[...]
    embed = embed_ref[...]
    out_w = out_w_ref[...].astype(F32)
    scaled = (out_w * (1.0 + scale)).astype(BF16)
    ones = jnp.ones((8, width), BF16)
    square = jnp.square(hidden.astype(F32))
    high = square.astype(BF16)
    low = (square - high.astype(F32)).astype(BF16)
    sums_ref[0:latent] = contract(scaled, hidden, 1, 1)
    columns = jnp.concatenate(
        [
            contract(embed, embed, 1, 1),
            jnp.sum(scaled.astype(F32), axis=1, keepdims=True),
            jnp.sum(out_w * shift, axis=1, keepdims=True),
            jnp.sum(embed.astype(F32), axis=1, keepdims=True),
            jnp.zeros((latent, tokens - latent - 3), F32),
        ],
        axis=1,
    )
    sums_ref[latent : 2 * latent] = columns
    row = lax.broadcasted_iota(jnp.int32, (8, tokens), 0)
    firsts = contract(ones, hidden, 1, 1)
    squares = contract(ones, high, 1, 1) + contract(ones, low, 1, 1)
    embeds = jnp.concatenate(
        [contract(ones, embed, 1, 1), jnp.zeros((8, tokens - latent), F32)], axis=1
    )
    sums_ref[2 * latent :] = jnp.where(row == 0, firsts, jnp.where(row == 1, squares, embeds))


def noise_body(time_ref, sums_ref, noise_ref, latents_ref, noised_ref, *, width):
    latent = noise_ref.shape[0]
    mean = sums_ref[2 * latent : 2 * latent + 1] / width
    var = sums_ref[2 * latent + 1 : 2 * latent + 2] / width - mean * mean
    scaled_sum = sums_ref[latent : 2 * latent, latent : latent + 1]
    shifted_sum = sums_ref[latent : 2 * latent, latent + 1 : latent + 2]
    latents = lax.rsqrt(var + EPSILON) * (sums_ref[0:latent] - mean * scaled_sum) + shifted_sum
    latents = latents.astype(BF16)
    latents_ref[...] = latents
    level = level_of(time_ref)
    noised_ref[...] = (
        (1.0 - level) * latents.astype(F32) + level * noise_ref[...].astype(F32)
    ).astype(BF16)


def act_body(
    sums_ref,
    before_ref,
    noised_ref,
    after_ref,
    weights_ref,
    cross_ref,
    out_ref,
    pre_ref,
    query_ref,
    side_ref,
    act_ref,
    *,
    width,
):
    latent, tokens = noised_ref.shape
    units = weights_ref.shape[0]
    copies, share, _ = out_ref.shape
    extent = 3 * tokens
    split = weights_ref.shape[1] - 128
    noised = jnp.concatenate([before_ref[...], noised_ref[...], after_ref[...]], axis=1)
    noised_f = noised.astype(F32)
    center_col = sums_ref[latent : 2 * latent, latent + 2 : latent + 3] / width
    center_row = sums_ref[2 * latent + 2 : 2 * latent + 3, :latent] / width
    gram = sums_ref[latent : 2 * latent, :latent] - width * (center_col * center_row)
    gram_noised = contract(gram, noised_f, 1, 0, HIGHEST)
    var = jnp.sum(noised_f * gram_noised, axis=0, keepdims=True) / width
    inv_std = lax.rsqrt(var + EPSILON)
    side_ref[0:latent] = gram_noised[:, tokens : 2 * tokens]
    side_ref[latent:] = jnp.broadcast_to(inv_std[:, tokens : 2 * tokens], (8, tokens))
    step = 128
    for begin in range(0, units, step):
        rows = slice(begin, begin + step)
        raw = weights_ref[rows, split : split + latent].astype(F32)
        gain = weights_ref[rows, split + latent : split + latent + 1].astype(F32)
        shift = weights_ref[rows, split + latent + 1 : split + latent + 2].astype(F32)
        query = (raw - gain * center_row).astype(BF16)
        query_ref[rows] = query
        pre = contract(query, noised, 1, 0) * inv_std + shift
        pre_ref[rows] = pre[:, tokens : 2 * tokens]
        act_ref[rows] = gelu_tanh(pre).astype(BF16)
    part = contract(weights_ref[:, :split], act_ref[...], 0, 0).astype(BF16)
    out_ref[:, :, :extent] = part.reshape(copies, share, extent)
    out_ref[:, :, extent:] = cross_ref[...]


def conv_body(
    parts_ref, before_ref, noised_ref, after_ref, taps_ref, pay_ref, back_ref, *, count
):
    _, share, _ = parts_ref.shape
    latent, own = noised_ref.shape
    extent = 3 * own
    channels = 2 * share
    noised = jnp.concatenate([before_ref[...], noised_ref[...], after_ref[...]], axis=1)
    total = jnp.sum(parts_ref[...].astype(F32), axis=0)
    cross = jnp.concatenate(
        [total[:, extent : extent + latent], total[:, extent + latent :]], axis=0
    ).astype(BF16)
    embed = contract(cross, noised, 1, 0)
    field_in = jnp.concatenate([embed[:share] + total[:, :extent], embed[share:]], axis=0)
    lane = lax.broadcasted_iota(jnp.int32, (channels, extent), 1)
    at = lax.axis_index("seq")
    first = jnp.where(at == 0, own, 0)
    last = jnp.where(at == count - 1, 2 * own, extent)
    inside = (lane >= first) & (lane < last)
    column = lane % GRID_W
    left_ok = column > 0
    right_ok = column < GRID_W - 1

    def tap(row, col):
        place = 3 * row + col
        return taps_ref[:, place : place + 1]

    def convolve(grid, flip):
        before = jnp.where(left_ok, pltpu.roll(grid, 1, 1), 0.0)
        after = jnp.where(right_ok, pltpu.roll(grid, extent - 1, 1), 0.0)
        rows = []
        for row in range(3):
            if flip:
                rows.append(tap(row, 2) * before + tap(row, 1) * grid + tap(row, 0) * after)
            else:
                rows.append(tap(row, 0) * before + tap(row, 1) * grid + tap(row, 2) * after)
        if flip:
            rows = rows[::-1]
        return pltpu.roll(rows[0], GRID_W, 1) + rows[1] + pltpu.roll(rows[2], extent - GRID_W, 1)

    field = convolve(jnp.where(inside, field_in, 0.0), False)
    gating = jax.nn.sigmoid(field)
    scale = taps_ref[:, 9:10]
    terms = field * gating * scale
    slope = -scale * gating * (1.0 + field * (1.0 - gating))
    grad = convolve(jnp.where(inside, slope, 0.0), True)[:, own : 2 * own]
    block_sum = jnp.sum(terms[:share, own : 2 * own], axis=0, keepdims=True)
    embed_sum = jnp.sum(terms[share:, own : 2 * own], axis=0, keepdims=True)
    sums = jnp.concatenate([block_sum, embed_sum], axis=0)
    high = sums.astype(BF16).astype(F32)
    low = sums - high
    tail = jnp.concatenate([high, low, jnp.zeros((12, own), F32)], axis=0)
    pay = jnp.concatenate([grad[:share], tail], axis=0).astype(BF16)
    pay_ref[...] = jnp.broadcast_to(pay[None], pay_ref.shape)
    back_ref[...] = contract(cross, grad.astype(BF16), 0, 0)


def back_body(
    disc_ref,
    pay_ref,
    weights_ref,
    query_ref,
    slope_ref,
    side_ref,
    noised_ref,
    back_ref,
    out_ref,
    logits_ref,
    *,
    width,
):
    copies, rows, tokens = pay_ref.shape
    share = rows - 16
    latent = noised_ref.shape[0]
    split = copies * share
    grads = jnp.concatenate([pay_ref[copy, :share] for copy in range(copies)], axis=0)
    hidden_grad = contract(weights_ref[:, :split], grads, 1, 0)
    preact_grad = (hidden_grad * slope_ref[...]).astype(BF16)
    query_grad = contract(query_ref[...], preact_grad, 0, 0)
    inv_std = side_ref[latent : latent + 1]
    along = jnp.sum(noised_ref[...].astype(F32) * query_grad, axis=0, keepdims=True)
    result = (
        inv_std * (query_grad - (inv_std * inv_std / width) * along * side_ref[0:latent])
        + back_ref[...]
    )
    out_ref[...] = jnp.broadcast_to(result.astype(BF16)[None], out_ref.shape)
    sums = []
    for place in range(2):
        total = jnp.zeros((16, tokens), F32)
        for copy in range(copies // 2 * place, copies // 2 * (place + 1)):
            total = total + pay_ref[copy, share:].astype(F32)
        sums.append(total[0:2] + total[2:4])
    block, other = pick_heads(disc_ref)
    for k in range(4):
        chosen = jnp.where(block[0] == k, 0, jnp.where(block[1] == k, 1, jnp.where(other[0] == k, 2, 3)))
        options = [sums[0][0:1], sums[1][0:1], sums[0][1:2], sums[1][1:2]]
        value = options[3]
        for place in range(3):
            value = jnp.where(chosen == place, options[place], value)
        logits_ref[k : k + 1] = value


def final_body(time_ref, parts_ref, out_ref):
    retain = 1.0 - level_of(time_ref)
    out_ref[...] = retain * jnp.sum(parts_ref[...].astype(F32), axis=0)


def per_device(
    student_hidden,
    student_cond,
    student_mod,
    student_out,
    timestep,
    noise,
    teacher_embed,
    teacher_mod,
    up_weight,
    down_weight,
    head_proj,
    head_kernel,
    head_out,
    disc_layer,
):
    groups = lax.axis_size("group")
    seqs = lax.axis_size("seq")
    mps = lax.axis_size("mp")
    _, tokens, local_width = student_hidden.shape
    width = local_width * mps
    latent = teacher_embed.shape[0]
    units = down_weight.shape[0]
    channels = head_proj.shape[2]
    share = 2 * channels // mps
    lanes = 2 * channels + 128
    extent = 3 * tokens

    pieces = local_width // 128
    (mods,) = call(
        smod_body, [((groups * seqs, pieces, 128), F32)], [], [student_cond, student_mod[:, 0]]
    )
    mods = exchange(mods, ("group", "seq"))

    tmod = jnp.einsum(
        "sf,fjd->sjd",
        time_features(timestep, teacher_mod.shape[0]),
        teacher_mod.astype(F32),
        precision=HIGHEST,
    )[0]
    ratio = seqs // mps
    rows = local_width // ratio
    (sent,) = call(
        prep_body,
        [((rows, lanes), BF16)],
        [disc_layer],
        [tmod, teacher_embed, head_proj],
        [((local_width, 128), F32)],
    )
    swap = [
        (at * mps + m, (ratio * m + at % ratio) * mps + at // ratio)
        for at in range(seqs)
        for m in range(mps)
    ]
    got = lax.ppermute(sent, ("seq", "mp"), swap)
    (terms,) = call(
        weight_body,
        [((seqs, units // seqs, lanes), BF16)],
        [],
        [got, down_weight.T, up_weight, mods],
    )
    terms = exchange(terms, "seq")
    table = jnp.concatenate(
        [head_kernel.reshape(4, 9, channels), head_out[:, None], jnp.zeros((4, 6, channels), F32)],
        axis=1,
    )
    cross, taps = call(
        cross_body,
        [((mps, share, 2 * latent), BF16), ((2 * share, 16), F32)],
        [disc_layer],
        [head_proj, teacher_embed, table],
        [((channels, 16), F32)],
    )

    (sums,) = call(
        sums_body,
        [((2 * latent + 8, tokens), F32)],
        [],
        [student_hidden[0], student_out.T, teacher_embed, mods],
    )
    stages = [sums]
    step = 1
    while step < mps:
        sums = sums + lax.ppermute(sums, "mp", [(i, i ^ step) for i in range(mps)])
        step *= 2
        stages.append(sums)
    halfway = stages[-2]
    (terms,) = call(gather_body, [((seqs, units // seqs, lanes), BF16)], [], [terms, halfway])
    weights = exchange(terms, "seq").reshape(units, lanes)

    latents, noised = call(
        functools.partial(noise_body, width=float(width)),
        [((latent, tokens), BF16), ((latent, tokens), BF16)],
        [timestep],
        [sums, noise[0].T],
        loose=(0,),
    )
    before = lax.ppermute(noised, "seq", [(i, i + 1) for i in range(seqs - 1)])
    after = lax.ppermute(noised, "seq", [(i + 1, i) for i in range(seqs - 1)])

    parts, preact, query, side = call(
        functools.partial(act_body, width=float(width)),
        [
            ((mps, share, extent + 2 * latent), BF16),
            ((units, tokens), F32),
            ((units, latent), BF16),
            ((latent + 8, tokens), F32),
        ],
        [],
        [sums, before, noised, after, weights, cross],
        [((units, extent), BF16)],
    )
    parts = exchange(parts, "mp")
    slope = gelu_slope(preact)
    pay, back = call(
        functools.partial(conv_body, count=seqs),
        [((mps, share + 16, tokens), BF16), ((latent, tokens), F32)],
        [],
        [parts, before, noised, after, taps],
    )
    pay = exchange(pay, "mp")
    back, logits = call(
        functools.partial(back_body, width=float(width)),
        [((mps, latent, tokens), BF16), ((4, tokens), F32)],
        [disc_layer],
        [pay, weights, query, slope, side, noised, back],
        loose=(1,),
    )
    back = exchange(back, "mp")
    (latent_grad,) = call(final_body, [((latent, tokens), F32)], [timestep], [back], loose=(0,))
    return (latents.T[None], logits[None], latent_grad.T[None])


def solution(mesh):
    return jax.shard_map(
        per_device,
        mesh=mesh,
        in_specs=(
            P("group", "seq", "mp"),
            P(None, "seq"),
            P("seq", "group", "mp"),
            P("mp", None),
            P("group"),
            P("group", "seq", None),
            P(None, "mp"),
            P(None, None, "mp"),
            P("seq", "mp"),
            P("mp", "seq"),
            P(None, "mp", None),
            P(),
            P(),
            P("group", None),
        ),
        out_specs=(P("group", "seq", None), P("group", None, "seq"), P("group", "seq", None)),
        check_vma=False,
    )
```

profile of v0, /device:TPU:14, one launch (start us, length us, event | category | flops | bytes accessed | tf_op | source)
XLA Modules:
  0.0 141.5 jit_solution(6932087304590811006)
XLA Ops:
  0.6 0.0 copy-start
  0.6 0.0 copy-start.9
  0.7 0.7 copy-done.9
  1.4 0.0 copy-start.6
  1.4 0.9 copy-done.6
  2.3 0.0 copy-start.1
  2.3 0.9 shard_map.157
  3.1 10.7 %all-to-all-start = ((f32[64,3,128]{2,1,0:T(4,128)}), f32[64,3,128]{2,1,0:T(4,128)S(1)}, u32[]{:S(2)}, u32[]{:S(2)}) async-start(f32[64,3,128]{2,1,0:T(4,128)} %shard_map.157), calls=%async_computation | async-start | bytes 262144 | tf_op jit(solution)/shard_map/all_to_all | solution.py:54
  14.5 0.1 fusion.9
  14.6 0.0 copy-done
  14.6 0.0 copy-start.2
  14.6 0.3 fusion.5
  14.9 0.0 copy-done.1
  14.9 0.5 copy-done.2
  15.4 0.0 copy-start.3
  15.4 0.0 copy-start.4
  15.4 0.9 shard_map.160
  16.3 10.8 %collective-permute-start.5 = (bf16[96,384]{1,0:T(8,128)(2,1)S(1)}, bf16[96,384]{1,0:T(8,128)(2,1)S(1)}, u32[]{:S(2)}, u32[]{:S(2)}) collective-permute-start(bf16[96,384]{1,0:T(8,128)(2,1)S(1)} %shard_map.160), channel_id=1, source_target_pairs={{0,0},{1,32},{2,64},{3,96},{4,128},{5,160},{6,192},{7,224},{8,8},{... | collective-permute-start | bytes 221192 | tf_op jit(solution)/shard_map/ppermute | solution.py:428
  27.1 4.1 %collective-permute-done.5.got_ref = bf16[96,384]{1,0:T(8,128)(2,1)S(1)} collective-permute-done((bf16[96,384]{1,0:T(8,128)(2,1)S(1)}, bf16[96,384]{1,0:T(8,128)(2,1)S(1)}, u32[]{:S(2)}, u32[]{:S(2)}) %collective-permute-start.5) | collective-permute-done | bytes 73760 | tf_op jit(solution)/shard_map/ppermute | solution.py:428
  31.2 0.0 all-to-all-done.mod_ref.order_ref
  31.2 0.0 copy-done.3
  31.2 0.0 copy-done.4
  31.2 1.2 shard_map.161
  32.4 0.0 copy-start.5
  32.4 0.0 copy-start.7
  32.4 12.1 %all-to-all-start.1 = ((bf16[32,24,384]{2,1,0:T(8,128)(2,1)}), bf16[32,24,384]{2,1,0:T(8,128)(2,1)S(1)}, u32[]{:S(2)}, u32[]{:S(2)}) async-start(bf16[32,24,384]{2,1,0:T(8,128)(2,1)} %shard_map.161), calls=%async_computation.1 | async-start | bytes 1179648 | tf_op jit(solution)/shard_map/all_to_all | solution.py:54
  44.5 0.0 copy-done.5
  44.5 0.0 copy-done.7
  44.6 0.3 shard_map.158
  44.8 2.0 %collective-permute-start = (f32[136,128]{1,0:T(8,128)S(1)}, f32[136,128]{1,0:T(8,128)S(1)}, u32[]{:S(2)}, u32[]{:S(2)}) collective-permute-start(f32[136,128]{1,0:T(8,128)S(1)} %shard_map.158), channel_id=1, source_target_pairs={{0,1},{1,0},{2,3},{3,2},{4,5},{5,4},{6,7},{7,6},{8,9},{9,8},{10,11... | collective-permute-start | bytes 208904 | tf_op jit(solution)/shard_map/ppermute | solution.py:457
  46.8 4.3 %collective-permute-done = f32[136,128]{1,0:T(8,128)S(1)} collective-permute-done((f32[136,128]{1,0:T(8,128)S(1)}, f32[136,128]{1,0:T(8,128)S(1)}, u32[]{:S(2)}, u32[]{:S(2)}) %collective-permute-start) | collective-permute-done | bytes 69664 | tf_op jit(solution)/shard_map/ppermute | solution.py:457
  51.1 5.8 %collective-permute-start.1 = (f32[136,128]{1,0:T(8,128)S(1)}, f32[136,128]{1,0:T(8,128)S(1)}, u32[]{:S(2)}, u32[]{:S(2)}) collective-permute-start(f32[136,128]{1,0:T(8,128)S(1)} %add.21), channel_id=1, source_target_pairs={{0,2},{1,3},{2,0},{3,1},{4,6},{5,7},{6,4},{7,5},{8,10},{9,11},{10,... | collective-permute-start | bytes 208904 | tf_op jit(solution)/shard_map/ppermute | solution.py:457
  56.9 3.0 %collective-permute-done.1 = f32[136,128]{1,0:T(8,128)S(1)} collective-permute-done((f32[136,128]{1,0:T(8,128)S(1)}, f32[136,128]{1,0:T(8,128)S(1)}, u32[]{:S(2)}, u32[]{:S(2)}) %collective-permute-start.1) | collective-permute-done | bytes 69664 | tf_op jit(solution)/shard_map/ppermute | solution.py:457
  59.9 2.1 %all-to-all-done.1.parts_ref = bf16[32,24,384]{2,1,0:T(8,128)(2,1)S(1)} async-done(((bf16[32,24,384]{2,1,0:T(8,128)(2,1)}), bf16[32,24,384]{2,1,0:T(8,128)(2,1)S(1)}, u32[]{:S(2)}, u32[]{:S(2)}) %all-to-all-start.1) | async-done | bytes 589856 | tf_op jit(solution)/shard_map/all_to_all | solution.py:54
  62.0 0.9 shard_map.162
  62.9 0.0 copy-start.10
  62.9 7.9 %all-to-all-start.2 = ((bf16[32,24,384]{2,1,0:T(8,128)(2,1)}), bf16[32,24,384]{2,1,0:T(8,128)(2,1)S(1)}, u32[]{:S(2)}, u32[]{:S(2)}) async-start(bf16[32,24,384]{2,1,0:T(8,128)(2,1)} %shard_map.162), calls=%async_computation.2 | async-start | bytes 1179648 | tf_op jit(solution)/shard_map/all_to_all | solution.py:54
  70.8 8.1 %collective-permute-start.2 = (f32[136,128]{1,0:T(8,128)S(1)}, f32[136,128]{1,0:T(8,128)S(1)}, u32[]{:S(2)}, u32[]{:S(2)}) collective-permute-start(f32[136,128]{1,0:T(8,128)S(1)} %add.22.order_ref), channel_id=1, source_target_pairs={{0,4},{1,5},{2,6},{3,7},{4,0},{5,1},{6,2},{7,3},{8,12},{9,13},{10,... | collective-permute-start | bytes 208904 | tf_op jit(solution)/shard_map/ppermute | solution.py:457
  78.9 0.0 copy-done.10
  79.0 0.1 pad.2.clone
  79.0 0.0 copy-start.8
  79.0 2.4 %collective-permute-done.2 = f32[136,128]{1,0:T(8,128)S(1)} collective-permute-done((f32[136,128]{1,0:T(8,128)S(1)}, f32[136,128]{1,0:T(8,128)S(1)}, u32[]{:S(2)}, u32[]{:S(2)}) %collective-permute-start.2) | collective-permute-done | bytes 69664 | tf_op jit(solution)/shard_map/ppermute | solution.py:457
  81.5 0.0 copy-done.8
  81.5 0.7 shard_map.159
  82.2 0.0 copy-start.11
  82.2 4.9 %collective-permute-start.4 = (bf16[64,128]{1,0:T(8,128)(2,1)S(1)}, bf16[64,128]{1,0:T(8,128)(2,1)S(1)}, u32[]{:S(2)}, u32[]{:S(2)}) collective-permute-start(bf16[64,128]{1,0:T(8,128)(2,1)S(1)} %get-tuple-element.16.noised_ref), channel_id=1, source_target_pairs={{8,0},{16,8},{24,16},{32,24},{40,32},{48,40},{56,48},{64,56},{72,6... | collective-permute-start | bytes 49160 | tf_op jit(solution)/shard_map/ppermute | solution.py:472
  87.1 1.9 %collective-permute-start.3 = (bf16[64,128]{1,0:T(8,128)(2,1)S(1)}, bf16[64,128]{1,0:T(8,128)(2,1)S(1)}, u32[]{:S(2)}, u32[]{:S(2)}) collective-permute-start(bf16[64,128]{1,0:T(8,128)(2,1)S(1)} %get-tuple-element.16.noised_ref), channel_id=1, source_target_pairs={{0,8},{8,16},{16,24},{24,32},{32,40},{40,48},{48,56},{56,64},{64,7... | collective-permute-start | bytes 49160 | tf_op jit(solution)/shard_map/ppermute | solution.py:471
  89.1 0.0 copy-done.11
  89.1 0.1 maximum_maximum_fusion.table_ref
  89.1 1.0 shard_map.163
  90.2 0.0 collective-permute-done.4.after_ref
  90.2 5.0 %collective-permute-done.3.before_ref = bf16[64,128]{1,0:T(8,128)(2,1)S(1)} collective-permute-done((bf16[64,128]{1,0:T(8,128)(2,1)S(1)}, bf16[64,128]{1,0:T(8,128)(2,1)S(1)}, u32[]{:S(2)}, u32[]{:S(2)}) %collective-permute-start.3) | collective-permute-done | bytes 16416 | tf_op jit(solution)/shard_map/ppermute | solution.py:471
  95.2 0.0 all-to-all-done.2
  95.2 1.1 shard_map.164
  96.3 18.3 %all_to_all.30.parts_ref = bf16[8,32,512]{2,1,0:T(8,128)(2,1)S(1)} all-to-all(bf16[8,32,512]{2,1,0:T(8,128)(2,1)S(1)} %get-tuple-element.18), channel_id=1, replica_groups=mesh['group'=2,'seq'=32,'mp'=8] {'mp'}, dimensions={0} | all-to-all | bytes 524288 | tf_op jit(solution)/shard_map/all_to_all | solution.py:54
  114.6 1.2 shard_map.165
  115.8 3.4 %all-to-all-start.4 = ((bf16[8,48,128]{2,1,0:T(8,128)(2,1)}), bf16[8,48,128]{2,1,0:T(8,128)(2,1)S(1)}, u32[]{:S(2)}, u32[]{:S(2)}) async-start(bf16[8,48,128]{2,1,0:T(8,128)(2,1)} %get-tuple-element.20), calls=%async_computation.4 | async-start | bytes 196608 | tf_op jit(solution)/shard_map/all_to_all | solution.py:54
  119.1 0.2 fusion.4.slope_ref
  119.4 8.4 %all-to-all-done.4.pay_ref = bf16[8,48,128]{2,1,0:T(8,128)(2,1)S(1)} async-done(((bf16[8,48,128]{2,1,0:T(8,128)(2,1)}), bf16[8,48,128]{2,1,0:T(8,128)(2,1)S(1)}, u32[]{:S(2)}, u32[]{:S(2)}) %all-to-all-start.4) | async-done | bytes 98336 | tf_op jit(solution)/shard_map/all_to_all | solution.py:54
  127.8 1.6 %shard_map.166 = (bf16[8,64,128]{2,1,0:T(8,128)(2,1)S(1)}, f32[4,128]{1,0:T(4,128)}) custom-call(s32[1,4]{1,0:T(1,128)} %disc_ref.5, bf16[8,48,128]{2,1,0:T(8,128)(2,1)S(1)} %all-to-all-done.4.pay_ref, bf16[768,384]{1,0:T(8,128)(2,1)S(1)} %bitcast.27, bf16[768,64]{1,0:T(8,128)(2,1)S(1)} %get-tuple-element.21.query_ref, f32[768,128]{1,0:T(8,128)S(1)} %fusion.4.slope_ref, ...), custom_call_target="tpu_custom_call" | custom-call | tf_op jit(solution)/shard_map/pallas_call | solution.py:68
  129.4 11.5 %all_to_all.31.parts_ref = bf16[8,64,128]{2,1,0:T(8,128)(2,1)S(1)} all-to-all(bf16[8,64,128]{2,1,0:T(8,128)(2,1)S(1)} %get-tuple-element.26), channel_id=1, replica_groups=mesh['group'=2,'seq'=32,'mp'=8] {'mp'}, dimensions={0} | all-to-all | bytes 262144 | tf_op jit(solution)/shard_map/all_to_all | solution.py:54
  140.8 0.6 shard_map.167
  (6 shorter events, 0.0 us)
Async XLA Ops:
  0.6 14.0 %copy-start = (bf16[256,2,384]{2,1,0:T(2,128)(2,1)S(1)}, bf16[256,2,384]{2,1,0:T(2,128)(2,1)}, u32[]{:S(2)}) copy-start(bf16[256,2,384]{2,1,0:T(2,128)(2,1)} %param.21) | copy-start | bytes 1179652
  0.6 0.7 copy-start.9
  1.4 0.9 copy-start.6
  2.3 12.6 %copy-start.1 = (bf16[4,384,128]{2,1,0:T(8,128)(2,1)S(1)}, bf16[4,384,128]{2,1,0:T(8,128)(2,1)}, u32[]{:S(2)}) copy-start(bf16[4,384,128]{2,1,0:T(8,128)(2,1)} %proj_ref.3) | copy-start | bytes 1179652
  3.1 28.1 %all-to-all-start = ((f32[64,3,128]{2,1,0:T(4,128)}), f32[64,3,128]{2,1,0:T(4,128)S(1)}, u32[]{:S(2)}, u32[]{:S(2)}) async-start(f32[64,3,128]{2,1,0:T(4,128)} %shard_map.157), calls=%async_computation | async-start | bytes 262144 | tf_op jit(solution)/shard_map/all_to_all | solution.py:54
  14.6 0.8 copy-start.2
  15.4 15.8 %copy-start.3 = (bf16[768,96]{0,1:T(8,128)(2,1)S(1)}, bf16[768,96]{0,1:T(8,128)(2,1)}, u32[]{:S(2)}) copy-start(bf16[768,96]{0,1:T(8,128)(2,1)} %param.23) | copy-start | bytes 442372
  15.4 15.8 %copy-start.4 = (bf16[96,768]{1,0:T(8,128)(2,1)S(1)}, bf16[96,768]{1,0:T(8,128)(2,1)}, u32[]{:S(2)}) copy-start(bf16[96,768]{1,0:T(8,128)(2,1)} %up_ref.1) | copy-start | bytes 442372
  16.3 14.9 %collective-permute-start.5 = (bf16[96,384]{1,0:T(8,128)(2,1)S(1)}, bf16[96,384]{1,0:T(8,128)(2,1)S(1)}, u32[]{:S(2)}, u32[]{:S(2)}) collective-permute-start(bf16[96,384]{1,0:T(8,128)(2,1)S(1)} %shard_map.160), channel_id=1, source_target_pairs={{0,0},{1,32},{2,64},{3,96},{4,128},{5,160},{6,192},{7,224},{8,8},{... | collective-permute-start | bytes 221192 | tf_op jit(solution)/shard_map/ppermute | solution.py:428
  32.4 12.1 %copy-start.5 = (bf16[1,128,384]{2,1,0:T(8,128)(2,1)S(1)}, bf16[1,128,384]{2,1,0:T(8,128)(2,1)}, u32[]{:S(2)}) copy-start(bf16[1,128,384]{2,1,0:T(8,128)(2,1)} %param.14) | copy-start | bytes 294916
  32.4 12.1 %copy-start.7 = (bf16[384,64]{0,1:T(8,128)(2,1)S(1)}, bf16[384,64]{0,1:T(8,128)(2,1)}, u32[]{:S(2)}) copy-start(bf16[384,64]{0,1:T(8,128)(2,1)} %param.17) | copy-start | bytes 147460
  32.4 29.6 %all-to-all-start.1 = ((bf16[32,24,384]{2,1,0:T(8,128)(2,1)}), bf16[32,24,384]{2,1,0:T(8,128)(2,1)S(1)}, u32[]{:S(2)}, u32[]{:S(2)}) async-start(bf16[32,24,384]{2,1,0:T(8,128)(2,1)} %shard_map.161), calls=%async_computation.1 | async-start | bytes 1179648 | tf_op jit(solution)/shard_map/all_to_all | solution.py:54
  44.8 6.2 %collective-permute-start = (f32[136,128]{1,0:T(8,128)S(1)}, f32[136,128]{1,0:T(8,128)S(1)}, u32[]{:S(2)}, u32[]{:S(2)}) collective-permute-start(f32[136,128]{1,0:T(8,128)S(1)} %shard_map.158), channel_id=1, source_target_pairs={{0,1},{1,0},{2,3},{3,2},{4,5},{5,4},{6,7},{7,6},{8,9},{9,8},{10,11... | collective-permute-start | bytes 208904 | tf_op jit(solution)/shard_map/ppermute | solution.py:457
  51.1 8.8 %collective-permute-start.1 = (f32[136,128]{1,0:T(8,128)S(1)}, f32[136,128]{1,0:T(8,128)S(1)}, u32[]{:S(2)}, u32[]{:S(2)}) collective-permute-start(f32[136,128]{1,0:T(8,128)S(1)} %add.21), channel_id=1, source_target_pairs={{0,2},{1,3},{2,0},{3,1},{4,6},{5,7},{6,4},{7,5},{8,10},{9,11},{10,... | collective-permute-start | bytes 208904 | tf_op jit(solution)/shard_map/ppermute | solution.py:457
  62.9 16.0 %copy-start.10 = (f32[4,3,3,128]{3,0,2,1:T(4,128)S(1)}, f32[4,3,3,128]{3,0,2,1:T(4,128)}, u32[]{:S(2)}) copy-start(f32[4,3,3,128]{3,0,2,1:T(4,128)} %param.25) | copy-start | bytes 55300
  62.9 32.3 %all-to-all-start.2 = ((bf16[32,24,384]{2,1,0:T(8,128)(2,1)}), bf16[32,24,384]{2,1,0:T(8,128)(2,1)S(1)}, u32[]{:S(2)}, u32[]{:S(2)}) async-start(bf16[32,24,384]{2,1,0:T(8,128)(2,1)} %shard_map.162), calls=%async_computation.2 | async-start | bytes 1179648 | tf_op jit(solution)/shard_map/all_to_all | solution.py:54
  70.8 10.7 %collective-permute-start.2 = (f32[136,128]{1,0:T(8,128)S(1)}, f32[136,128]{1,0:T(8,128)S(1)}, u32[]{:S(2)}, u32[]{:S(2)}) collective-permute-start(f32[136,128]{1,0:T(8,128)S(1)} %add.22.order_ref), channel_id=1, source_target_pairs={{0,4},{1,5},{2,6},{3,7},{4,0},{5,1},{6,2},{7,3},{8,12},{9,13},{10,... | collective-permute-start | bytes 208904 | tf_op jit(solution)/shard_map/ppermute | solution.py:457
  79.0 2.5 %copy-start.8 = (bf16[1,128,64]{1,2,0:T(8,128)(2,1)S(1)}, bf16[1,128,64]{1,2,0:T(8,128)(2,1)}, u32[]{:S(2)}) copy-start(bf16[1,128,64]{1,2,0:T(8,128)(2,1)} %param.19) | copy-start | bytes 49156
  82.2 6.9 %copy-start.11 = (f32[4,128]{1,0:T(4,128)S(1)}, f32[4,128]{1,0:T(4,128)}, u32[]{:S(2)}) copy-start(f32[4,128]{1,0:T(4,128)} %param.26) | copy-start | bytes 6148
  82.2 8.0 %collective-permute-start.4 = (bf16[64,128]{1,0:T(8,128)(2,1)S(1)}, bf16[64,128]{1,0:T(8,128)(2,1)S(1)}, u32[]{:S(2)}, u32[]{:S(2)}) collective-permute-start(bf16[64,128]{1,0:T(8,128)(2,1)S(1)} %get-tuple-element.16.noised_ref), channel_id=1, source_target_pairs={{8,0},{16,8},{24,16},{32,24},{40,32},{48,40},{56,48},{64,56},{72,6... | collective-permute-start | bytes 49160 | tf_op jit(solution)/shard_map/ppermute | solution.py:472
  87.1 8.1 %collective-permute-start.3 = (bf16[64,128]{1,0:T(8,128)(2,1)S(1)}, bf16[64,128]{1,0:T(8,128)(2,1)S(1)}, u32[]{:S(2)}, u32[]{:S(2)}) collective-permute-start(bf16[64,128]{1,0:T(8,128)(2,1)S(1)} %get-tuple-element.16.noised_ref), channel_id=1, source_target_pairs={{0,8},{8,16},{16,24},{24,32},{32,40},{40,48},{48,56},{56,64},{64,7... | collective-permute-start | bytes 49160 | tf_op jit(solution)/shard_map/ppermute | solution.py:471
  115.8 12.0 %all-to-all-start.4 = ((bf16[8,48,128]{2,1,0:T(8,128)(2,1)}), bf16[8,48,128]{2,1,0:T(8,128)(2,1)S(1)}, u32[]{:S(2)}, u32[]{:S(2)}) async-start(bf16[8,48,128]{2,1,0:T(8,128)(2,1)} %get-tuple-element.20), calls=%async_computation.4 | async-start | bytes 196608 | tf_op jit(solution)/shard_map/all_to_all | solution.py:54
where the time goes:
time: 142 us; the launch traced here: 141 us
  starting transfers between devices  67.6 us (48%)
  blocking collectives  29.7 us (21%)
  waiting for transfers between devices  29.3 us (21%)
  Pallas kernels  10.4 us (7%)
  local copies, waits for them, and re-layouts  2.24 us (2%)
  between operations  1.52 us (1%)
    all_to_all x4, starting transfers between devices, exchange(): return lax.all_to_all(value, axes, 0, 0, tiled=False)  34.1 us
    all_to_all x2, blocking collectives, exchange(): return lax.all_to_all(value, axes, 0, 0, tiled=False)  29.7 us
    ppermute x3, starting transfers between devices, per_device(): sums = sums + lax.ppermute(sums, 'mp', [(i, i ^ step) for i in range(mps)])  15.9 us
    ppermute x1, starting transfers between devices, per_device(): got = lax.ppermute(sent, ('seq', 'mp'), swap)  10.8 us
    all_to_all x4, waiting for transfers between devices, exchange(): return lax.all_to_all(value, axes, 0, 0, tiled=False)  10.5 us
    pallas_call x11, Pallas kernels, call(): pl.pallas_call(body, in_specs=[smem] * len(scalars) + [vmem] * len(arrays...  10.4 us
    ppermute x3, waiting for transfers between devices, per_device(): sums = sums + lax.ppermute(sums, 'mp', [(i, i ^ step) for i in range(mps)])  9.71 us
    ppermute x1, waiting for transfers between devices, per_device(): before = lax.ppermute(noised, 'seq', [(i, i + 1) for i in range(seqs - 1)])  4.99 us
  transfers between devices with their start and end apart: 10, of which 7 were waited for; matrix products, arithmetic and copies ran while one was open for 1% of the time, Pallas kernels for 2%

commit v1 on v0

--- a/solution.py
+++ b/solution.py
@@ -6,6 +6,7 @@
 from jax import lax
 from jax.experimental import pallas as pl
 from jax.experimental.pallas import tpu as pltpu
+from jax.sharding import Mesh
 from jax.sharding import PartitionSpec as P
 
 
@@ -48,6 +49,13 @@
     freqs = jnp.exp(-math.log(10000.0) * index / half_width)
     angles = timestep.astype(F32)[:, None] * freqs[None, :]
     return jnp.concatenate([jnp.cos(angles), jnp.sin(angles)], axis=-1)
+
+
+SEQ = ("plane", "core")
+
+
+def seq_index():
+    return lax.axis_index("plane") * 2 + lax.axis_index("core")
 
 
 def exchange(value, axes):
@@ -99,7 +107,9 @@
         block = jnp.concatenate(
             [row[:, lanes * p : lanes * (p + 1)] for p in range(pieces)], axis=0
         )
-        out_ref[seqs * group : seqs * (group + 1)] = jnp.broadcast_to(block[None], (seqs, pieces, lanes))
+        out_ref[seqs * group : seqs * (group + 1)] = jnp.broadcast_to(
+            block.astype(BF16)[None], (seqs, pieces, lanes)
+        )
 
 
 def prep_body(disc_ref, tmod_ref, embed_ref, proj_ref, out_ref, turned_ref):
@@ -107,7 +117,7 @@
     channels = proj_ref.shape[2]
     width = embed_ref.shape[1]
     latent = embed_ref.shape[0]
-    start = (lax.axis_index("seq") % (width // rows)) * rows
+    start = (seq_index() % (width // rows)) * rows
     gain = 1.0 + tmod_ref[1:2]
     queries = jnp.concatenate(
         [
@@ -128,10 +138,11 @@
     del order_ref
     copies, rows, lanes = out_ref.shape
     split = lanes - 128
+    half = pl.ds(pl.multiple_of(lax.axis_index("core") * (copies * rows), 128), copies * rows)
     terms = jnp.concatenate(
         [
-            contract(down_ref[...], got_ref[:, :split], 0, 0),
-            contract(up_ref[...], got_ref[:, split:], 0, 0),
+            contract(down_ref[:, half], got_ref[:, :split], 0, 0),
+            contract(up_ref[:, half], got_ref[:, split:], 0, 0),
         ],
         axis=1,
     )
@@ -171,7 +182,7 @@
     tokens = hidden_ref.shape[0]
     halves = []
     for half in range(2):
-        total = jnp.sum(mod_ref[copies // 2 * half : copies // 2 * (half + 1)], axis=0)
+        total = jnp.sum(mod_ref[copies // 2 * half : copies // 2 * (half + 1)].astype(F32), axis=0)
         halves.append(jnp.concatenate([total[p : p + 1] for p in range(pieces)], axis=1))
     shift, scale = halves
     hidden = hidden_ref[...]
@@ -183,33 +194,31 @@
     high = square.astype(BF16)
     low = (square - high.astype(F32)).astype(BF16)
     sums_ref[0:latent] = contract(scaled, hidden, 1, 1)
-    columns = jnp.concatenate(
-        [
-            contract(embed, embed, 1, 1),
-            jnp.sum(scaled.astype(F32), axis=1, keepdims=True),
-            jnp.sum(out_w * shift, axis=1, keepdims=True),
-            jnp.sum(embed.astype(F32), axis=1, keepdims=True),
-            jnp.zeros((latent, tokens - latent - 3), F32),
-        ],
-        axis=1,
-    )
-    sums_ref[latent : 2 * latent] = columns
+    gram = contract(embed, embed, 1, 1)
+    fold = latent // 2
+    sums_ref[latent : latent + fold] = jnp.concatenate([gram[:fold], gram[fold:]], axis=1)
     row = lax.broadcasted_iota(jnp.int32, (8, tokens), 0)
     firsts = contract(ones, hidden, 1, 1)
     squares = contract(ones, high, 1, 1) + contract(ones, low, 1, 1)
-    embeds = jnp.concatenate(
-        [contract(ones, embed, 1, 1), jnp.zeros((8, tokens - latent), F32)], axis=1
-    )
-    sums_ref[2 * latent :] = jnp.where(row == 0, firsts, jnp.where(row == 1, squares, embeds))
+    pairs = jnp.concatenate([contract(ones, embed, 1, 1), contract(ones, scaled, 1, 1)], axis=1)
+    shifted = contract(jnp.broadcast_to(shift, (8, width)), out_w, 1, 1, HIGHEST)
+    shifted = jnp.concatenate([shifted, shifted], axis=1)
+    sums_ref[latent + fold :] = jnp.where(
+        row == 0, firsts, jnp.where(row == 1, squares, jnp.where(row == 2, pairs, shifted))
+    )
 
 
 def noise_body(time_ref, sums_ref, noise_ref, latents_ref, noised_ref, *, width):
-    latent = noise_ref.shape[0]
-    mean = sums_ref[2 * latent : 2 * latent + 1] / width
-    var = sums_ref[2 * latent + 1 : 2 * latent + 2] / width - mean * mean
-    scaled_sum = sums_ref[latent : 2 * latent, latent : latent + 1]
-    shifted_sum = sums_ref[latent : 2 * latent, latent + 1 : latent + 2]
-    latents = lax.rsqrt(var + EPSILON) * (sums_ref[0:latent] - mean * scaled_sum) + shifted_sum
+    latent, tokens = noise_ref.shape
+    base = latent + latent // 2
+    mean = sums_ref[base : base + 1] / width
+    var = sums_ref[base + 1 : base + 2] / width - mean * mean
+    inv_std = lax.rsqrt(var + EPSILON)
+    scaled_sum = sums_ref[base + 2 : base + 3, latent:]
+    shifted_sum = sums_ref[base + 3 : base + 4, :latent]
+    ones = jnp.ones((1, tokens), F32)
+    centered = sums_ref[0:latent] - contract(scaled_sum, mean, 0, 0, HIGHEST)
+    latents = inv_std * centered + contract(shifted_sum, ones, 0, 0, HIGHEST)
     latents = latents.astype(BF16)
     latents_ref[...] = latents
     level = level_of(time_ref)
@@ -220,29 +229,38 @@
 
 def act_body(
     sums_ref,
-    before_ref,
-    noised_ref,
-    after_ref,
+    cross_noised_ref,
+    pair_ref,
     weights_ref,
     cross_ref,
     out_ref,
     pre_ref,
     query_ref,
     side_ref,
+    wide_ref,
     act_ref,
     *,
     width,
 ):
-    latent, tokens = noised_ref.shape
+    latent, extent = wide_ref.shape
+    tokens = extent // 3
     units = weights_ref.shape[0]
     copies, share, _ = out_ref.shape
-    extent = 3 * tokens
     split = weights_ref.shape[1] - 128
-    noised = jnp.concatenate([before_ref[...], noised_ref[...], after_ref[...]], axis=1)
-    noised_f = noised.astype(F32)
-    center_col = sums_ref[latent : 2 * latent, latent + 2 : latent + 3] / width
-    center_row = sums_ref[2 * latent + 2 : 2 * latent + 3, :latent] / width
-    gram = sums_ref[latent : 2 * latent, :latent] - width * (center_col * center_row)
+    edge = cross_noised_ref[...]
+    first = pair_ref[0:latent]
+    second = pair_ref[latent:]
+    noised_f = jnp.where(
+        lax.axis_index("core") == 0,
+        jnp.concatenate([edge, first, second], axis=1).astype(F32),
+        jnp.concatenate([first, second, edge], axis=1).astype(F32),
+    )
+    noised = noised_f.astype(BF16)
+    wide_ref[...] = noised
+    base = latent + latent // 2
+    center_row = sums_ref[base + 2 : base + 3, :latent] / width
+    gram = jnp.concatenate([sums_ref[latent:base, :latent], sums_ref[latent:base, latent:]], axis=0)
+    gram = gram - width * contract(center_row, center_row, 0, 0, HIGHEST)
     gram_noised = contract(gram, noised_f, 1, 0, HIGHEST)
     var = jnp.sum(noised_f * gram_noised, axis=0, keepdims=True) / width
     inv_std = lax.rsqrt(var + EPSILON)
@@ -265,13 +283,13 @@
 
 
 def conv_body(
-    parts_ref, before_ref, noised_ref, after_ref, taps_ref, pay_ref, back_ref, *, count
+    parts_ref, wide_ref, taps_ref, pay_ref, back_ref, *, count
 ):
     _, share, _ = parts_ref.shape
-    latent, own = noised_ref.shape
-    extent = 3 * own
+    latent, extent = wide_ref.shape
+    own = extent // 3
     channels = 2 * share
-    noised = jnp.concatenate([before_ref[...], noised_ref[...], after_ref[...]], axis=1)
+    noised = wide_ref[...]
     total = jnp.sum(parts_ref[...].astype(F32), axis=0)
     cross = jnp.concatenate(
         [total[:, extent : extent + latent], total[:, extent + latent :]], axis=0
@@ -279,7 +297,7 @@
     embed = contract(cross, noised, 1, 0)
     field_in = jnp.concatenate([embed[:share] + total[:, :extent], embed[share:]], axis=0)
     lane = lax.broadcasted_iota(jnp.int32, (channels, extent), 1)
-    at = lax.axis_index("seq")
+    at = seq_index()
     first = jnp.where(at == 0, own, 0)
     last = jnp.where(at == count - 1, 2 * own, extent)
     inside = (lane >= first) & (lane < last)
@@ -388,7 +406,8 @@
     disc_layer,
 ):
     groups = lax.axis_size("group")
-    seqs = lax.axis_size("seq")
+    planes = lax.axis_size("plane")
+    seqs = 2 * planes
     mps = lax.axis_size("mp")
     _, tokens, local_width = student_hidden.shape
     width = local_width * mps
@@ -401,9 +420,9 @@
 
     pieces = local_width // 128
     (mods,) = call(
-        smod_body, [((groups * seqs, pieces, 128), F32)], [], [student_cond, student_mod[:, 0]]
-    )
-    mods = exchange(mods, ("group", "seq"))
+        smod_body, [((groups * seqs, pieces, 128), BF16)], [], [student_cond, student_mod[:, 0]]
+    )
+    mods = exchange(mods, ("group",) + SEQ)
 
     tmod = jnp.einsum(
         "sf,fjd->sjd",
@@ -425,14 +444,14 @@
         for at in range(seqs)
         for m in range(mps)
     ]
-    got = lax.ppermute(sent, ("seq", "mp"), swap)
+    got = lax.ppermute(sent, SEQ + ("mp",), swap)
+    down_pair = lax.all_gather(down_weight.T, "core", axis=0, tiled=True)
+    up_pair = lax.all_gather(up_weight, "core", axis=0, tiled=True)
+    got = lax.all_gather(got, "core", axis=0, tiled=True)
     (terms,) = call(
-        weight_body,
-        [((seqs, units // seqs, lanes), BF16)],
-        [],
-        [got, down_weight.T, up_weight, mods],
-    )
-    terms = exchange(terms, "seq")
+        weight_body, [((planes, units // seqs, lanes), BF16)], [], [got, down_pair, up_pair, mods]
+    )
+    terms = exchange(terms, "plane")
     table = jnp.concatenate(
         [head_kernel.reshape(4, 9, channels), head_out[:, None], jnp.zeros((4, 6, channels), F32)],
         axis=1,
@@ -447,7 +466,7 @@
 
     (sums,) = call(
         sums_body,
-        [((2 * latent + 8, tokens), F32)],
+        [((latent + latent // 2 + 8, tokens), F32)],
         [],
         [student_hidden[0], student_out.T, teacher_embed, mods],
     )
@@ -458,8 +477,9 @@
         step *= 2
         stages.append(sums)
     halfway = stages[-2]
-    (terms,) = call(gather_body, [((seqs, units // seqs, lanes), BF16)], [], [terms, halfway])
-    weights = exchange(terms, "seq").reshape(units, lanes)
+    (terms,) = call(gather_body, [((planes, units // seqs, lanes), BF16)], [], [terms, halfway])
+    weights = exchange(terms, "plane").reshape(units // 2, lanes)
+    weights = lax.all_gather(weights, "core", axis=0, tiled=True)
 
     latents, noised = call(
         functools.partial(noise_body, width=float(width)),
@@ -468,19 +488,21 @@
         [sums, noise[0].T],
         loose=(0,),
     )
-    before = lax.ppermute(noised, "seq", [(i, i + 1) for i in range(seqs - 1)])
-    after = lax.ppermute(noised, "seq", [(i + 1, i) for i in range(seqs - 1)])
-
-    parts, preact, query, side = call(
+    swap = [(i, i + 1 if i % 2 else i - 1) for i in range(1, seqs - 1)]
+    edge = lax.ppermute(noised, SEQ, swap)
+    pair = lax.all_gather(noised, "core", axis=0, tiled=True)
+
+    parts, preact, query, side, wide = call(
         functools.partial(act_body, width=float(width)),
         [
             ((mps, share, extent + 2 * latent), BF16),
             ((units, tokens), F32),
             ((units, latent), BF16),
             ((latent + 8, tokens), F32),
+            ((latent, extent), BF16),
         ],
         [],
-        [sums, before, noised, after, weights, cross],
+        [sums, edge, pair, weights, cross],
         [((units, extent), BF16)],
     )
     parts = exchange(parts, "mp")
@@ -489,7 +511,7 @@
         functools.partial(conv_body, count=seqs),
         [((mps, share + 16, tokens), BF16), ((latent, tokens), F32)],
         [],
-        [parts, before, noised, after, taps],
+        [parts, wide, taps],
     )
     pay = exchange(pay, "mp")
     back, logits = call(
@@ -505,25 +527,29 @@
 
 
 def solution(mesh):
+    groups, seqs, mps = mesh.devices.shape
+    split = Mesh(
+        mesh.devices.reshape(groups, seqs // 2, 2, mps), ("group", "plane", "core", "mp")
+    )
     return jax.shard_map(
         per_device,
-        mesh=mesh,
+        mesh=split,
         in_specs=(
-            P("group", "seq", "mp"),
-            P(None, "seq"),
-            P("seq", "group", "mp"),
+            P("group", SEQ, "mp"),
+            P(None, SEQ),
+            P(SEQ, "group", "mp"),
             P("mp", None),
             P("group"),
-            P("group", "seq", None),
+            P("group", SEQ, None),
             P(None, "mp"),
             P(None, None, "mp"),
-            P("seq", "mp"),
-            P("mp", "seq"),
+            P(SEQ, "mp"),
+            P("mp", SEQ),
             P(None, "mp", None),
             P(),
             P(),
             P("group", None),
         ),
-        out_specs=(P("group", "seq", None), P("group", None, "seq"), P("group", "seq", None)),
+        out_specs=(P("group", SEQ, None), P("group", None, SEQ), P("group", SEQ, None)),
         check_vma=False,
     )

time: 142 us -> 141 us (level)
  the two profiles are of different devices: /device:TPU:14 before, /device:TPU:24 now
where the time goes in v1:
time: 141 us; the launch traced here: 140 us
  starting transfers between devices  64.7 us (46%)
  blocking collectives  44.5 us (32%)
  waiting for transfers between devices  15.8 us (11%)
  Pallas kernels  10.6 us (8%)
  local copies, waits for them, and re-layouts  2.27 us (2%)
  between operations  1.52 us (1%)
    all_to_all x4, starting transfers between devices, exchange(): return lax.all_to_all(value, axes, 0, 0, tiled=False)  45.8 us
    all_to_all x2, blocking collectives, exchange(): return lax.all_to_all(value, axes, 0, 0, tiled=False)  31.2 us
    ppermute x3, starting transfers between devices, per_device(): sums = sums + lax.ppermute(sums, 'mp', [(i, i ^ step) for i in range(mps)])  16.2 us
    pallas_call x11, Pallas kernels, call(): pl.pallas_call(body, in_specs=[smem] * len(scalars) + [vmem] * len(arrays...  10.6 us
    all_to_all x4, waiting for transfers between devices, exchange(): return lax.all_to_all(value, axes, 0, 0, tiled=False)  8.53 us
    ppermute x3, waiting for transfers between devices, per_device(): sums = sums + lax.ppermute(sums, 'mp', [(i, i ^ step) for i in range(mps)])  7.26 us
    all_gather x1, blocking collectives, per_device(): pair = lax.all_gather(noised, 'core', axis=0, tiled=True)  5.16 us
  transfers between devices with their start and end apart: 9, of which 4 were waited for; matrix products, arithmetic and copies ran while one was open for 1% of the time, Pallas kernels for 2%

profile of v1, /device:TPU:24, one launch (start us, length us, event | category | flops | bytes accessed | tf_op | source)
XLA Modules:
  0.0 140.1 jit_solution(14360668895885008957)
XLA Ops:
  0.6 0.0 copy-start
  0.6 0.0 copy-start.1
  0.7 0.0 copy-start.4
  0.7 0.9 copy-done.4
  1.6 0.7 copy-done.7
  2.3 0.8 shard_map.157
  3.1 10.5 %all-to-all-start = ((bf16[64,3,128]{2,1,0:T(4,128)(2,1)}), bf16[64,3,128]{2,1,0:T(4,128)(2,1)S(1)}, u32[]{:S(2)}, u32[]{:S(2)}) async-start(bf16[64,3,128]{2,1,0:T(4,128)(2,1)} %shard_map.157), calls=%async_computation | async-start | bytes 131072 | tf_op jit(solution)/shard_map/all_to_all | solution.py:62
  14.2 0.1 fusion.9
  14.3 0.0 copy-done
  14.3 0.0 copy-start.2
  14.3 0.3 fusion.5
  14.6 0.0 copy-done.1
  14.6 0.5 copy-done.2
  15.1 0.0 copy-start.8
  15.1 0.9 shard_map.160
  16.0 0.0 copy-start.9
  16.1 0.8 collective-permute-start.4
  16.9 0.0 copy-done.8
  16.9 2.0 %all_gather.18.up_ref = bf16[192,768]{1,0:T(8,128)(2,1)S(1)} all-gather(bf16[96,768]{1,0:T(8,128)(2,1)S(1)} %copy-done.8), channel_id=1, replica_groups=mesh['group'=2,'plane'=16,'core'=2,'mp'=8] {'core'}, dimensions={0}, use_global_device_ids=true | all-gather | bytes 442368 | tf_op jit(solution)/shard_map/all_gather | solution.py:449
  18.9 0.0 copy-done.9
  18.9 2.0 %all_gather.17.down_ref = bf16[192,768]{1,0:T(8,128)(2,1)S(1)} all-gather(bf16[96,768]{1,0:T(8,128)(2,1)S(1)} %bitcast.32), channel_id=1, replica_groups=mesh['group'=2,'plane'=16,'core'=2,'mp'=8] {'core'}, dimensions={0}, use_global_device_ids=true | all-gather | bytes 442368 | tf_op jit(solution)/shard_map/all_gather | solution.py:448
  20.9 0.0 collective-permute-done.4
  20.9 1.9 %all_gather.16.got_ref = bf16[192,384]{1,0:T(8,128)(2,1)S(1)} all-gather(bf16[96,384]{1,0:T(8,128)(2,1)S(1)} %collective-permute-done.4), channel_id=1, replica_groups=mesh['group'=2,'plane'=16,'core'=2,'mp'=8] {'core'}, dimensions={0}, use_global_device_ids=true | all-gather | bytes 221184 | tf_op jit(solution)/shard_map/all_gather | solution.py:450
  22.8 0.0 all-to-all-done.mod_ref.order_ref
  22.8 1.0 shard_map.161
  23.8 0.0 copy-start.3
  23.8 0.0 copy-start.5
  23.8 22.3 %all-to-all-start.1 = ((bf16[16,24,384]{2,1,0:T(8,128)(2,1)}), bf16[16,24,384]{2,1,0:T(8,128)(2,1)S(1)}, u32[]{:S(2)}, u32[]{:S(2)}) async-start(bf16[16,24,384]{2,1,0:T(8,128)(2,1)} %shard_map.161), calls=%async_computation.1 | async-start | bytes 589824 | tf_op jit(solution)/shard_map/all_to_all | solution.py:62
  46.1 0.0 copy-done.3
  46.1 0.0 copy-done.5
  46.1 0.5 shard_map.158
  46.6 1.9 %collective-permute-start = (f32[104,128]{1,0:T(8,128)S(1)}, f32[104,128]{1,0:T(8,128)S(1)}, u32[]{:S(2)}, u32[]{:S(2)}) collective-permute-start(f32[104,128]{1,0:T(8,128)S(1)} %shard_map.158), channel_id=1, source_target_pairs={{0,1},{1,0},{2,3},{3,2},{4,5},{5,4},{6,7},{7,6},{8,9},{9,8},{10,11... | collective-permute-start | bytes 159752 | tf_op jit(solution)/shard_map/ppermute | solution.py:476
  48.5 4.1 %collective-permute-done = f32[104,128]{1,0:T(8,128)S(1)} collective-permute-done((f32[104,128]{1,0:T(8,128)S(1)}, f32[104,128]{1,0:T(8,128)S(1)}, u32[]{:S(2)}, u32[]{:S(2)}) %collective-permute-start) | collective-permute-done | bytes 53280 | tf_op jit(solution)/shard_map/ppermute | solution.py:476
  52.6 5.9 %collective-permute-start.1 = (f32[104,128]{1,0:T(8,128)S(1)}, f32[104,128]{1,0:T(8,128)S(1)}, u32[]{:S(2)}, u32[]{:S(2)}) collective-permute-start(f32[104,128]{1,0:T(8,128)S(1)} %add.21), channel_id=1, source_target_pairs={{0,2},{1,3},{2,0},{3,1},{4,6},{5,7},{6,4},{7,5},{8,10},{9,11},{10,... | collective-permute-start | bytes 159752 | tf_op jit(solution)/shard_map/ppermute | solution.py:476
  58.5 2.1 %collective-permute-done.1 = f32[104,128]{1,0:T(8,128)S(1)} collective-permute-done((f32[104,128]{1,0:T(8,128)S(1)}, f32[104,128]{1,0:T(8,128)S(1)}, u32[]{:S(2)}, u32[]{:S(2)}) %collective-permute-start.1) | collective-permute-done | bytes 53280 | tf_op jit(solution)/shard_map/ppermute | solution.py:476
  60.6 0.0 all-to-all-done.1.parts_ref
  60.6 0.8 shard_map.162
  61.4 0.0 copy-start.10
  61.4 9.8 %all-to-all-start.2 = ((bf16[16,24,384]{2,1,0:T(8,128)(2,1)}), bf16[16,24,384]{2,1,0:T(8,128)(2,1)S(1)}, u32[]{:S(2)}, u32[]{:S(2)}) async-start(bf16[16,24,384]{2,1,0:T(8,128)(2,1)} %shard_map.162), calls=%async_computation.2 | async-start | bytes 589824 | tf_op jit(solution)/shard_map/all_to_all | solution.py:62
  71.1 0.0 copy-done.10
  71.2 0.0 copy-start.11
  71.2 0.1 pad.2.clone
  71.2 8.4 %collective-permute-start.2 = (f32[104,128]{1,0:T(8,128)S(1)}, f32[104,128]{1,0:T(8,128)S(1)}, u32[]{:S(2)}, u32[]{:S(2)}) collective-permute-start(f32[104,128]{1,0:T(8,128)S(1)} %add.22.order_ref), channel_id=1, source_target_pairs={{0,4},{1,5},{2,6},{3,7},{4,0},{5,1},{6,2},{7,3},{8,12},{9,13},{10,... | collective-permute-start | bytes 159752 | tf_op jit(solution)/shard_map/ppermute | solution.py:476
  79.6 0.0 copy-done.11
  79.7 0.1 maximum_maximum_fusion.table_ref
  79.7 1.0 shard_map.163
  80.8 0.0 copy-start.6
  80.8 1.0 collective-permute-done.2
  81.9 0.0 copy-done.6
  81.9 0.9 shard_map.159
  82.8 1.9 %collective-permute-start.3 = (bf16[64,128]{1,0:T(8,128)(2,1)S(1)}, bf16[64,128]{1,0:T(8,128)(2,1)S(1)}, u32[]{:S(2)}, u32[]{:S(2)}) collective-permute-start(bf16[64,128]{1,0:T(8,128)(2,1)S(1)} %get-tuple-element.17.noised_ref), channel_id=1, source_target_pairs={{8,16},{16,8},{24,32},{32,24},{40,48},{48,40},{56,64},{64,56},{72,... | collective-permute-start | bytes 49160 | tf_op jit(solution)/shard_map/ppermute | solution.py:492
  84.7 5.2 %all_gather.15.pair_ref = bf16[128,128]{1,0:T(8,128)(2,1)S(1)} all-gather(bf16[64,128]{1,0:T(8,128)(2,1)S(1)} %get-tuple-element.17.noised_ref), channel_id=1, replica_groups=mesh['group'=2,'plane'=16,'core'=2,'mp'=8] {'core'}, dimensions={0}, use_global_device_ids=true | all-gather | bytes 49152 | tf_op jit(solution)/shard_map/all_gather | solution.py:493
  89.9 0.0 all-to-all-done.2
  89.9 2.2 %all_gather.19.weights_ref = bf16[768,384]{1,0:T(8,128)(2,1)S(1)} all-gather(bf16[384,384]{1,0:T(8,128)(2,1)S(1)} %bitcast.31), channel_id=1, replica_groups=mesh['group'=2,'plane'=16,'core'=2,'mp'=8] {'core'}, dimensions={0}, use_global_device_ids=true | all-gather | bytes 884736 | tf_op jit(solution)/shard_map/all_gather | solution.py:482
  92.1 0.0 collective-permute-done.3.cross_noised_ref
  92.1 1.2 shard_map.164
  93.3 19.8 %all_to_all.30.parts_ref = bf16[8,32,512]{2,1,0:T(8,128)(2,1)S(1)} all-to-all(bf16[8,32,512]{2,1,0:T(8,128)(2,1)S(1)} %get-tuple-element.19), channel_id=1, replica_groups=mesh['group'=2,'plane'=16,'core'=2,'mp'=8] {'mp'}, dimensions={0} | all-to-all | bytes 524288 | tf_op jit(solution)/shard_map/all_to_all | solution.py:62
  113.1 1.2 shard_map.165
  114.3 3.4 %all-to-all-start.4 = ((bf16[8,48,128]{2,1,0:T(8,128)(2,1)}), bf16[8,48,128]{2,1,0:T(8,128)(2,1)S(1)}, u32[]{:S(2)}, u32[]{:S(2)}) async-start(bf16[8,48,128]{2,1,0:T(8,128)(2,1)} %get-tuple-element.22), calls=%async_computation.4 | async-start | bytes 196608 | tf_op jit(solution)/shard_map/all_to_all | solution.py:62
  117.7 0.2 fusion.4.slope_ref
  117.9 8.5 %all-to-all-done.4.pay_ref = bf16[8,48,128]{2,1,0:T(8,128)(2,1)S(1)} async-done(((bf16[8,48,128]{2,1,0:T(8,128)(2,1)}), bf16[8,48,128]{2,1,0:T(8,128)(2,1)S(1)}, u32[]{:S(2)}, u32[]{:S(2)}) %all-to-all-start.4) | async-done | bytes 98336 | tf_op jit(solution)/shard_map/all_to_all | solution.py:62
  126.4 1.6 %shard_map.166 = (bf16[8,64,128]{2,1,0:T(8,128)(2,1)S(1)}, f32[4,128]{1,0:T(4,128)}) custom-call(s32[1,4]{1,0:T(1,128)} %disc_ref.5, bf16[8,48,128]{2,1,0:T(8,128)(2,1)S(1)} %all-to-all-done.4.pay_ref, bf16[768,384]{1,0:T(8,128)(2,1)S(1)} %all_gather.19.weights_ref, bf16[768,64]{1,0:T(8,128)(2,1)S(1)} %get-tuple-element.23.query_ref, ...), custom_call_target="tpu_custom_call" | custom-call | tf_op jit(solution)/shard_map/pallas_call | solution.py:76
  128.0 11.5 %all_to_all.31.parts_ref = bf16[8,64,128]{2,1,0:T(8,128)(2,1)S(1)} all-to-all(bf16[8,64,128]{2,1,0:T(8,128)(2,1)S(1)} %get-tuple-element.28), channel_id=1, replica_groups=mesh['group'=2,'plane'=16,'core'=2,'mp'=8] {'mp'}, dimensions={0} | all-to-all | bytes 262144 | tf_op jit(solution)/shard_map/all_to_all | solution.py:62
  139.5 0.6 shard_map.167
  (7 shorter events, 0.0 us)
Async XLA Ops:
  0.6 13.7 %copy-start = (bf16[256,2,384]{2,1,0:T(2,128)(2,1)S(1)}, bf16[256,2,384]{2,1,0:T(2,128)(2,1)}, u32[]{:S(2)}) copy-start(bf16[256,2,384]{2,1,0:T(2,128)(2,1)} %param.21) | copy-start | bytes 1179652
  0.6 14.0 %copy-start.1 = (bf16[4,384,128]{2,1,0:T(8,128)(2,1)S(1)}, bf16[4,384,128]{2,1,0:T(8,128)(2,1)}, u32[]{:S(2)}) copy-start(bf16[4,384,128]{2,1,0:T(8,128)(2,1)} %proj_ref.3) | copy-start | bytes 1179652
  0.7 1.0 copy-start.4
  1.6 0.7 copy-start.7
  3.1 19.7 %all-to-all-start = ((bf16[64,3,128]{2,1,0:T(4,128)(2,1)}), bf16[64,3,128]{2,1,0:T(4,128)(2,1)S(1)}, u32[]{:S(2)}, u32[]{:S(2)}) async-start(bf16[64,3,128]{2,1,0:T(4,128)(2,1)} %shard_map.157), calls=%async_computation | async-start | bytes 131072 | tf_op jit(solution)/shard_map/all_to_all | solution.py:62
  14.3 0.8 copy-start.2
  15.1 1.8 %copy-start.8 = (bf16[96,768]{1,0:T(8,128)(2,1)S(1)}, bf16[96,768]{1,0:T(8,128)(2,1)}, u32[]{:S(2)}) copy-start(bf16[96,768]{1,0:T(8,128)(2,1)} %param.22) | copy-start | bytes 442372
  16.0 2.8 %copy-start.9 = (bf16[768,96]{0,1:T(8,128)(2,1)S(1)}, bf16[768,96]{0,1:T(8,128)(2,1)}, u32[]{:S(2)}) copy-start(bf16[768,96]{0,1:T(8,128)(2,1)} %param.23) | copy-start | bytes 442372
  16.1 4.8 %collective-permute-start.4 = (bf16[96,384]{1,0:T(8,128)(2,1)S(1)}, bf16[96,384]{1,0:T(8,128)(2,1)S(1)}, u32[]{:S(2)}, u32[]{:S(2)}) collective-permute-start(bf16[96,384]{1,0:T(8,128)(2,1)S(1)} %shard_map.160), channel_id=1, source_target_pairs={{0,0},{1,32},{2,64},{3,96},{4,128},{5,160},{6,192},{7,224},{8,8},{... | collective-permute-start | bytes 221192 | tf_op jit(solution)/shard_map/ppermute | solution.py:447
  23.8 22.3 %copy-start.3 = (bf16[1,128,384]{2,1,0:T(8,128)(2,1)S(1)}, bf16[1,128,384]{2,1,0:T(8,128)(2,1)}, u32[]{:S(2)}) copy-start(bf16[1,128,384]{2,1,0:T(8,128)(2,1)} %param.14) | copy-start | bytes 294916
  23.8 22.3 %copy-start.5 = (bf16[384,64]{0,1:T(8,128)(2,1)S(1)}, bf16[384,64]{0,1:T(8,128)(2,1)}, u32[]{:S(2)}) copy-start(bf16[384,64]{0,1:T(8,128)(2,1)} %param.17) | copy-start | bytes 147460
  23.8 36.8 %all-to-all-start.1 = ((bf16[16,24,384]{2,1,0:T(8,128)(2,1)}), bf16[16,24,384]{2,1,0:T(8,128)(2,1)S(1)}, u32[]{:S(2)}, u32[]{:S(2)}) async-start(bf16[16,24,384]{2,1,0:T(8,128)(2,1)} %shard_map.161), calls=%async_computation.1 | async-start | bytes 589824 | tf_op jit(solution)/shard_map/all_to_all | solution.py:62
  46.6 6.0 %collective-permute-start = (f32[104,128]{1,0:T(8,128)S(1)}, f32[104,128]{1,0:T(8,128)S(1)}, u32[]{:S(2)}, u32[]{:S(2)}) collective-permute-start(f32[104,128]{1,0:T(8,128)S(1)} %shard_map.158), channel_id=1, source_target_pairs={{0,1},{1,0},{2,3},{3,2},{4,5},{5,4},{6,7},{7,6},{8,9},{9,8},{10,11... | collective-permute-start | bytes 159752 | tf_op jit(solution)/shard_map/ppermute | solution.py:476
  52.6 8.0 %collective-permute-start.1 = (f32[104,128]{1,0:T(8,128)S(1)}, f32[104,128]{1,0:T(8,128)S(1)}, u32[]{:S(2)}, u32[]{:S(2)}) collective-permute-start(f32[104,128]{1,0:T(8,128)S(1)} %add.21), channel_id=1, source_target_pairs={{0,2},{1,3},{2,0},{3,1},{4,6},{5,7},{6,4},{7,5},{8,10},{9,11},{10,... | collective-permute-start | bytes 159752 | tf_op jit(solution)/shard_map/ppermute | solution.py:476
  61.4 9.8 %copy-start.10 = (f32[4,3,3,128]{3,0,2,1:T(4,128)S(1)}, f32[4,3,3,128]{3,0,2,1:T(4,128)}, u32[]{:S(2)}) copy-start(f32[4,3,3,128]{3,0,2,1:T(4,128)} %param.25) | copy-start | bytes 55300
  61.4 28.5 %all-to-all-start.2 = ((bf16[16,24,384]{2,1,0:T(8,128)(2,1)}), bf16[16,24,384]{2,1,0:T(8,128)(2,1)S(1)}, u32[]{:S(2)}, u32[]{:S(2)}) async-start(bf16[16,24,384]{2,1,0:T(8,128)(2,1)} %shard_map.162), calls=%async_computation.2 | async-start | bytes 589824 | tf_op jit(solution)/shard_map/all_to_all | solution.py:62
  71.2 8.5 %copy-start.11 = (f32[4,128]{1,0:T(4,128)S(1)}, f32[4,128]{1,0:T(4,128)}, u32[]{:S(2)}) copy-start(f32[4,128]{1,0:T(4,128)} %param.26) | copy-start | bytes 6148
  71.2 10.6 %collective-permute-start.2 = (f32[104,128]{1,0:T(8,128)S(1)}, f32[104,128]{1,0:T(8,128)S(1)}, u32[]{:S(2)}, u32[]{:S(2)}) collective-permute-start(f32[104,128]{1,0:T(8,128)S(1)} %add.22.order_ref), channel_id=1, source_target_pairs={{0,4},{1,5},{2,6},{3,7},{4,0},{5,1},{6,2},{7,3},{8,12},{9,13},{10,... | collective-permute-start | bytes 159752 | tf_op jit(solution)/shard_map/ppermute | solution.py:476
  80.8 1.1 copy-start.6
  82.8 9.3 %collective-permute-start.3 = (bf16[64,128]{1,0:T(8,128)(2,1)S(1)}, bf16[64,128]{1,0:T(8,128)(2,1)S(1)}, u32[]{:S(2)}, u32[]{:S(2)}) collective-permute-start(bf16[64,128]{1,0:T(8,128)(2,1)S(1)} %get-tuple-element.17.noised_ref), channel_id=1, source_target_pairs={{8,16},{16,8},{24,32},{32,24},{40,48},{48,40},{56,64},{64,56},{72,... | collective-permute-start | bytes 49160 | tf_op jit(solution)/shard_map/ppermute | solution.py:492
  114.3 12.1 %all-to-all-start.4 = ((bf16[8,48,128]{2,1,0:T(8,128)(2,1)}), bf16[8,48,128]{2,1,0:T(8,128)(2,1)S(1)}, u32[]{:S(2)}, u32[]{:S(2)}) async-start(bf16[8,48,128]{2,1,0:T(8,128)(2,1)} %get-tuple-element.22), calls=%async_computation.4 | async-start | bytes 196608 | tf_op jit(solution)/shard_map/all_to_all | solution.py:62

commit v2 on v1

--- a/solution.py
+++ b/solution.py
@@ -62,7 +62,7 @@
     return lax.all_to_all(value, axes, 0, 0, tiled=False)
 
 
-def call(body, outs, scalars, arrays, scratch=(), loose=()):
+def call(body, outs, scalars, arrays, scratch=(), loose=(), distant=(), plain=()):
     smem = pl.BlockSpec(memory_space=pltpu.SMEM)
     vmem = pl.BlockSpec(memory_space=pltpu.VMEM)
     if INTERPRET:
@@ -72,15 +72,21 @@
             jax.ShapeDtypeStruct(*out) if place in loose else pltpu.VMEM(*out)
             for place, out in enumerate(outs)
         ]
-        arrays = [pltpu.with_memory_space_constraint(value, pltpu.VMEM) for value in arrays]
+        arrays = [
+            value if place in plain else pltpu.with_memory_space_constraint(value, pltpu.VMEM)
+            for place, value in enumerate(arrays)
+        ]
     return pl.pallas_call(
         body,
-        in_specs=[smem] * len(scalars) + [vmem] * len(arrays),
+        in_specs=[smem] * len(scalars)
+        + [vmem] * len(arrays)
+        + [pl.BlockSpec(memory_space=pl.ANY)] * len(distant),
         out_specs=[vmem] * len(outs),
         out_shape=shapes,
-        scratch_shapes=[pltpu.VMEM(shape, dtype) for shape, dtype in scratch],
+        scratch_shapes=[pltpu.VMEM(shape, dtype) for shape, dtype in scratch]
+        + [pltpu.SemaphoreType.DMA] * len(distant),
         interpret=INTERPRET,
-    )(*scalars, *arrays)
+    )(*scalars, *arrays, *distant)
 
 
 def pick_heads(disc_ref):
@@ -97,83 +103,104 @@
     return time_ref[0].astype(F32) / 1000.0
 
 
-def smod_body(cond_ref, mod_ref, out_ref):
-    groups = cond_ref.shape[0]
-    copies, pieces, lanes = out_ref.shape
-    seqs = copies // groups
-    half = contract(cond_ref[...], mod_ref[...].astype(F32), 1, 0, HIGHEST)
-    for group in range(groups):
-        row = half[group : group + 1]
-        block = jnp.concatenate(
-            [row[:, lanes * p : lanes * (p + 1)] for p in range(pieces)], axis=0
-        )
-        out_ref[seqs * group : seqs * (group + 1)] = jnp.broadcast_to(
-            block.astype(BF16)[None], (seqs, pieces, lanes)
-        )
-
-
-def prep_body(disc_ref, tmod_ref, embed_ref, proj_ref, out_ref, turned_ref):
-    rows = out_ref.shape[0]
+def open_body(
+    disc_ref,
+    cond_ref,
+    mod_ref,
+    tmod_ref,
+    embed_ref,
+    proj_ref,
+    taps_in_ref,
+    head_out_ref,
+    noise_in_ref,
+    sent_ref,
+    mods_ref,
+    cross_ref,
+    taps_ref,
+    noise_ref,
+    queries_ref,
+    turned_ref,
+    noise_sem,
+):
+    fetch = pltpu.make_async_copy(noise_in_ref, noise_ref, noise_sem)
+    fetch.start()
+    block, other = pick_heads(disc_ref)
     channels = proj_ref.shape[2]
-    width = embed_ref.shape[1]
-    latent = embed_ref.shape[0]
-    start = (seq_index() % (width // rows)) * rows
+    latent, width = embed_ref.shape
+
+    rows = sent_ref.shape[0]
+    start = pl.multiple_of((seq_index() % (width // rows)) * rows, rows)
+    embed = embed_ref[...]
     gain = 1.0 + tmod_ref[1:2]
     queries = jnp.concatenate(
         [
-            embed_ref[...].astype(F32) * gain,
+            embed.astype(F32) * gain,
             gain,
             tmod_ref[0:1],
             jnp.zeros((128 - latent - 2, width), F32),
         ],
         axis=0,
     )
-    turned_ref[...] = queries.T
-    out_ref[:, 2 * channels :] = turned_ref[pl.ds(start, rows), :].astype(BF16)
-    for place, head in enumerate(pick_heads(disc_ref)[0]):
-        out_ref[:, channels * place : channels * (place + 1)] = proj_ref[head, pl.ds(start, rows), :]
-
-
-def weight_body(got_ref, down_ref, up_ref, order_ref, out_ref):
-    del order_ref
-    copies, rows, lanes = out_ref.shape
-    split = lanes - 128
-    half = pl.ds(pl.multiple_of(lax.axis_index("core") * (copies * rows), 128), copies * rows)
-    terms = jnp.concatenate(
-        [
-            contract(down_ref[:, half], got_ref[:, :split], 0, 0),
-            contract(up_ref[:, half], got_ref[:, split:], 0, 0),
-        ],
-        axis=1,
-    )
-    out_ref[...] = terms.astype(BF16).reshape(copies, rows, lanes)
-
-
-def gather_body(parts_ref, order_ref, out_ref):
-    del order_ref
-    total = jnp.sum(parts_ref[...].astype(F32), axis=0).astype(BF16)
-    out_ref[...] = jnp.broadcast_to(total[None], out_ref.shape)
-
-
-def cross_body(disc_ref, proj_ref, embed_ref, table_ref, cross_ref, taps_ref, turned_ref):
-    _, share, lanes = cross_ref.shape
-    channels = proj_ref.shape[2]
+    queries_ref[...] = queries.T
+    sent_ref[:, 2 * channels :] = queries_ref[pl.ds(start, rows), :].astype(BF16)
+    for place, head in enumerate(block):
+        sent_ref[:, channels * place : channels * (place + 1)] = proj_ref[head, pl.ds(start, rows), :]
+
+    groups = cond_ref.shape[0]
+    copies, pieces, lanes = mods_ref.shape
+    seqs = copies // groups
+    half = contract(cond_ref[...], mod_ref[...].astype(F32), 1, 0, HIGHEST)
+    for group in range(groups):
+        row = half[group : group + 1]
+        pieces_of = jnp.concatenate(
+            [row[:, lanes * p : lanes * (p + 1)] for p in range(pieces)], axis=0
+        )
+        mods_ref[seqs * group : seqs * (group + 1)] = jnp.broadcast_to(
+            pieces_of.astype(BF16)[None], (seqs, pieces, lanes)
+        )
+
+    _, share, pair_lanes = cross_ref.shape
     per_head = channels // share
     begin = lax.axis_index("mp") * share
     slot = begin // channels
     offset = pl.multiple_of(begin % channels, 8)
-    embed = embed_ref[...]
-    block, other = pick_heads(disc_ref)
     for place in range(2):
         both = jnp.concatenate(
             [contract(proj_ref[head], embed, 0, 1) for head in (block[place], other[place])], axis=1
         )
         cross_ref[per_head * place : per_head * (place + 1)] = (
-            both.astype(BF16).reshape(per_head, share, lanes)
+            both.astype(BF16).reshape(per_head, share, pair_lanes)
         )
     for place, pair in enumerate((block, other)):
-        turned_ref[...] = table_ref[jnp.where(slot == 0, pair[0], pair[1])].T
+        head = jnp.where(slot == 0, pair[0], pair[1])
+        table = jnp.concatenate(
+            [taps_in_ref[tap, pl.ds(head, 1), :] for tap in range(9)]
+            + [head_out_ref[pl.ds(head, 1), :], jnp.zeros((6, channels), F32)],
+            axis=0,
+        )
+        turned_ref[...] = table.T
         taps_ref[share * place : share * (place + 1)] = turned_ref[pl.ds(offset, share), :]
+    fetch.wait()
+
+
+def weight_body(got_ref, pair_ref, order_ref, out_ref):
+    del order_ref
+    copies, rows, lanes = out_ref.shape
+    split = lanes - 128
+    depth = got_ref.shape[0] // 2
+    half = pl.ds(pl.multiple_of(lax.axis_index("core") * (copies * rows), 128), copies * rows)
+    down = jnp.concatenate([pair_ref[0:depth, half], pair_ref[2 * depth : 3 * depth, half]], axis=0)
+    up = jnp.concatenate([pair_ref[depth : 2 * depth, half], pair_ref[3 * depth :, half]], axis=0)
+    terms = jnp.concatenate(
+        [contract(down, got_ref[:, :split], 0, 0), contract(up, got_ref[:, split:], 0, 0)], axis=1
+    )
+    out_ref[...] = terms.astype(BF16).reshape(copies, rows, lanes)
+
+
+def gather_body(parts_ref, order_ref, out_ref):
+    del order_ref
+    total = jnp.sum(parts_ref[...].astype(F32), axis=0).astype(BF16)
+    out_ref[...] = jnp.broadcast_to(total[None], out_ref.shape)
 
 
 def sums_body(hidden_ref, out_w_ref, embed_ref, mod_ref, sums_ref):
@@ -418,12 +445,6 @@
     lanes = 2 * channels + 128
     extent = 3 * tokens
 
-    pieces = local_width // 128
-    (mods,) = call(
-        smod_body, [((groups * seqs, pieces, 128), BF16)], [], [student_cond, student_mod[:, 0]]
-    )
-    mods = exchange(mods, ("group",) + SEQ)
-
     tmod = jnp.einsum(
         "sf,fjd->sjd",
         time_features(timestep, teacher_mod.shape[0]),
@@ -432,38 +453,44 @@
     )[0]
     ratio = seqs // mps
     rows = local_width // ratio
-    (sent,) = call(
-        prep_body,
-        [((rows, lanes), BF16)],
+    pieces = local_width // 128
+    sent, mods, cross, taps, noise_t = call(
+        open_body,
+        [
+            ((rows, lanes), BF16),
+            ((groups * seqs, pieces, 128), BF16),
+            ((mps, share, 2 * latent), BF16),
+            ((2 * share, 16), F32),
+            ((latent, tokens), BF16),
+        ],
         [disc_layer],
-        [tmod, teacher_embed, head_proj],
-        [((local_width, 128), F32)],
-    )
+        [
+            student_cond,
+            student_mod[:, 0],
+            tmod,
+            teacher_embed,
+            head_proj,
+            jnp.transpose(head_kernel, (1, 2, 0, 3)).reshape(9, 4, channels),
+            head_out,
+        ],
+        [((local_width, 128), F32), ((channels, 16), F32)],
+        distant=[noise[0].T],
+        plain=(0, 1, 3, 5, 6),
+    )
+
     swap = [
         (at * mps + m, (ratio * m + at % ratio) * mps + at // ratio)
         for at in range(seqs)
         for m in range(mps)
     ]
     got = lax.ppermute(sent, SEQ + ("mp",), swap)
-    down_pair = lax.all_gather(down_weight.T, "core", axis=0, tiled=True)
-    up_pair = lax.all_gather(up_weight, "core", axis=0, tiled=True)
+
+    mods = exchange(mods, ("group",) + SEQ)
+    slices = jnp.concatenate([down_weight.T, up_weight], axis=0)
+    slices = lax.all_gather(slices, "core", axis=0, tiled=True)
     got = lax.all_gather(got, "core", axis=0, tiled=True)
-    (terms,) = call(
-        weight_body, [((planes, units // seqs, lanes), BF16)], [], [got, down_pair, up_pair, mods]
-    )
+    (terms,) = call(weight_body, [((planes, units // seqs, lanes), BF16)], [], [got, slices, mods])
     terms = exchange(terms, "plane")
-    table = jnp.concatenate(
-        [head_kernel.reshape(4, 9, channels), head_out[:, None], jnp.zeros((4, 6, channels), F32)],
-        axis=1,
-    )
-    cross, taps = call(
-        cross_body,
-        [((mps, share, 2 * latent), BF16), ((2 * share, 16), F32)],
-        [disc_layer],
-        [head_proj, teacher_embed, table],
-        [((channels, 16), F32)],
-    )
-
     (sums,) = call(
         sums_body,
         [((latent + latent // 2 + 8, tokens), F32)],
@@ -485,7 +512,7 @@
         functools.partial(noise_body, width=float(width)),
         [((latent, tokens), BF16), ((latent, tokens), BF16)],
         [timestep],
-        [sums, noise[0].T],
+        [sums, noise_t],
         loose=(0,),
     )
     swap = [(i, i + 1 if i % 2 else i - 1) for i in range(1, seqs - 1)]

time: 141 us -> 139 us (0.986)
  waiting for transfers between devices: 15.8 us -> 19.2 us
  local copies, waits for them, and re-layouts: 2.27 us -> 0.26 us
  blocking collectives: 44.5 us -> 42.7 us
    all_to_all x4, waiting for transfers between devices: 8.53 us -> 10.8 us  [exchange(): return lax.all_to_all(value, axes, 0, 0, tiled=False)]
    unnamed x24 -> x14, local copies, waits for them, and re-layouts: 2.19 us -> 0.26 us
    all_gather x2 -> x1, blocking collectives: 4.02 us -> 2.23 us  [per_device(): slices = lax.all_gather(slices, 'core', axis=0, tiled=True)]
    pallas_call x11 -> x9, Pallas kernels: 10.6 us -> 10.2 us  [call(): pl.pallas_call(body, in_specs=[smem] * len(scalars) + [vmem] * len(arrays...]
  transfers between devices with their start and end apart: 9 -> 9, of which waited for: 4 -> 5; matrix products, arithmetic and copies ran while one was open for 1% -> 0% of each run, Pallas kernels for 2% -> 1%
where the time goes in v2:
time: 139 us
  starting transfers between devices  64 us (46%)
  blocking collectives  42.7 us (31%)
  waiting for transfers between devices  19.2 us (14%)
  Pallas kernels  10.2 us (7%)
  between operations  1.53 us (1%)
    all_to_all x4, starting transfers between devices, exchange(): return lax.all_to_all(value, axes, 0, 0, tiled=False)  45.2 us
    all_to_all x2, blocking collectives, exchange(): return lax.all_to_all(value, axes, 0, 0, tiled=False)  31.2 us
    ppermute x3, starting transfers between devices, per_device(): sums = sums + lax.ppermute(sums, 'mp', [(i, i ^ step) for i in range(mps)])  16.2 us
    all_to_all x4, waiting for transfers between devices, exchange(): return lax.all_to_all(value, axes, 0, 0, tiled=False)  10.8 us
    pallas_call x9, Pallas kernels, call(): pl.pallas_call(body, in_specs=[smem] * len(scalars) + [vmem] * len(arrays...  10.2 us
    ppermute x3, waiting for transfers between devices, per_device(): sums = sums + lax.ppermute(sums, 'mp', [(i, i ^ step) for i in range(mps)])  8.41 us
    all_gather x1, blocking collectives, per_device(): pair = lax.all_gather(noised, 'core', axis=0, tiled=True)  5.16 us
  transfers between devices with their start and end apart: 9, of which 5 were waited for; matrix products, arithmetic and copies ran while one was open for 0% of the time, Pallas kernels for 1%

profile of v2, /device:TPU:24, one launch (start us, length us, event | category | flops | bytes accessed | tf_op | source)
XLA Modules:
  0.0 138.5 jit_solution(5236718426112839335)
XLA Ops:
  0.6 0.0 copy-start
  0.6 0.0 copy-start.1
  1.4 0.1 fusion.9
  1.4 0.2 copy-done
  1.6 0.3 fusion.5
  1.9 0.0 copy-done.1
  1.9 0.0 copy-start.5
  1.9 0.0 copy-start.6
  2.0 2.4 %shard_map.157 = (bf16[96,384]{1,0:T(8,128)(2,1)S(1)}, bf16[64,3,128]{2,1,0:T(4,128)(2,1)}, bf16[8,32,128]{2,1,0:T(8,128)(2,1)S(1)}, f32[64,16]{1,0:T(8,128)S(1)}, bf16[64,128]{1,0:T(8,128)(2,1)S(1)}) custom-call(s32[1,4]{1,0:T(1,128)} %disc_ref.3, f32[2,96]{1,0:T(2,128)} %cond_ref.1, bf16[96,384]{1,0:T(8,128)(2,1)} %bitcast.32, f32[2,384]{1,0:T(2,128)S(1)} %bitcast.29, ...), custom_call_target="tpu_custom_call" | custom-call | tf_op jit(solution)/shard_map/pallas_call | solution.py:79
  4.4 10.5 %all-to-all-start = ((bf16[64,3,128]{2,1,0:T(4,128)(2,1)}), bf16[64,3,128]{2,1,0:T(4,128)(2,1)S(1)}, u32[]{:S(2)}, u32[]{:S(2)}) async-start(bf16[64,3,128]{2,1,0:T(4,128)(2,1)} %get-tuple-element.19), calls=%async_computation | async-start | bytes 131072 | tf_op jit(solution)/shard_map/all_to_all | solution.py:62
  14.9 0.7 collective-permute-start.4
  15.5 0.0 copy-done.5
  15.5 0.0 copy-done.6
  15.6 2.2 %all_gather.14.pair_ref = bf16[384,768]{1,0:T(8,128)(2,1)S(1)} all-gather(bf16[192,768]{1,0:T(8,128)(2,1)S(1)} %pad_maximum_fusion), channel_id=1, replica_groups=mesh['group'=2,'plane'=16,'core'=2,'mp'=8] {'core'}, dimensions={0}, use_global_device_ids=true | all-gather | bytes 884736 | tf_op jit(solution)/shard_map/all_gather | solution.py:490
  17.8 0.0 collective-permute-done.4
  17.8 1.9 %all_gather.13.got_ref = bf16[192,384]{1,0:T(8,128)(2,1)S(1)} all-gather(bf16[96,384]{1,0:T(8,128)(2,1)S(1)} %collective-permute-done.4), channel_id=1, replica_groups=mesh['group'=2,'plane'=16,'core'=2,'mp'=8] {'core'}, dimensions={0}, use_global_device_ids=true | all-gather | bytes 221184 | tf_op jit(solution)/shard_map/all_gather | solution.py:491
  19.7 2.3 %all-to-all-done.mod_ref.order_ref = bf16[64,3,128]{2,1,0:T(4,128)(2,1)S(1)} async-done(((bf16[64,3,128]{2,1,0:T(4,128)(2,1)}), bf16[64,3,128]{2,1,0:T(4,128)(2,1)S(1)}, u32[]{:S(2)}, u32[]{:S(2)}) %all-to-all-start) | async-done | bytes 49184 | tf_op jit(solution)/shard_map/all_to_all | solution.py:62
  22.0 1.0 shard_map.160
  23.0 0.0 copy-start.2
  23.0 0.0 copy-start.3
  23.0 0.0 copy-start.4
  23.0 21.8 %all-to-all-start.1 = ((bf16[16,24,384]{2,1,0:T(8,128)(2,1)}), bf16[16,24,384]{2,1,0:T(8,128)(2,1)S(1)}, u32[]{:S(2)}, u32[]{:S(2)}) async-start(bf16[16,24,384]{2,1,0:T(8,128)(2,1)} %shard_map.160), calls=%async_computation.1 | async-start | bytes 589824 | tf_op jit(solution)/shard_map/all_to_all | solution.py:62
  44.8 0.0 copy-done.2
  44.8 0.0 copy-done.3
  44.8 0.0 copy-done.4
  44.8 0.4 shard_map.158
  45.2 1.9 %collective-permute-start = (f32[104,128]{1,0:T(8,128)S(1)}, f32[104,128]{1,0:T(8,128)S(1)}, u32[]{:S(2)}, u32[]{:S(2)}) collective-permute-start(f32[104,128]{1,0:T(8,128)S(1)} %shard_map.158), channel_id=1, source_target_pairs={{0,1},{1,0},{2,3},{3,2},{4,5},{5,4},{6,7},{7,6},{8,9},{9,8},{10,11... | collective-permute-start | bytes 159752 | tf_op jit(solution)/shard_map/ppermute | solution.py:503
  47.2 4.1 %collective-permute-done = f32[104,128]{1,0:T(8,128)S(1)} collective-permute-done((f32[104,128]{1,0:T(8,128)S(1)}, f32[104,128]{1,0:T(8,128)S(1)}, u32[]{:S(2)}, u32[]{:S(2)}) %collective-permute-start) | collective-permute-done | bytes 53280 | tf_op jit(solution)/shard_map/ppermute | solution.py:503
  51.3 5.8 %collective-permute-start.1 = (f32[104,128]{1,0:T(8,128)S(1)}, f32[104,128]{1,0:T(8,128)S(1)}, u32[]{:S(2)}, u32[]{:S(2)}) collective-permute-start(f32[104,128]{1,0:T(8,128)S(1)} %add.21), channel_id=1, source_target_pairs={{0,2},{1,3},{2,0},{3,1},{4,6},{5,7},{6,4},{7,5},{8,10},{9,11},{10,... | collective-permute-start | bytes 159752 | tf_op jit(solution)/shard_map/ppermute | solution.py:503
  57.2 2.1 %collective-permute-done.1 = f32[104,128]{1,0:T(8,128)S(1)} collective-permute-done((f32[104,128]{1,0:T(8,128)S(1)}, f32[104,128]{1,0:T(8,128)S(1)}, u32[]{:S(2)}, u32[]{:S(2)}) %collective-permute-start.1) | collective-permute-done | bytes 53280 | tf_op jit(solution)/shard_map/ppermute | solution.py:503
  59.3 0.0 all-to-all-done.1.parts_ref
  59.3 0.8 shard_map.161
  60.0 9.6 %all-to-all-start.2 = ((bf16[16,24,384]{2,1,0:T(8,128)(2,1)}), bf16[16,24,384]{2,1,0:T(8,128)(2,1)S(1)}, u32[]{:S(2)}, u32[]{:S(2)}) async-start(bf16[16,24,384]{2,1,0:T(8,128)(2,1)} %shard_map.161), calls=%async_computation.2 | async-start | bytes 589824 | tf_op jit(solution)/shard_map/all_to_all | solution.py:62
  69.7 8.4 %collective-permute-start.2 = (f32[104,128]{1,0:T(8,128)S(1)}, f32[104,128]{1,0:T(8,128)S(1)}, u32[]{:S(2)}, u32[]{:S(2)}) collective-permute-start(f32[104,128]{1,0:T(8,128)S(1)} %add.22.order_ref), channel_id=1, source_target_pairs={{0,4},{1,5},{2,6},{3,7},{4,0},{5,1},{6,2},{7,3},{8,12},{9,13},{10,... | collective-permute-start | bytes 159752 | tf_op jit(solution)/shard_map/ppermute | solution.py:503
  78.1 2.2 %collective-permute-done.2 = f32[104,128]{1,0:T(8,128)S(1)} collective-permute-done((f32[104,128]{1,0:T(8,128)S(1)}, f32[104,128]{1,0:T(8,128)S(1)}, u32[]{:S(2)}, u32[]{:S(2)}) %collective-permute-start.2) | collective-permute-done | bytes 53280 | tf_op jit(solution)/shard_map/ppermute | solution.py:503
  80.3 0.9 shard_map.159
  81.2 1.9 %collective-permute-start.3 = (bf16[64,128]{1,0:T(8,128)(2,1)S(1)}, bf16[64,128]{1,0:T(8,128)(2,1)S(1)}, u32[]{:S(2)}, u32[]{:S(2)}) collective-permute-start(bf16[64,128]{1,0:T(8,128)(2,1)S(1)} %get-tuple-element.22.noised_ref), channel_id=1, source_target_pairs={{8,16},{16,8},{24,32},{32,24},{40,48},{48,40},{56,64},{64,56},{72,... | collective-permute-start | bytes 49160 | tf_op jit(solution)/shard_map/ppermute | solution.py:519
  83.1 5.2 %all_gather.12.pair_ref = bf16[128,128]{1,0:T(8,128)(2,1)S(1)} all-gather(bf16[64,128]{1,0:T(8,128)(2,1)S(1)} %get-tuple-element.22.noised_ref), channel_id=1, replica_groups=mesh['group'=2,'plane'=16,'core'=2,'mp'=8] {'core'}, dimensions={0}, use_global_device_ids=true | all-gather | bytes 49152 | tf_op jit(solution)/shard_map/all_gather | solution.py:520
  88.3 0.0 all-to-all-done.2
  88.3 2.2 %all_gather.15.weights_ref = bf16[768,384]{1,0:T(8,128)(2,1)S(1)} all-gather(bf16[384,384]{1,0:T(8,128)(2,1)S(1)} %bitcast.30), channel_id=1, replica_groups=mesh['group'=2,'plane'=16,'core'=2,'mp'=8] {'core'}, dimensions={0}, use_global_device_ids=true | all-gather | bytes 884736 | tf_op jit(solution)/shard_map/all_gather | solution.py:509
  90.5 0.0 collective-permute-done.3.cross_noised_ref
  90.5 1.2 shard_map.162
  91.7 19.8 %all_to_all.30.parts_ref = bf16[8,32,512]{2,1,0:T(8,128)(2,1)S(1)} all-to-all(bf16[8,32,512]{2,1,0:T(8,128)(2,1)S(1)} %get-tuple-element.25), channel_id=1, replica_groups=mesh['group'=2,'plane'=16,'core'=2,'mp'=8] {'mp'}, dimensions={0} | all-to-all | bytes 524288 | tf_op jit(solution)/shard_map/all_to_all | solution.py:62
  111.5 1.2 shard_map.163
  112.7 3.4 %all-to-all-start.4 = ((bf16[8,48,128]{2,1,0:T(8,128)(2,1)}), bf16[8,48,128]{2,1,0:T(8,128)(2,1)S(1)}, u32[]{:S(2)}, u32[]{:S(2)}) async-start(bf16[8,48,128]{2,1,0:T(8,128)(2,1)} %get-tuple-element.28), calls=%async_computation.4 | async-start | bytes 196608 | tf_op jit(solution)/shard_map/all_to_all | solution.py:62
  116.1 0.2 fusion.4.slope_ref
  116.3 8.5 %all-to-all-done.4.pay_ref = bf16[8,48,128]{2,1,0:T(8,128)(2,1)S(1)} async-done(((bf16[8,48,128]{2,1,0:T(8,128)(2,1)}), bf16[8,48,128]{2,1,0:T(8,128)(2,1)S(1)}, u32[]{:S(2)}, u32[]{:S(2)}) %all-to-all-start.4) | async-done | bytes 98336 | tf_op jit(solution)/shard_map/all_to_all | solution.py:62
  124.9 1.6 %shard_map.164 = (bf16[8,64,128]{2,1,0:T(8,128)(2,1)S(1)}, f32[4,128]{1,0:T(4,128)}) custom-call(s32[1,4]{1,0:T(1,128)} %disc_ref.3, bf16[8,48,128]{2,1,0:T(8,128)(2,1)S(1)} %all-to-all-done.4.pay_ref, bf16[768,384]{1,0:T(8,128)(2,1)S(1)} %all_gather.15.weights_ref, bf16[768,64]{1,0:T(8,128)(2,1)S(1)} %get-tuple-element.29.query_ref, ...), custom_call_target="tpu_custom_call" | custom-call | tf_op jit(solution)/shard_map/pallas_call | solution.py:79
  126.5 11.5 %all_to_all.31.parts_ref = bf16[8,64,128]{2,1,0:T(8,128)(2,1)S(1)} all-to-all(bf16[8,64,128]{2,1,0:T(8,128)(2,1)S(1)} %get-tuple-element.34), channel_id=1, replica_groups=mesh['group'=2,'plane'=16,'core'=2,'mp'=8] {'mp'}, dimensions={0} | all-to-all | bytes 262144 | tf_op jit(solution)/shard_map/all_to_all | solution.py:62
  137.9 0.6 shard_map.165
  (5 shorter events, 0.1 us)
Async XLA Ops:
  0.6 1.0 copy-start
  0.6 1.3 copy-start.1
  1.9 13.6 %copy-start.5 = (bf16[96,768]{1,0:T(8,128)(2,1)S(1)}, bf16[96,768]{1,0:T(8,128)(2,1)}, u32[]{:S(2)}) copy-start(bf16[96,768]{1,0:T(8,128)(2,1)} %param.22) | copy-start | bytes 442372
  1.9 13.6 %copy-start.6 = (bf16[768,96]{0,1:T(8,128)(2,1)S(1)}, bf16[768,96]{0,1:T(8,128)(2,1)}, u32[]{:S(2)}) copy-start(bf16[768,96]{0,1:T(8,128)(2,1)} %param.23) | copy-start | bytes 442372
  4.4 17.6 %all-to-all-start = ((bf16[64,3,128]{2,1,0:T(4,128)(2,1)}), bf16[64,3,128]{2,1,0:T(4,128)(2,1)S(1)}, u32[]{:S(2)}, u32[]{:S(2)}) async-start(bf16[64,3,128]{2,1,0:T(4,128)(2,1)} %get-tuple-element.19), calls=%async_computation | async-start | bytes 131072 | tf_op jit(solution)/shard_map/all_to_all | solution.py:62
  14.9 3.0 %collective-permute-start.4 = (bf16[96,384]{1,0:T(8,128)(2,1)S(1)}, bf16[96,384]{1,0:T(8,128)(2,1)S(1)}, u32[]{:S(2)}, u32[]{:S(2)}) collective-permute-start(bf16[96,384]{1,0:T(8,128)(2,1)S(1)} %get-tuple-element.23), channel_id=1, source_target_pairs={{0,0},{1,32},{2,64},{3,96},{4,128},{5,160},{6,192},{7,224},{8,8},{... | collective-permute-start | bytes 221192 | tf_op jit(solution)/shard_map/ppermute | solution.py:486
  23.0 21.8 %copy-start.2 = (bf16[64,384]{1,0:T(8,128)(2,1)S(1)}, bf16[64,384]{1,0:T(8,128)(2,1)}, u32[]{:S(2)}) copy-start(bf16[64,384]{1,0:T(8,128)(2,1)} %embed_ref.3) | copy-start | bytes 147460
  23.0 21.8 %copy-start.3 = (bf16[1,128,384]{2,1,0:T(8,128)(2,1)S(1)}, bf16[1,128,384]{2,1,0:T(8,128)(2,1)}, u32[]{:S(2)}) copy-start(bf16[1,128,384]{2,1,0:T(8,128)(2,1)} %param.14) | copy-start | bytes 294916
  23.0 21.8 %copy-start.4 = (bf16[384,64]{0,1:T(8,128)(2,1)S(1)}, bf16[384,64]{0,1:T(8,128)(2,1)}, u32[]{:S(2)}) copy-start(bf16[384,64]{0,1:T(8,128)(2,1)} %param.17) | copy-start | bytes 147460
  23.0 36.3 %all-to-all-start.1 = ((bf16[16,24,384]{2,1,0:T(8,128)(2,1)}), bf16[16,24,384]{2,1,0:T(8,128)(2,1)S(1)}, u32[]{:S(2)}, u32[]{:S(2)}) async-start(bf16[16,24,384]{2,1,0:T(8,128)(2,1)} %shard_map.160), calls=%async_computation.1 | async-start | bytes 589824 | tf_op jit(solution)/shard_map/all_to_all | solution.py:62
  45.2 6.0 %collective-permute-start = (f32[104,128]{1,0:T(8,128)S(1)}, f32[104,128]{1,0:T(8,128)S(1)}, u32[]{:S(2)}, u32[]{:S(2)}) collective-permute-start(f32[104,128]{1,0:T(8,128)S(1)} %shard_map.158), channel_id=1, source_target_pairs={{0,1},{1,0},{2,3},{3,2},{4,5},{5,4},{6,7},{7,6},{8,9},{9,8},{10,11... | collective-permute-start | bytes 159752 | tf_op jit(solution)/shard_map/ppermute | solution.py:503
  51.3 8.0 %collective-permute-start.1 = (f32[104,128]{1,0:T(8,128)S(1)}, f32[104,128]{1,0:T(8,128)S(1)}, u32[]{:S(2)}, u32[]{:S(2)}) collective-permute-start(f32[104,128]{1,0:T(8,128)S(1)} %add.21), channel_id=1, source_target_pairs={{0,2},{1,3},{2,0},{3,1},{4,6},{5,7},{6,4},{7,5},{8,10},{9,11},{10,... | collective-permute-start | bytes 159752 | tf_op jit(solution)/shard_map/ppermute | solution.py:503
  60.0 28.2 %all-to-all-start.2 = ((bf16[16,24,384]{2,1,0:T(8,128)(2,1)}), bf16[16,24,384]{2,1,0:T(8,128)(2,1)S(1)}, u32[]{:S(2)}, u32[]{:S(2)}) async-start(bf16[16,24,384]{2,1,0:T(8,128)(2,1)} %shard_map.161), calls=%async_computation.2 | async-start | bytes 589824 | tf_op jit(solution)/shard_map/all_to_all | solution.py:62
  69.7 10.6 %collective-permute-start.2 = (f32[104,128]{1,0:T(8,128)S(1)}, f32[104,128]{1,0:T(8,128)S(1)}, u32[]{:S(2)}, u32[]{:S(2)}) collective-permute-start(f32[104,128]{1,0:T(8,128)S(1)} %add.22.order_ref), channel_id=1, source_target_pairs={{0,4},{1,5},{2,6},{3,7},{4,0},{5,1},{6,2},{7,3},{8,12},{9,13},{10,... | collective-permute-start | bytes 159752 | tf_op jit(solution)/shard_map/ppermute | solution.py:503
  81.2 9.3 %collective-permute-start.3 = (bf16[64,128]{1,0:T(8,128)(2,1)S(1)}, bf16[64,128]{1,0:T(8,128)(2,1)S(1)}, u32[]{:S(2)}, u32[]{:S(2)}) collective-permute-start(bf16[64,128]{1,0:T(8,128)(2,1)S(1)} %get-tuple-element.22.noised_ref), channel_id=1, source_target_pairs={{8,16},{16,8},{24,32},{32,24},{40,48},{48,40},{56,64},{64,56},{72,... | collective-permute-start | bytes 49160 | tf_op jit(solution)/shard_map/ppermute | solution.py:519
  112.7 12.1 %all-to-all-start.4 = ((bf16[8,48,128]{2,1,0:T(8,128)(2,1)}), bf16[8,48,128]{2,1,0:T(8,128)(2,1)S(1)}, u32[]{:S(2)}, u32[]{:S(2)}) async-start(bf16[8,48,128]{2,1,0:T(8,128)(2,1)} %get-tuple-element.28), calls=%async_computation.4 | async-start | bytes 196608 | tf_op jit(solution)/shard_map/all_to_all | solution.py:62

commit v3 on v2

--- a/solution.py
+++ b/solution.py
@@ -62,14 +62,14 @@
     return lax.all_to_all(value, axes, 0, 0, tiled=False)
 
 
-def call(body, outs, scalars, arrays, scratch=(), loose=(), distant=(), plain=()):
+def call(body, outs, scalars, arrays, scratch=(), loose=(), distant=(), plain=(), away=()):
     smem = pl.BlockSpec(memory_space=pltpu.SMEM)
     vmem = pl.BlockSpec(memory_space=pltpu.VMEM)
     if INTERPRET:
         shapes = [jax.ShapeDtypeStruct(shape, dtype) for shape, dtype in outs]
     else:
         shapes = [
-            jax.ShapeDtypeStruct(*out) if place in loose else pltpu.VMEM(*out)
+            jax.ShapeDtypeStruct(*out) if place in loose + away else pltpu.VMEM(*out)
             for place, out in enumerate(outs)
         ]
         arrays = [
@@ -81,10 +81,12 @@
         in_specs=[smem] * len(scalars)
         + [vmem] * len(arrays)
         + [pl.BlockSpec(memory_space=pl.ANY)] * len(distant),
-        out_specs=[vmem] * len(outs),
+        out_specs=[
+            pl.BlockSpec(memory_space=pl.ANY) if place in away else vmem for place in range(len(outs))
+        ],
         out_shape=shapes,
         scratch_shapes=[pltpu.VMEM(shape, dtype) for shape, dtype in scratch]
-        + [pltpu.SemaphoreType.DMA] * len(distant),
+        + [pltpu.SemaphoreType.DMA] * (len(distant) + len(away)),
         interpret=INTERPRET,
     )(*scalars, *arrays, *distant)
 
@@ -100,7 +102,7 @@
 
 
 def level_of(time_ref):
-    return time_ref[0].astype(F32) / 1000.0
+    return time_ref[0:1] / 1000.0
 
 
 def open_body(
@@ -120,13 +122,30 @@
     noise_ref,
     queries_ref,
     turned_ref,
+    terms_ref,
     noise_sem,
+    terms_sem,
 ):
     fetch = pltpu.make_async_copy(noise_in_ref, noise_ref, noise_sem)
     fetch.start()
     block, other = pick_heads(disc_ref)
     channels = proj_ref.shape[2]
     latent, width = embed_ref.shape
+
+    groups = cond_ref.shape[0]
+    copies, pieces, lanes = mods_ref.shape
+    seqs = copies // groups
+    half = contract(cond_ref[...], mod_ref[...].astype(F32), 1, 0, HIGHEST)
+    for group in range(groups):
+        row = half[group : group + 1]
+        pieces_of = jnp.concatenate(
+            [row[:, lanes * p : lanes * (p + 1)] for p in range(pieces)], axis=0
+        )
+        terms_ref[seqs * group : seqs * (group + 1)] = jnp.broadcast_to(
+            pieces_of.astype(BF16)[None], (seqs, pieces, lanes)
+        )
+    store = pltpu.make_async_copy(terms_ref, mods_ref, terms_sem)
+    store.start()
 
     rows = sent_ref.shape[0]
     start = pl.multiple_of((seq_index() % (width // rows)) * rows, rows)
@@ -145,19 +164,6 @@
     sent_ref[:, 2 * channels :] = queries_ref[pl.ds(start, rows), :].astype(BF16)
     for place, head in enumerate(block):
         sent_ref[:, channels * place : channels * (place + 1)] = proj_ref[head, pl.ds(start, rows), :]
-
-    groups = cond_ref.shape[0]
-    copies, pieces, lanes = mods_ref.shape
-    seqs = copies // groups
-    half = contract(cond_ref[...], mod_ref[...].astype(F32), 1, 0, HIGHEST)
-    for group in range(groups):
-        row = half[group : group + 1]
-        pieces_of = jnp.concatenate(
-            [row[:, lanes * p : lanes * (p + 1)] for p in range(pieces)], axis=0
-        )
-        mods_ref[seqs * group : seqs * (group + 1)] = jnp.broadcast_to(
-            pieces_of.astype(BF16)[None], (seqs, pieces, lanes)
-        )
 
     _, share, pair_lanes = cross_ref.shape
     per_head = channels // share
@@ -180,6 +186,7 @@
         )
         turned_ref[...] = table.T
         taps_ref[share * place : share * (place + 1)] = turned_ref[pl.ds(offset, share), :]
+    store.wait()
     fetch.wait()
 
 
@@ -371,7 +378,7 @@
     pay_ref,
     weights_ref,
     query_ref,
-    slope_ref,
+    pre_ref,
     side_ref,
     noised_ref,
     back_ref,
@@ -386,7 +393,7 @@
     split = copies * share
     grads = jnp.concatenate([pay_ref[copy, :share] for copy in range(copies)], axis=0)
     hidden_grad = contract(weights_ref[:, :split], grads, 1, 0)
-    preact_grad = (hidden_grad * slope_ref[...]).astype(BF16)
+    preact_grad = (hidden_grad * gelu_slope(pre_ref[...])).astype(BF16)
     query_grad = contract(query_ref[...], preact_grad, 0, 0)
     inv_std = side_ref[latent : latent + 1]
     along = jnp.sum(noised_ref[...].astype(F32) * query_grad, axis=0, keepdims=True)
@@ -411,9 +418,11 @@
         logits_ref[k : k + 1] = value
 
 
-def final_body(time_ref, parts_ref, out_ref):
+def final_body(time_ref, parts_ref, latents_ref, logits_ref, out_ref, latents_out_ref, logits_out_ref):
     retain = 1.0 - level_of(time_ref)
     out_ref[...] = retain * jnp.sum(parts_ref[...].astype(F32), axis=0)
+    latents_out_ref[...] = latents_ref[...]
+    logits_out_ref[...] = logits_ref[...]
 
 
 def per_device(
@@ -451,6 +460,7 @@
         teacher_mod.astype(F32),
         precision=HIGHEST,
     )[0]
+    time_row = jnp.broadcast_to(timestep.astype(F32)[:, None], (8, tokens))
     ratio = seqs // mps
     rows = local_width // ratio
     pieces = local_width // 128
@@ -473,7 +483,12 @@
             jnp.transpose(head_kernel, (1, 2, 0, 3)).reshape(9, 4, channels),
             head_out,
         ],
-        [((local_width, 128), F32), ((channels, 16), F32)],
+        [
+            ((local_width, 128), F32),
+            ((channels, 16), F32),
+            ((groups * seqs, pieces, 128), BF16),
+        ],
+        away=(1,),
         distant=[noise[0].T],
         plain=(0, 1, 3, 5, 6),
     )
@@ -511,9 +526,8 @@
     latents, noised = call(
         functools.partial(noise_body, width=float(width)),
         [((latent, tokens), BF16), ((latent, tokens), BF16)],
-        [timestep],
-        [sums, noise_t],
-        loose=(0,),
+        [],
+        [time_row, sums, noise_t],
     )
     swap = [(i, i + 1 if i % 2 else i - 1) for i in range(1, seqs - 1)]
     edge = lax.ppermute(noised, SEQ, swap)
@@ -533,7 +547,6 @@
         [((units, extent), BF16)],
     )
     parts = exchange(parts, "mp")
-    slope = gelu_slope(preact)
     pay, back = call(
         functools.partial(conv_body, count=seqs),
         [((mps, share + 16, tokens), BF16), ((latent, tokens), F32)],
@@ -545,11 +558,16 @@
         functools.partial(back_body, width=float(width)),
         [((mps, latent, tokens), BF16), ((4, tokens), F32)],
         [disc_layer],
-        [pay, weights, query, slope, side, noised, back],
-        loose=(1,),
+        [pay, weights, query, preact, side, noised, back],
     )
     back = exchange(back, "mp")
-    (latent_grad,) = call(final_body, [((latent, tokens), F32)], [timestep], [back], loose=(0,))
+    latent_grad, latents, logits = call(
+        final_body,
+        [((latent, tokens), F32), ((latent, tokens), BF16), ((4, tokens), F32)],
+        [],
+        [time_row, back, latents, logits],
+        loose=(0, 1, 2),
+    )
     return (latents.T[None], logits[None], latent_grad.T[None])
 
 

time: 139 us -> 136 us (0.978)
  blocking collectives: 42.7 us -> 54 us
  waiting for transfers between devices: 19.2 us -> 10.7 us
  starting transfers between devices: 64 us -> 60.6 us
  Pallas kernels: 10.2 us -> 8.09 us
    all_to_all x2 -> x3, blocking collectives: 31.2 us -> 42.5 us  [exchange(): return lax.all_to_all(value, axes, 0, 0, tiled=False)]
    all_to_all x4 -> x3, waiting for transfers between devices: 10.8 us -> 2.27 us  [exchange(): return lax.all_to_all(value, axes, 0, 0, tiled=False)]
    all_to_all x4 -> x3, starting transfers between devices: 45.2 us -> 41.8 us  [exchange(): return lax.all_to_all(value, axes, 0, 0, tiled=False)]
    pallas_call x9, Pallas kernels: 10.2 us -> 8.09 us  [call(): pl.pallas_call(body, in_specs=[smem] * len(scalars) + [vmem] * len(arrays...]
  transfers between devices with their start and end apart: 9 -> 8, of which waited for: 5 -> 4; matrix products, arithmetic and copies ran while one was open for 0% -> 0% of each run, Pallas kernels for 1% -> 1%
where the time goes in v3:
time: 136 us
  starting transfers between devices  60.6 us (45%)
  blocking collectives  54 us (40%)
  waiting for transfers between devices  10.7 us (8%)
  Pallas kernels  8.09 us (6%)
  between operations  1.54 us (1%)
    all_to_all x3, blocking collectives, exchange(): return lax.all_to_all(value, axes, 0, 0, tiled=False)  42.5 us
    all_to_all x3, starting transfers between devices, exchange(): return lax.all_to_all(value, axes, 0, 0, tiled=False)  41.8 us
    ppermute x3, starting transfers between devices, per_device(): sums = sums + lax.ppermute(sums, 'mp', [(i, i ^ step) for i in range(mps)])  16.2 us
    ppermute x3, waiting for transfers between devices, per_device(): sums = sums + lax.ppermute(sums, 'mp', [(i, i ^ step) for i in range(mps)])  8.41 us
    pallas_call x9, Pallas kernels, call(): pl.pallas_call(body, in_specs=[smem] * len(scalars) + [vmem] * len(arrays...  8.09 us
    all_gather x1, blocking collectives, per_device(): pair = lax.all_gather(noised, 'core', axis=0, tiled=True)  5.16 us
  transfers between devices with their start and end apart: 8, of which 4 were waited for; matrix products, arithmetic and copies ran while one was open for 0% of the time, Pallas kernels for 1%

profile of v3, /device:TPU:24, one launch (start us, length us, event | category | flops | bytes accessed | tf_op | source)
XLA Modules:
  0.0 135.5 jit_solution(6491881301815770377)
XLA Ops:
  0.6 0.0 copy-start
  0.6 0.0 copy-start.1
  1.4 0.1 fusion.4
  1.4 0.2 copy-done
  1.6 0.3 fusion
  1.9 0.0 copy-done.1
  1.9 0.0 copy-start.5
  1.9 0.0 copy-start.6
  2.0 1.9 %shard_map.157 = (bf16[96,384]{1,0:T(8,128)(2,1)S(1)}, bf16[64,3,128]{2,1,0:T(4,128)(2,1)}, bf16[8,32,128]{2,1,0:T(8,128)(2,1)S(1)}, f32[64,16]{1,0:T(8,128)S(1)}, bf16[64,128]{1,0:T(8,128)(2,1)S(1)}) custom-call(s32[1,4]{1,0:T(1,128)} %disc_ref.3, f32[2,96]{1,0:T(2,128)} %cond_ref.1, bf16[96,384]{1,0:T(8,128)(2,1)} %bitcast.32, f32[2,384]{1,0:T(2,128)S(1)} %bitcast.29, ...), custom_call_target="tpu_custom_call" | custom-call | tf_op jit(solution)/shard_map/pallas_call | solution.py:79
  3.8 10.5 %all-to-all-start = ((bf16[64,3,128]{2,1,0:T(4,128)(2,1)}), bf16[64,3,128]{2,1,0:T(4,128)(2,1)S(1)}, u32[]{:S(2)}, u32[]{:S(2)}) async-start(bf16[64,3,128]{2,1,0:T(4,128)(2,1)} %get-tuple-element.22), calls=%async_computation | async-start | bytes 131072 | tf_op jit(solution)/shard_map/all_to_all | solution.py:62
  14.3 0.7 collective-permute-start.4
  15.0 0.0 copy-done.5
  15.0 0.0 copy-done.6
  15.0 2.2 %all_gather.14.pair_ref = bf16[384,768]{1,0:T(8,128)(2,1)S(1)} all-gather(bf16[192,768]{1,0:T(8,128)(2,1)S(1)} %pad_maximum_fusion), channel_id=1, replica_groups=mesh['group'=2,'plane'=16,'core'=2,'mp'=8] {'core'}, dimensions={0}, use_global_device_ids=true | all-gather | bytes 884736 | tf_op jit(solution)/shard_map/all_gather | solution.py:505
  17.2 0.0 collective-permute-done.4
  17.2 1.9 %all_gather.13.got_ref = bf16[192,384]{1,0:T(8,128)(2,1)S(1)} all-gather(bf16[96,384]{1,0:T(8,128)(2,1)S(1)} %collective-permute-done.4), channel_id=1, replica_groups=mesh['group'=2,'plane'=16,'core'=2,'mp'=8] {'core'}, dimensions={0}, use_global_device_ids=true | all-gather | bytes 221184 | tf_op jit(solution)/shard_map/all_gather | solution.py:506
  19.1 2.3 %all-to-all-done.mod_ref.order_ref = bf16[64,3,128]{2,1,0:T(4,128)(2,1)S(1)} async-done(((bf16[64,3,128]{2,1,0:T(4,128)(2,1)}), bf16[64,3,128]{2,1,0:T(4,128)(2,1)S(1)}, u32[]{:S(2)}, u32[]{:S(2)}) %all-to-all-start) | async-done | bytes 49184 | tf_op jit(solution)/shard_map/all_to_all | solution.py:62
  21.4 1.0 shard_map.160
  22.4 0.0 copy-start.2
  22.4 0.0 copy-start.3
  22.4 0.0 copy-start.4
  22.4 21.8 %all-to-all-start.1 = ((bf16[16,24,384]{2,1,0:T(8,128)(2,1)}), bf16[16,24,384]{2,1,0:T(8,128)(2,1)S(1)}, u32[]{:S(2)}, u32[]{:S(2)}) async-start(bf16[16,24,384]{2,1,0:T(8,128)(2,1)} %shard_map.160), calls=%async_computation.1 | async-start | bytes 589824 | tf_op jit(solution)/shard_map/all_to_all | solution.py:62
  44.2 0.0 copy-done.2
  44.2 0.0 copy-done.3
  44.2 0.0 copy-done.4
  44.2 0.4 shard_map.158
  44.7 1.9 %collective-permute-start = (f32[104,128]{1,0:T(8,128)S(1)}, f32[104,128]{1,0:T(8,128)S(1)}, u32[]{:S(2)}, u32[]{:S(2)}) collective-permute-start(f32[104,128]{1,0:T(8,128)S(1)} %shard_map.158), channel_id=1, source_target_pairs={{0,1},{1,0},{2,3},{3,2},{4,5},{5,4},{6,7},{7,6},{8,9},{9,8},{10,11... | collective-permute-start | bytes 159752 | tf_op jit(solution)/shard_map/ppermute | solution.py:518
  46.6 4.1 %collective-permute-done = f32[104,128]{1,0:T(8,128)S(1)} collective-permute-done((f32[104,128]{1,0:T(8,128)S(1)}, f32[104,128]{1,0:T(8,128)S(1)}, u32[]{:S(2)}, u32[]{:S(2)}) %collective-permute-start) | collective-permute-done | bytes 53280 | tf_op jit(solution)/shard_map/ppermute | solution.py:518
  50.7 5.9 %collective-permute-start.1 = (f32[104,128]{1,0:T(8,128)S(1)}, f32[104,128]{1,0:T(8,128)S(1)}, u32[]{:S(2)}, u32[]{:S(2)}) collective-permute-start(f32[104,128]{1,0:T(8,128)S(1)} %add.9), channel_id=1, source_target_pairs={{0,2},{1,3},{2,0},{3,1},{4,6},{5,7},{6,4},{7,5},{8,10},{9,11},{10,... | collective-permute-start | bytes 159752 | tf_op jit(solution)/shard_map/ppermute | solution.py:518
  56.6 2.1 %collective-permute-done.1 = f32[104,128]{1,0:T(8,128)S(1)} collective-permute-done((f32[104,128]{1,0:T(8,128)S(1)}, f32[104,128]{1,0:T(8,128)S(1)}, u32[]{:S(2)}, u32[]{:S(2)}) %collective-permute-start.1) | collective-permute-done | bytes 53280 | tf_op jit(solution)/shard_map/ppermute | solution.py:518
  58.7 0.0 all-to-all-done.1.parts_ref
  58.7 0.8 shard_map.161
  59.5 9.6 %all-to-all-start.2 = ((bf16[16,24,384]{2,1,0:T(8,128)(2,1)}), bf16[16,24,384]{2,1,0:T(8,128)(2,1)S(1)}, u32[]{:S(2)}, u32[]{:S(2)}) async-start(bf16[16,24,384]{2,1,0:T(8,128)(2,1)} %shard_map.161), calls=%async_computation.2 | async-start | bytes 589824 | tf_op jit(solution)/shard_map/all_to_all | solution.py:62
  69.1 8.4 %collective-permute-start.2 = (f32[104,128]{1,0:T(8,128)S(1)}, f32[104,128]{1,0:T(8,128)S(1)}, u32[]{:S(2)}, u32[]{:S(2)}) collective-permute-start(f32[104,128]{1,0:T(8,128)S(1)} %add.10.order_ref), channel_id=1, source_target_pairs={{0,4},{1,5},{2,6},{3,7},{4,0},{5,1},{6,2},{7,3},{8,12},{9,13},{10,... | collective-permute-start | bytes 159752 | tf_op jit(solution)/shard_map/ppermute | solution.py:518
  77.5 2.2 %collective-permute-done.2 = f32[104,128]{1,0:T(8,128)S(1)} collective-permute-done((f32[104,128]{1,0:T(8,128)S(1)}, f32[104,128]{1,0:T(8,128)S(1)}, u32[]{:S(2)}, u32[]{:S(2)}) %collective-permute-start.2) | collective-permute-done | bytes 53280 | tf_op jit(solution)/shard_map/ppermute | solution.py:518
  79.7 0.3 shard_map.159
  80.1 1.9 %collective-permute-start.3 = (bf16[64,128]{1,0:T(8,128)(2,1)S(1)}, bf16[64,128]{1,0:T(8,128)(2,1)S(1)}, u32[]{:S(2)}, u32[]{:S(2)}) collective-permute-start(bf16[64,128]{1,0:T(8,128)(2,1)S(1)} %get-tuple-element.24.noised_ref), channel_id=1, source_target_pairs={{8,16},{16,8},{24,32},{32,24},{40,48},{48,40},{56,64},{64,56},{72,... | collective-permute-start | bytes 49160 | tf_op jit(solution)/shard_map/ppermute | solution.py:533
  82.0 5.2 %all_gather.12.pair_ref = bf16[128,128]{1,0:T(8,128)(2,1)S(1)} all-gather(bf16[64,128]{1,0:T(8,128)(2,1)S(1)} %get-tuple-element.24.noised_ref), channel_id=1, replica_groups=mesh['group'=2,'plane'=16,'core'=2,'mp'=8] {'core'}, dimensions={0}, use_global_device_ids=true | all-gather | bytes 49152 | tf_op jit(solution)/shard_map/all_gather | solution.py:534
  87.1 0.0 all-to-all-done.2
  87.1 2.2 %all_gather.15.weights_ref = bf16[768,384]{1,0:T(8,128)(2,1)S(1)} all-gather(bf16[384,384]{1,0:T(8,128)(2,1)S(1)} %bitcast.30), channel_id=1, replica_groups=mesh['group'=2,'plane'=16,'core'=2,'mp'=8] {'core'}, dimensions={0}, use_global_device_ids=true | all-gather | bytes 884736 | tf_op jit(solution)/shard_map/all_gather | solution.py:524
  89.4 0.0 collective-permute-done.3.cross_noised_ref
  89.4 1.2 shard_map.162
  90.6 19.8 %all_to_all.30.parts_ref = bf16[8,32,512]{2,1,0:T(8,128)(2,1)S(1)} all-to-all(bf16[8,32,512]{2,1,0:T(8,128)(2,1)S(1)} %get-tuple-element.27), channel_id=1, replica_groups=mesh['group'=2,'plane'=16,'core'=2,'mp'=8] {'mp'}, dimensions={0} | all-to-all | bytes 524288 | tf_op jit(solution)/shard_map/all_to_all | solution.py:62
  110.4 0.7 shard_map.163
  111.0 11.2 %all_to_all.31.pay_ref = bf16[8,48,128]{2,1,0:T(8,128)(2,1)S(1)} all-to-all(bf16[8,48,128]{2,1,0:T(8,128)(2,1)S(1)} %get-tuple-element.30), channel_id=1, replica_groups=mesh['group'=2,'plane'=16,'core'=2,'mp'=8] {'mp'}, dimensions={0} | all-to-all | bytes 196608 | tf_op jit(solution)/shard_map/all_to_all | solution.py:62
  122.3 1.2 shard_map.164
  123.4 11.5 %all_to_all.32.parts_ref = bf16[8,64,128]{2,1,0:T(8,128)(2,1)S(1)} all-to-all(bf16[8,64,128]{2,1,0:T(8,128)(2,1)S(1)} %get-tuple-element.35), channel_id=1, replica_groups=mesh['group'=2,'plane'=16,'core'=2,'mp'=8] {'mp'}, dimensions={0} | all-to-all | bytes 262144 | tf_op jit(solution)/shard_map/all_to_all | solution.py:62
  134.9 0.6 shard_map.165
  (6 shorter events, 0.1 us)
Async XLA Ops:
  0.6 1.0 copy-start
  0.6 1.3 copy-start.1
  1.9 13.0 %copy-start.5 = (bf16[96,768]{1,0:T(8,128)(2,1)S(1)}, bf16[96,768]{1,0:T(8,128)(2,1)}, u32[]{:S(2)}) copy-start(bf16[96,768]{1,0:T(8,128)(2,1)} %param.22) | copy-start | bytes 442372
  1.9 13.0 %copy-start.6 = (bf16[768,96]{0,1:T(8,128)(2,1)S(1)}, bf16[768,96]{0,1:T(8,128)(2,1)}, u32[]{:S(2)}) copy-start(bf16[768,96]{0,1:T(8,128)(2,1)} %param.23) | copy-start | bytes 442372
  3.8 17.6 %all-to-all-start = ((bf16[64,3,128]{2,1,0:T(4,128)(2,1)}), bf16[64,3,128]{2,1,0:T(4,128)(2,1)S(1)}, u32[]{:S(2)}, u32[]{:S(2)}) async-start(bf16[64,3,128]{2,1,0:T(4,128)(2,1)} %get-tuple-element.22), calls=%async_computation | async-start | bytes 131072 | tf_op jit(solution)/shard_map/all_to_all | solution.py:62
  14.3 3.0 %collective-permute-start.4 = (bf16[96,384]{1,0:T(8,128)(2,1)S(1)}, bf16[96,384]{1,0:T(8,128)(2,1)S(1)}, u32[]{:S(2)}, u32[]{:S(2)}) collective-permute-start(bf16[96,384]{1,0:T(8,128)(2,1)S(1)} %get-tuple-element.25), channel_id=1, source_target_pairs={{0,0},{1,32},{2,64},{3,96},{4,128},{5,160},{6,192},{7,224},{8,8},{... | collective-permute-start | bytes 221192 | tf_op jit(solution)/shard_map/ppermute | solution.py:501
  22.4 21.8 %copy-start.2 = (bf16[64,384]{1,0:T(8,128)(2,1)S(1)}, bf16[64,384]{1,0:T(8,128)(2,1)}, u32[]{:S(2)}) copy-start(bf16[64,384]{1,0:T(8,128)(2,1)} %embed_ref.3) | copy-start | bytes 147460
  22.4 21.8 %copy-start.3 = (bf16[1,128,384]{2,1,0:T(8,128)(2,1)S(1)}, bf16[1,128,384]{2,1,0:T(8,128)(2,1)}, u32[]{:S(2)}) copy-start(bf16[1,128,384]{2,1,0:T(8,128)(2,1)} %param.14) | copy-start | bytes 294916
  22.4 21.8 %copy-start.4 = (bf16[384,64]{0,1:T(8,128)(2,1)S(1)}, bf16[384,64]{0,1:T(8,128)(2,1)}, u32[]{:S(2)}) copy-start(bf16[384,64]{0,1:T(8,128)(2,1)} %param.17) | copy-start | bytes 147460
  22.4 36.3 %all-to-all-start.1 = ((bf16[16,24,384]{2,1,0:T(8,128)(2,1)}), bf16[16,24,384]{2,1,0:T(8,128)(2,1)S(1)}, u32[]{:S(2)}, u32[]{:S(2)}) async-start(bf16[16,24,384]{2,1,0:T(8,128)(2,1)} %shard_map.160), calls=%async_computation.1 | async-start | bytes 589824 | tf_op jit(solution)/shard_map/all_to_all | solution.py:62
  44.7 6.0 %collective-permute-start = (f32[104,128]{1,0:T(8,128)S(1)}, f32[104,128]{1,0:T(8,128)S(1)}, u32[]{:S(2)}, u32[]{:S(2)}) collective-permute-start(f32[104,128]{1,0:T(8,128)S(1)} %shard_map.158), channel_id=1, source_target_pairs={{0,1},{1,0},{2,3},{3,2},{4,5},{5,4},{6,7},{7,6},{8,9},{9,8},{10,11... | collective-permute-start | bytes 159752 | tf_op jit(solution)/shard_map/ppermute | solution.py:518
  50.7 8.0 %collective-permute-start.1 = (f32[104,128]{1,0:T(8,128)S(1)}, f32[104,128]{1,0:T(8,128)S(1)}, u32[]{:S(2)}, u32[]{:S(2)}) collective-permute-start(f32[104,128]{1,0:T(8,128)S(1)} %add.9), channel_id=1, source_target_pairs={{0,2},{1,3},{2,0},{3,1},{4,6},{5,7},{6,4},{7,5},{8,10},{9,11},{10,... | collective-permute-start | bytes 159752 | tf_op jit(solution)/shard_map/ppermute | solution.py:518
  59.5 27.7 %all-to-all-start.2 = ((bf16[16,24,384]{2,1,0:T(8,128)(2,1)}), bf16[16,24,384]{2,1,0:T(8,128)(2,1)S(1)}, u32[]{:S(2)}, u32[]{:S(2)}) async-start(bf16[16,24,384]{2,1,0:T(8,128)(2,1)} %shard_map.161), calls=%async_computation.2 | async-start | bytes 589824 | tf_op jit(solution)/shard_map/all_to_all | solution.py:62
  69.1 10.6 %collective-permute-start.2 = (f32[104,128]{1,0:T(8,128)S(1)}, f32[104,128]{1,0:T(8,128)S(1)}, u32[]{:S(2)}, u32[]{:S(2)}) collective-permute-start(f32[104,128]{1,0:T(8,128)S(1)} %add.10.order_ref), channel_id=1, source_target_pairs={{0,4},{1,5},{2,6},{3,7},{4,0},{5,1},{6,2},{7,3},{8,12},{9,13},{10,... | collective-permute-start | bytes 159752 | tf_op jit(solution)/shard_map/ppermute | solution.py:518
  80.1 9.3 %collective-permute-start.3 = (bf16[64,128]{1,0:T(8,128)(2,1)S(1)}, bf16[64,128]{1,0:T(8,128)(2,1)S(1)}, u32[]{:S(2)}, u32[]{:S(2)}) collective-permute-start(bf16[64,128]{1,0:T(8,128)(2,1)S(1)} %get-tuple-element.24.noised_ref), channel_id=1, source_target_pairs={{8,16},{16,8},{24,32},{32,24},{40,48},{48,40},{56,64},{64,56},{72,... | collective-permute-start | bytes 49160 | tf_op jit(solution)/shard_map/ppermute | solution.py:533

commit v4 on v3

--- a/solution.py
+++ b/solution.py
@@ -190,18 +190,25 @@
     fetch.wait()
 
 
-def weight_body(got_ref, pair_ref, order_ref, out_ref):
+def weight_body(got_ref, pair_ref, order_ref, out_ref, *, latent):
     del order_ref
-    copies, rows, lanes = out_ref.shape
-    split = lanes - 128
+    copies, all_rows, lanes = out_ref.shape
+    rows = all_rows - 8
     depth = got_ref.shape[0] // 2
     half = pl.ds(pl.multiple_of(lax.axis_index("core") * (copies * rows), 128), copies * rows)
     down = jnp.concatenate([pair_ref[0:depth, half], pair_ref[2 * depth : 3 * depth, half]], axis=0)
     up = jnp.concatenate([pair_ref[depth : 2 * depth, half], pair_ref[3 * depth :, half]], axis=0)
-    terms = jnp.concatenate(
-        [contract(down, got_ref[:, :split], 0, 0), contract(up, got_ref[:, split:], 0, 0)], axis=1
-    )
-    out_ref[...] = terms.astype(BF16).reshape(copies, rows, lanes)
+    value = contract(down, got_ref[:, :lanes], 0, 0)
+    query = contract(up, got_ref[:, lanes:], 0, 0).reshape(copies, rows, 128)
+    pieces = [query[:, 8 * fold : 8 * (fold + 1)] for fold in range(rows // 8)]
+    tail = jnp.concatenate(
+        [piece[:, :, :latent] for piece in pieces]
+        + [piece[:, :, latent : latent + 2] for piece in pieces]
+        + [jnp.zeros((copies, 8, lanes - len(pieces) * (latent + 2)), F32)],
+        axis=2,
+    )
+    out_ref[:, :rows] = value.astype(BF16).reshape(copies, rows, lanes)
+    out_ref[:, rows:] = tail.astype(BF16)
 
 
 def gather_body(parts_ref, order_ref, out_ref):
@@ -247,7 +254,7 @@
     base = latent + latent // 2
     mean = sums_ref[base : base + 1] / width
     var = sums_ref[base + 1 : base + 2] / width - mean * mean
-    inv_std = lax.rsqrt(var + EPSILON)
+    inv_std = lax.rsqrt(jnp.maximum(var, 0.0) + EPSILON)
     scaled_sum = sums_ref[base + 2 : base + 3, latent:]
     shifted_sum = sums_ref[base + 3 : base + 4, :latent]
     ones = jnp.ones((1, tokens), F32)
@@ -272,15 +279,16 @@
     query_ref,
     side_ref,
     wide_ref,
+    values_ref,
     act_ref,
     *,
     width,
 ):
     latent, extent = wide_ref.shape
     tokens = extent // 3
-    units = weights_ref.shape[0]
+    chunks, all_rows, split = weights_ref.shape
+    unit_rows = all_rows - 8
     copies, share, _ = out_ref.shape
-    split = weights_ref.shape[1] - 128
     edge = cross_noised_ref[...]
     first = pair_ref[0:latent]
     second = pair_ref[latent:]
@@ -297,21 +305,29 @@
     gram = gram - width * contract(center_row, center_row, 0, 0, HIGHEST)
     gram_noised = contract(gram, noised_f, 1, 0, HIGHEST)
     var = jnp.sum(noised_f * gram_noised, axis=0, keepdims=True) / width
-    inv_std = lax.rsqrt(var + EPSILON)
+    inv_std = lax.rsqrt(jnp.maximum(var, 0.0) + EPSILON)
     side_ref[0:latent] = gram_noised[:, tokens : 2 * tokens]
     side_ref[latent:] = jnp.broadcast_to(inv_std[:, tokens : 2 * tokens], (8, tokens))
-    step = 128
-    for begin in range(0, units, step):
-        rows = slice(begin, begin + step)
-        raw = weights_ref[rows, split : split + latent].astype(F32)
-        gain = weights_ref[rows, split + latent : split + latent + 1].astype(F32)
-        shift = weights_ref[rows, split + latent + 1 : split + latent + 2].astype(F32)
-        query = (raw - gain * center_row).astype(BF16)
+    folds = unit_rows // 8
+    base = folds * latent
+    step = 4
+    for begin in range(0, chunks, step):
+        rows = slice(begin * unit_rows, (begin + step) * unit_rows)
+        tail = weights_ref[begin : begin + step, unit_rows:].astype(F32)
+
+        def unfold(start, stride, size):
+            parts = [tail[:, :, start + stride * f : start + stride * f + size] for f in range(folds)]
+            return jnp.concatenate(parts, axis=1).reshape(step * unit_rows, size)
+
+        query = (unfold(0, latent, latent) - unfold(base, 2, 1) * center_row).astype(BF16)
         query_ref[rows] = query
-        pre = contract(query, noised, 1, 0) * inv_std + shift
+        pre = contract(query, noised, 1, 0) * inv_std + unfold(base + 1, 2, 1)
         pre_ref[rows] = pre[:, tokens : 2 * tokens]
         act_ref[rows] = gelu_tanh(pre).astype(BF16)
-    part = contract(weights_ref[:, :split], act_ref[...], 0, 0).astype(BF16)
+        values_ref[rows] = weights_ref[begin : begin + step, :unit_rows].reshape(
+            step * unit_rows, split
+        )
+    part = contract(values_ref[...], act_ref[...], 0, 0).astype(BF16)
     out_ref[:, :, :extent] = part.reshape(copies, share, extent)
     out_ref[:, :, extent:] = cross_ref[...]
 
@@ -376,7 +392,7 @@
 def back_body(
     disc_ref,
     pay_ref,
-    weights_ref,
+    values_ref,
     query_ref,
     pre_ref,
     side_ref,
@@ -390,9 +406,8 @@
     copies, rows, tokens = pay_ref.shape
     share = rows - 16
     latent = noised_ref.shape[0]
-    split = copies * share
     grads = jnp.concatenate([pay_ref[copy, :share] for copy in range(copies)], axis=0)
-    hidden_grad = contract(weights_ref[:, :split], grads, 1, 0)
+    hidden_grad = contract(values_ref[...], grads, 1, 0)
     preact_grad = (hidden_grad * gelu_slope(pre_ref[...])).astype(BF16)
     query_grad = contract(query_ref[...], preact_grad, 0, 0)
     inv_std = side_ref[latent : latent + 1]
@@ -504,7 +519,12 @@
     slices = jnp.concatenate([down_weight.T, up_weight], axis=0)
     slices = lax.all_gather(slices, "core", axis=0, tiled=True)
     got = lax.all_gather(got, "core", axis=0, tiled=True)
-    (terms,) = call(weight_body, [((planes, units // seqs, lanes), BF16)], [], [got, slices, mods])
+    (terms,) = call(
+        functools.partial(weight_body, latent=latent),
+        [((planes, units // seqs + 8, 2 * channels), BF16)],
+        [],
+        [got, slices, mods],
+    )
     terms = exchange(terms, "plane")
     (sums,) = call(
         sums_body,
@@ -519,8 +539,8 @@
         step *= 2
         stages.append(sums)
     halfway = stages[-2]
-    (terms,) = call(gather_body, [((planes, units // seqs, lanes), BF16)], [], [terms, halfway])
-    weights = exchange(terms, "plane").reshape(units // 2, lanes)
+    (terms,) = call(gather_body, [((planes, units // seqs + 8, 2 * channels), BF16)], [], [terms, halfway])
+    weights = exchange(terms, "plane")
     weights = lax.all_gather(weights, "core", axis=0, tiled=True)
 
     latents, noised = call(
@@ -533,7 +553,7 @@
     edge = lax.ppermute(noised, SEQ, swap)
     pair = lax.all_gather(noised, "core", axis=0, tiled=True)
 
-    parts, preact, query, side, wide = call(
+    parts, preact, query, side, wide, values = call(
         functools.partial(act_body, width=float(width)),
         [
             ((mps, share, extent + 2 * latent), BF16),
@@ -541,6 +561,7 @@
             ((units, latent), BF16),
             ((latent + 8, tokens), F32),
             ((latent, extent), BF16),
+            ((units, 2 * channels), BF16),
         ],
         [],
         [sums, edge, pair, weights, cross],
@@ -558,7 +579,7 @@
         functools.partial(back_body, width=float(width)),
         [((mps, latent, tokens), BF16), ((4, tokens), F32)],
         [disc_layer],
-        [pay, weights, query, preact, side, noised, back],
+        [pay, values, query, preact, side, noised, back],
     )
     back = exchange(back, "mp")
     latent_grad, latents, logits = call(

time: 136 us -> 136 us (level)
  no operation moved by 1% of the time
where the time goes in v4:
time: 136 us
  starting transfers between devices  60.6 us (45%)
  blocking collectives  53.9 us (40%)
  waiting for transfers between devices  10.7 us (8%)
  Pallas kernels  8.27 us (6%)
  between operations  1.54 us (1%)
    all_to_all x3, blocking collectives, exchange(): return lax.all_to_all(value, axes, 0, 0, tiled=False)  42.5 us
    all_to_all x3, starting transfers between devices, exchange(): return lax.all_to_all(value, axes, 0, 0, tiled=False)  41.8 us
    ppermute x3, starting transfers between devices, per_device(): sums = sums + lax.ppermute(sums, 'mp', [(i, i ^ step) for i in range(mps)])  16.2 us
    ppermute x3, waiting for transfers between devices, per_device(): sums = sums + lax.ppermute(sums, 'mp', [(i, i ^ step) for i in range(mps)])  8.41 us
    pallas_call x9, Pallas kernels, call(): pl.pallas_call(body, in_specs=[smem] * len(scalars) + [vmem] * len(arrays...  8.27 us
    all_gather x1, blocking collectives, per_device(): pair = lax.all_gather(noised, 'core', axis=0, tiled=True)  5.16 us
  transfers between devices with their start and end apart: 8, of which 4 were waited for; matrix products, arithmetic and copies ran while one was open for 0% of the time, Pallas kernels for 1%

profile of v4, /device:TPU:24, one launch (start us, length us, event | category | flops | bytes accessed | tf_op | source)
XLA Modules:
  0.0 135.7 jit_solution(4794300846491653661)
XLA Ops:
  0.6 0.0 copy-start
  0.6 0.0 copy-start.1
  1.4 0.1 fusion.4
  1.4 0.2 copy-done
  1.6 0.3 fusion
  1.9 0.0 copy-done.1
  1.9 0.0 copy-start.5
  1.9 0.0 copy-start.6
  2.0 1.9 %shard_map.157 = (bf16[96,384]{1,0:T(8,128)(2,1)S(1)}, bf16[64,3,128]{2,1,0:T(4,128)(2,1)}, bf16[8,32,128]{2,1,0:T(8,128)(2,1)S(1)}, f32[64,16]{1,0:T(8,128)S(1)}, bf16[64,128]{1,0:T(8,128)(2,1)S(1)}) custom-call(s32[1,4]{1,0:T(1,128)} %disc_ref.3, f32[2,96]{1,0:T(2,128)} %cond_ref.1, bf16[96,384]{1,0:T(8,128)(2,1)} %bitcast.30, f32[2,384]{1,0:T(2,128)S(1)} %bitcast.28, ...), custom_call_target="tpu_custom_call" | custom-call | tf_op jit(solution)/shard_map/pallas_call | solution.py:79
  3.8 10.5 %all-to-all-start = ((bf16[64,3,128]{2,1,0:T(4,128)(2,1)}), bf16[64,3,128]{2,1,0:T(4,128)(2,1)S(1)}, u32[]{:S(2)}, u32[]{:S(2)}) async-start(bf16[64,3,128]{2,1,0:T(4,128)(2,1)} %get-tuple-element.23), calls=%async_computation | async-start | bytes 131072 | tf_op jit(solution)/shard_map/all_to_all | solution.py:62
  14.3 0.7 collective-permute-start.4
  15.0 0.0 copy-done.5
  15.0 0.0 copy-done.6
  15.0 2.2 %all_gather.14.pair_ref = bf16[384,768]{1,0:T(8,128)(2,1)S(1)} all-gather(bf16[192,768]{1,0:T(8,128)(2,1)S(1)} %pad_maximum_fusion), channel_id=1, replica_groups=mesh['group'=2,'plane'=16,'core'=2,'mp'=8] {'core'}, dimensions={0}, use_global_device_ids=true | all-gather | bytes 884736 | tf_op jit(solution)/shard_map/all_gather | solution.py:520
  17.2 0.0 collective-permute-done.4
  17.2 1.9 %all_gather.13.got_ref = bf16[192,384]{1,0:T(8,128)(2,1)S(1)} all-gather(bf16[96,384]{1,0:T(8,128)(2,1)S(1)} %collective-permute-done.4), channel_id=1, replica_groups=mesh['group'=2,'plane'=16,'core'=2,'mp'=8] {'core'}, dimensions={0}, use_global_device_ids=true | all-gather | bytes 221184 | tf_op jit(solution)/shard_map/all_gather | solution.py:521
  19.1 2.3 %all-to-all-done.mod_ref.order_ref = bf16[64,3,128]{2,1,0:T(4,128)(2,1)S(1)} async-done(((bf16[64,3,128]{2,1,0:T(4,128)(2,1)}), bf16[64,3,128]{2,1,0:T(4,128)(2,1)S(1)}, u32[]{:S(2)}, u32[]{:S(2)}) %all-to-all-start) | async-done | bytes 49184 | tf_op jit(solution)/shard_map/all_to_all | solution.py:62
  21.4 1.1 shard_map.160
  22.5 0.0 copy-start.2
  22.5 0.0 copy-start.3
  22.5 0.0 copy-start.4
  22.5 21.8 %all-to-all-start.1 = ((bf16[16,32,256]{2,1,0:T(8,128)(2,1)}), bf16[16,32,256]{2,1,0:T(8,128)(2,1)S(1)}, u32[]{:S(2)}, u32[]{:S(2)}) async-start(bf16[16,32,256]{2,1,0:T(8,128)(2,1)} %shard_map.160), calls=%async_computation.1 | async-start | bytes 524288 | tf_op jit(solution)/shard_map/all_to_all | solution.py:62
  44.2 0.0 copy-done.2
  44.3 0.0 copy-done.3
  44.3 0.0 copy-done.4
  44.3 0.4 shard_map.158
  44.7 1.9 %collective-permute-start = (f32[104,128]{1,0:T(8,128)S(1)}, f32[104,128]{1,0:T(8,128)S(1)}, u32[]{:S(2)}, u32[]{:S(2)}) collective-permute-start(f32[104,128]{1,0:T(8,128)S(1)} %shard_map.158), channel_id=1, source_target_pairs={{0,1},{1,0},{2,3},{3,2},{4,5},{5,4},{6,7},{7,6},{8,9},{9,8},{10,11... | collective-permute-start | bytes 159752 | tf_op jit(solution)/shard_map/ppermute | solution.py:538
  46.7 4.1 %collective-permute-done = f32[104,128]{1,0:T(8,128)S(1)} collective-permute-done((f32[104,128]{1,0:T(8,128)S(1)}, f32[104,128]{1,0:T(8,128)S(1)}, u32[]{:S(2)}, u32[]{:S(2)}) %collective-permute-start) | collective-permute-done | bytes 53280 | tf_op jit(solution)/shard_map/ppermute | solution.py:538
  50.8 5.9 %collective-permute-start.1 = (f32[104,128]{1,0:T(8,128)S(1)}, f32[104,128]{1,0:T(8,128)S(1)}, u32[]{:S(2)}, u32[]{:S(2)}) collective-permute-start(f32[104,128]{1,0:T(8,128)S(1)} %add.9), channel_id=1, source_target_pairs={{0,2},{1,3},{2,0},{3,1},{4,6},{5,7},{6,4},{7,5},{8,10},{9,11},{10,... | collective-permute-start | bytes 159752 | tf_op jit(solution)/shard_map/ppermute | solution.py:538
  56.6 2.1 %collective-permute-done.1 = f32[104,128]{1,0:T(8,128)S(1)} collective-permute-done((f32[104,128]{1,0:T(8,128)S(1)}, f32[104,128]{1,0:T(8,128)S(1)}, u32[]{:S(2)}, u32[]{:S(2)}) %collective-permute-start.1) | collective-permute-done | bytes 53280 | tf_op jit(solution)/shard_map/ppermute | solution.py:538
  58.8 0.0 all-to-all-done.1.parts_ref
  58.8 0.8 shard_map.161
  59.5 9.6 %all-to-all-start.2 = ((bf16[16,32,256]{2,1,0:T(8,128)(2,1)}), bf16[16,32,256]{2,1,0:T(8,128)(2,1)S(1)}, u32[]{:S(2)}, u32[]{:S(2)}) async-start(bf16[16,32,256]{2,1,0:T(8,128)(2,1)} %shard_map.161), calls=%async_computation.2 | async-start | bytes 524288 | tf_op jit(solution)/shard_map/all_to_all | solution.py:62
  69.2 8.4 %collective-permute-start.2 = (f32[104,128]{1,0:T(8,128)S(1)}, f32[104,128]{1,0:T(8,128)S(1)}, u32[]{:S(2)}, u32[]{:S(2)}) collective-permute-start(f32[104,128]{1,0:T(8,128)S(1)} %add.10.order_ref), channel_id=1, source_target_pairs={{0,4},{1,5},{2,6},{3,7},{4,0},{5,1},{6,2},{7,3},{8,12},{9,13},{10,... | collective-permute-start | bytes 159752 | tf_op jit(solution)/shard_map/ppermute | solution.py:538
  77.6 2.2 %collective-permute-done.2 = f32[104,128]{1,0:T(8,128)S(1)} collective-permute-done((f32[104,128]{1,0:T(8,128)S(1)}, f32[104,128]{1,0:T(8,128)S(1)}, u32[]{:S(2)}, u32[]{:S(2)}) %collective-permute-start.2) | collective-permute-done | bytes 53280 | tf_op jit(solution)/shard_map/ppermute | solution.py:538
  79.8 0.3 shard_map.159
  80.1 1.9 %collective-permute-start.3 = (bf16[64,128]{1,0:T(8,128)(2,1)S(1)}, bf16[64,128]{1,0:T(8,128)(2,1)S(1)}, u32[]{:S(2)}, u32[]{:S(2)}) collective-permute-start(bf16[64,128]{1,0:T(8,128)(2,1)S(1)} %get-tuple-element.25.noised_ref), channel_id=1, source_target_pairs={{8,16},{16,8},{24,32},{32,24},{40,48},{48,40},{56,64},{64,56},{72,... | collective-permute-start | bytes 49160 | tf_op jit(solution)/shard_map/ppermute | solution.py:553
  82.0 5.2 %all_gather.12.pair_ref = bf16[128,128]{1,0:T(8,128)(2,1)S(1)} all-gather(bf16[64,128]{1,0:T(8,128)(2,1)S(1)} %get-tuple-element.25.noised_ref), channel_id=1, replica_groups=mesh['group'=2,'plane'=16,'core'=2,'mp'=8] {'core'}, dimensions={0}, use_global_device_ids=true | all-gather | bytes 49152 | tf_op jit(solution)/shard_map/all_gather | solution.py:554
  87.2 0.0 all-to-all-done.2
  87.2 2.2 %all_gather.15.weights_ref = bf16[32,32,256]{2,1,0:T(8,128)(2,1)S(1)} all-gather(bf16[16,32,256]{2,1,0:T(8,128)(2,1)S(1)} %all-to-all-done.2), channel_id=1, replica_groups=mesh['group'=2,'plane'=16,'core'=2,'mp'=8] {'core'}, dimensions={0}, use_global_device_ids=true | all-gather | bytes 786432 | tf_op jit(solution)/shard_map/all_gather | solution.py:544
  89.4 0.0 collective-permute-done.3.cross_noised_ref
  89.4 1.3 shard_map.162
  90.7 19.8 %all_to_all.30.parts_ref = bf16[8,32,512]{2,1,0:T(8,128)(2,1)S(1)} all-to-all(bf16[8,32,512]{2,1,0:T(8,128)(2,1)S(1)} %get-tuple-element.28), channel_id=1, replica_groups=mesh['group'=2,'plane'=16,'core'=2,'mp'=8] {'mp'}, dimensions={0} | all-to-all | bytes 524288 | tf_op jit(solution)/shard_map/all_to_all | solution.py:62
  110.5 0.7 shard_map.163
  111.2 11.2 %all_to_all.31.pay_ref = bf16[8,48,128]{2,1,0:T(8,128)(2,1)S(1)} all-to-all(bf16[8,48,128]{2,1,0:T(8,128)(2,1)S(1)} %get-tuple-element.31), channel_id=1, replica_groups=mesh['group'=2,'plane'=16,'core'=2,'mp'=8] {'mp'}, dimensions={0} | all-to-all | bytes 196608 | tf_op jit(solution)/shard_map/all_to_all | solution.py:62
  122.4 1.2 shard_map.164
  123.6 11.5 %all_to_all.32.parts_ref = bf16[8,64,128]{2,1,0:T(8,128)(2,1)S(1)} all-to-all(bf16[8,64,128]{2,1,0:T(8,128)(2,1)S(1)} %get-tuple-element.37), channel_id=1, replica_groups=mesh['group'=2,'plane'=16,'core'=2,'mp'=8] {'mp'}, dimensions={0} | all-to-all | bytes 262144 | tf_op jit(solution)/shard_map/all_to_all | solution.py:62
  135.0 0.6 shard_map.165
  (6 shorter events, 0.1 us)
Async XLA Ops:
  0.6 1.0 copy-start
  0.6 1.3 copy-start.1
  1.9 13.0 %copy-start.5 = (bf16[96,768]{1,0:T(8,128)(2,1)S(1)}, bf16[96,768]{1,0:T(8,128)(2,1)}, u32[]{:S(2)}) copy-start(bf16[96,768]{1,0:T(8,128)(2,1)} %param.22) | copy-start | bytes 442372
  1.9 13.0 %copy-start.6 = (bf16[768,96]{0,1:T(8,128)(2,1)S(1)}, bf16[768,96]{0,1:T(8,128)(2,1)}, u32[]{:S(2)}) copy-start(bf16[768,96]{0,1:T(8,128)(2,1)} %param.23) | copy-start | bytes 442372
  3.8 17.6 %all-to-all-start = ((bf16[64,3,128]{2,1,0:T(4,128)(2,1)}), bf16[64,3,128]{2,1,0:T(4,128)(2,1)S(1)}, u32[]{:S(2)}, u32[]{:S(2)}) async-start(bf16[64,3,128]{2,1,0:T(4,128)(2,1)} %get-tuple-element.23), calls=%async_computation | async-start | bytes 131072 | tf_op jit(solution)/shard_map/all_to_all | solution.py:62
  14.3 3.0 %collective-permute-start.4 = (bf16[96,384]{1,0:T(8,128)(2,1)S(1)}, bf16[96,384]{1,0:T(8,128)(2,1)S(1)}, u32[]{:S(2)}, u32[]{:S(2)}) collective-permute-start(bf16[96,384]{1,0:T(8,128)(2,1)S(1)} %get-tuple-element.26), channel_id=1, source_target_pairs={{0,0},{1,32},{2,64},{3,96},{4,128},{5,160},{6,192},{7,224},{8,8},{... | collective-permute-start | bytes 221192 | tf_op jit(solution)/shard_map/ppermute | solution.py:516
  22.5 21.8 %copy-start.2 = (bf16[64,384]{1,0:T(8,128)(2,1)S(1)}, bf16[64,384]{1,0:T(8,128)(2,1)}, u32[]{:S(2)}) copy-start(bf16[64,384]{1,0:T(8,128)(2,1)} %embed_ref.3) | copy-start | bytes 147460
  22.5 21.8 %copy-start.3 = (bf16[1,128,384]{2,1,0:T(8,128)(2,1)S(1)}, bf16[1,128,384]{2,1,0:T(8,128)(2,1)}, u32[]{:S(2)}) copy-start(bf16[1,128,384]{2,1,0:T(8,128)(2,1)} %param.14) | copy-start | bytes 294916
  22.5 21.8 %copy-start.4 = (bf16[384,64]{0,1:T(8,128)(2,1)S(1)}, bf16[384,64]{0,1:T(8,128)(2,1)}, u32[]{:S(2)}) copy-start(bf16[384,64]{0,1:T(8,128)(2,1)} %param.17) | copy-start | bytes 147460
  22.5 36.3 %all-to-all-start.1 = ((bf16[16,32,256]{2,1,0:T(8,128)(2,1)}), bf16[16,32,256]{2,1,0:T(8,128)(2,1)S(1)}, u32[]{:S(2)}, u32[]{:S(2)}) async-start(bf16[16,32,256]{2,1,0:T(8,128)(2,1)} %shard_map.160), calls=%async_computation.1 | async-start | bytes 524288 | tf_op jit(solution)/shard_map/all_to_all | solution.py:62
  44.7 6.0 %collective-permute-start = (f32[104,128]{1,0:T(8,128)S(1)}, f32[104,128]{1,0:T(8,128)S(1)}, u32[]{:S(2)}, u32[]{:S(2)}) collective-permute-start(f32[104,128]{1,0:T(8,128)S(1)} %shard_map.158), channel_id=1, source_target_pairs={{0,1},{1,0},{2,3},{3,2},{4,5},{5,4},{6,7},{7,6},{8,9},{9,8},{10,11... | collective-permute-start | bytes 159752 | tf_op jit(solution)/shard_map/ppermute | solution.py:538
  50.8 8.0 %collective-permute-start.1 = (f32[104,128]{1,0:T(8,128)S(1)}, f32[104,128]{1,0:T(8,128)S(1)}, u32[]{:S(2)}, u32[]{:S(2)}) collective-permute-start(f32[104,128]{1,0:T(8,128)S(1)} %add.9), channel_id=1, source_target_pairs={{0,2},{1,3},{2,0},{3,1},{4,6},{5,7},{6,4},{7,5},{8,10},{9,11},{10,... | collective-permute-start | bytes 159752 | tf_op jit(solution)/shard_map/ppermute | solution.py:538
  59.5 27.7 %all-to-all-start.2 = ((bf16[16,32,256]{2,1,0:T(8,128)(2,1)}), bf16[16,32,256]{2,1,0:T(8,128)(2,1)S(1)}, u32[]{:S(2)}, u32[]{:S(2)}) async-start(bf16[16,32,256]{2,1,0:T(8,128)(2,1)} %shard_map.161), calls=%async_computation.2 | async-start | bytes 524288 | tf_op jit(solution)/shard_map/all_to_all | solution.py:62
  69.2 10.6 %collective-permute-start.2 = (f32[104,128]{1,0:T(8,128)S(1)}, f32[104,128]{1,0:T(8,128)S(1)}, u32[]{:S(2)}, u32[]{:S(2)}) collective-permute-start(f32[104,128]{1,0:T(8,128)S(1)} %add.10.order_ref), channel_id=1, source_target_pairs={{0,4},{1,5},{2,6},{3,7},{4,0},{5,1},{6,2},{7,3},{8,12},{9,13},{10,... | collective-permute-start | bytes 159752 | tf_op jit(solution)/shard_map/ppermute | solution.py:538
  80.1 9.3 %collective-permute-start.3 = (bf16[64,128]{1,0:T(8,128)(2,1)S(1)}, bf16[64,128]{1,0:T(8,128)(2,1)S(1)}, u32[]{:S(2)}, u32[]{:S(2)}) collective-permute-start(bf16[64,128]{1,0:T(8,128)(2,1)S(1)} %get-tuple-element.25.noised_ref), channel_id=1, source_target_pairs={{8,16},{16,8},{24,32},{32,24},{40,48},{48,40},{56,64},{64,56},{72,... | collective-permute-start | bytes 49160 | tf_op jit(solution)/shard_map/ppermute | solution.py:553

commit v5 on v4

--- a/solution.py
+++ b/solution.py
@@ -148,7 +148,7 @@
     store.start()
 
     rows = sent_ref.shape[0]
-    start = pl.multiple_of((seq_index() % (width // rows)) * rows, rows)
+    start = pl.multiple_of((lax.axis_index("plane") % (width // rows)) * rows, rows)
     embed = embed_ref[...]
     gain = 1.0 + tmod_ref[1:2]
     queries = jnp.concatenate(
@@ -477,7 +477,7 @@
     )[0]
     time_row = jnp.broadcast_to(timestep.astype(F32)[:, None], (8, tokens))
     ratio = seqs // mps
-    rows = local_width // ratio
+    rows = 2 * local_width // ratio
     pieces = local_width // 128
     sent, mods, cross, taps, noise_t = call(
         open_body,
@@ -518,7 +518,6 @@
     mods = exchange(mods, ("group",) + SEQ)
     slices = jnp.concatenate([down_weight.T, up_weight], axis=0)
     slices = lax.all_gather(slices, "core", axis=0, tiled=True)
-    got = lax.all_gather(got, "core", axis=0, tiled=True)
     (terms,) = call(
         functools.partial(weight_body, latent=latent),
         [((planes, units // seqs + 8, 2 * channels), BF16)],

time: 136 us -> 139 us (1.022)
  starting transfers between devices: 60.6 us -> 63.9 us
  blocking collectives: 53.9 us -> 51.6 us
  waiting for transfers between devices: 10.7 us -> 12.5 us
    all_to_all x3, starting transfers between devices: 41.8 us -> 44.1 us  [exchange(): return lax.all_to_all(value, axes, 0, 0, tiled=False)]
    all_gather x1 -> x0, blocking collectives: 1.9 us -> none  [per_device(): got = lax.all_gather(got, 'core', axis=0, tiled=True)]
    all_to_all x3, waiting for transfers between devices: 2.27 us -> 4.16 us  [exchange(): return lax.all_to_all(value, axes, 0, 0, tiled=False)]
where the time goes in v5:
time: 139 us
  starting transfers between devices  63.9 us (46%)
  blocking collectives  51.6 us (37%)
  waiting for transfers between devices  12.5 us (9%)
  Pallas kernels  8.26 us (6%)
  between operations  1.54 us (1%)
    all_to_all x3, starting transfers between devices, exchange(): return lax.all_to_all(value, axes, 0, 0, tiled=False)  44.1 us
    all_to_all x3, blocking collectives, exchange(): return lax.all_to_all(value, axes, 0, 0, tiled=False)  42.1 us
    ppermute x3, starting transfers between devices, per_device(): sums = sums + lax.ppermute(sums, 'mp', [(i, i ^ step) for i in range(mps)])  17.3 us
    ppermute x3, waiting for transfers between devices, per_device(): sums = sums + lax.ppermute(sums, 'mp', [(i, i ^ step) for i in range(mps)])  8.31 us
    pallas_call x9, Pallas kernels, call(): pl.pallas_call(body, in_specs=[smem] * len(scalars) + [vmem] * len(arrays...  8.26 us
    all_gather x1, blocking collectives, per_device(): pair = lax.all_gather(noised, 'core', axis=0, tiled=True)  5.16 us
    all_to_all x3, waiting for transfers between devices, exchange(): return lax.all_to_all(value, axes, 0, 0, tiled=False)  4.16 us
  transfers between devices with their start and end apart: 8, of which 4 were waited for; matrix products, arithmetic and copies ran while one was open for 0% of the time, Pallas kernels for 1%

profile of v5, /device:TPU:24, one launch (start us, length us, event | category | flops | bytes accessed | tf_op | source)
XLA Modules:
  0.0 138.5 jit_solution(13880118243614555036)
XLA Ops:
  0.6 0.0 copy-start
  0.6 0.0 copy-start.1
  1.4 0.1 fusion.4
  1.4 0.2 copy-done
  1.6 0.3 fusion
  1.9 0.0 copy-done.1
  1.9 0.0 copy-start.5
  1.9 0.0 copy-start.6
  2.0 1.9 %shard_map.157 = (bf16[192,384]{1,0:T(8,128)(2,1)S(1)}, bf16[64,3,128]{2,1,0:T(4,128)(2,1)}, bf16[8,32,128]{2,1,0:T(8,128)(2,1)S(1)}, f32[64,16]{1,0:T(8,128)S(1)}, bf16[64,128]{1,0:T(8,128)(2,1)S(1)}) custom-call(s32[1,4]{1,0:T(1,128)} %disc_ref.3, f32[2,96]{1,0:T(2,128)} %cond_ref.1, bf16[96,384]{1,0:T(8,128)(2,1)} %bitcast.30, f32[2,384]{1,0:T(2,128)S(1)} %bitcast.28, ...), custom_call_target="tpu_custom_call" | custom-call | tf_op jit(solution)/shard_map/pallas_call | solution.py:79
  3.8 10.5 %all-to-all-start = ((bf16[64,3,128]{2,1,0:T(4,128)(2,1)}), bf16[64,3,128]{2,1,0:T(4,128)(2,1)S(1)}, u32[]{:S(2)}, u32[]{:S(2)}) async-start(bf16[64,3,128]{2,1,0:T(4,128)(2,1)} %get-tuple-element.23), calls=%async_computation | async-start | bytes 131072 | tf_op jit(solution)/shard_map/all_to_all | solution.py:62
  14.3 0.7 collective-permute-start.4
  15.0 0.0 copy-done.5
  15.0 0.0 copy-done.6
  15.0 2.2 %all_gather.10.pair_ref = bf16[384,768]{1,0:T(8,128)(2,1)S(1)} all-gather(bf16[192,768]{1,0:T(8,128)(2,1)S(1)} %pad_maximum_fusion), channel_id=1, replica_groups=mesh['group'=2,'plane'=16,'core'=2,'mp'=8] {'core'}, dimensions={0}, use_global_device_ids=true | all-gather | bytes 884736 | tf_op jit(solution)/shard_map/all_gather | solution.py:520
  17.2 4.2 %all-to-all-done.mod_ref.order_ref = bf16[64,3,128]{2,1,0:T(4,128)(2,1)S(1)} async-done(((bf16[64,3,128]{2,1,0:T(4,128)(2,1)}), bf16[64,3,128]{2,1,0:T(4,128)(2,1)S(1)}, u32[]{:S(2)}, u32[]{:S(2)}) %all-to-all-start) | async-done | bytes 49184 | tf_op jit(solution)/shard_map/all_to_all | solution.py:62
  21.4 0.0 collective-permute-done.4.got_ref
  21.4 1.1 shard_map.160
  22.5 0.0 copy-start.2
  22.5 0.0 copy-start.3
  22.5 0.0 copy-start.4
  22.5 24.0 %all-to-all-start.1 = ((bf16[16,32,256]{2,1,0:T(8,128)(2,1)}), bf16[16,32,256]{2,1,0:T(8,128)(2,1)S(1)}, u32[]{:S(2)}, u32[]{:S(2)}) async-start(bf16[16,32,256]{2,1,0:T(8,128)(2,1)} %shard_map.160), calls=%async_computation.1 | async-start | bytes 524288 | tf_op jit(solution)/shard_map/all_to_all | solution.py:62
  46.5 0.0 copy-done.2
  46.5 0.0 copy-done.3
  46.5 0.0 copy-done.4
  46.5 0.5 shard_map.158
  47.0 1.9 %collective-permute-start = (f32[104,128]{1,0:T(8,128)S(1)}, f32[104,128]{1,0:T(8,128)S(1)}, u32[]{:S(2)}, u32[]{:S(2)}) collective-permute-start(f32[104,128]{1,0:T(8,128)S(1)} %shard_map.158), channel_id=1, source_target_pairs={{0,1},{1,0},{2,3},{3,2},{4,5},{5,4},{6,7},{7,6},{8,9},{9,8},{10,11... | collective-permute-start | bytes 159752 | tf_op jit(solution)/shard_map/ppermute | solution.py:537
  48.9 4.1 %collective-permute-done = f32[104,128]{1,0:T(8,128)S(1)} collective-permute-done((f32[104,128]{1,0:T(8,128)S(1)}, f32[104,128]{1,0:T(8,128)S(1)}, u32[]{:S(2)}, u32[]{:S(2)}) %collective-permute-start) | collective-permute-done | bytes 53280 | tf_op jit(solution)/shard_map/ppermute | solution.py:537
  53.0 4.9 %collective-permute-start.1 = (f32[104,128]{1,0:T(8,128)S(1)}, f32[104,128]{1,0:T(8,128)S(1)}, u32[]{:S(2)}, u32[]{:S(2)}) collective-permute-start(f32[104,128]{1,0:T(8,128)S(1)} %add.9), channel_id=1, source_target_pairs={{0,2},{1,3},{2,0},{3,1},{4,6},{5,7},{6,4},{7,5},{8,10},{9,11},{10,... | collective-permute-start | bytes 159752 | tf_op jit(solution)/shard_map/ppermute | solution.py:537
  57.9 2.1 %collective-permute-done.1 = f32[104,128]{1,0:T(8,128)S(1)} collective-permute-done((f32[104,128]{1,0:T(8,128)S(1)}, f32[104,128]{1,0:T(8,128)S(1)}, u32[]{:S(2)}, u32[]{:S(2)}) %collective-permute-start.1) | collective-permute-done | bytes 53280 | tf_op jit(solution)/shard_map/ppermute | solution.py:537
  60.0 0.0 all-to-all-done.1.parts_ref
  60.0 0.8 shard_map.161
  60.8 9.6 %all-to-all-start.2 = ((bf16[16,32,256]{2,1,0:T(8,128)(2,1)}), bf16[16,32,256]{2,1,0:T(8,128)(2,1)S(1)}, u32[]{:S(2)}, u32[]{:S(2)}) async-start(bf16[16,32,256]{2,1,0:T(8,128)(2,1)} %shard_map.161), calls=%async_computation.2 | async-start | bytes 524288 | tf_op jit(solution)/shard_map/all_to_all | solution.py:62
  70.4 10.5 %collective-permute-start.2 = (f32[104,128]{1,0:T(8,128)S(1)}, f32[104,128]{1,0:T(8,128)S(1)}, u32[]{:S(2)}, u32[]{:S(2)}) collective-permute-start(f32[104,128]{1,0:T(8,128)S(1)} %add.10.order_ref), channel_id=1, source_target_pairs={{0,4},{1,5},{2,6},{3,7},{4,0},{5,1},{6,2},{7,3},{8,12},{9,13},{10,... | collective-permute-start | bytes 159752 | tf_op jit(solution)/shard_map/ppermute | solution.py:537
  80.9 2.1 %collective-permute-done.2 = f32[104,128]{1,0:T(8,128)S(1)} collective-permute-done((f32[104,128]{1,0:T(8,128)S(1)}, f32[104,128]{1,0:T(8,128)S(1)}, u32[]{:S(2)}, u32[]{:S(2)}) %collective-permute-start.2) | collective-permute-done | bytes 53280 | tf_op jit(solution)/shard_map/ppermute | solution.py:537
  83.0 0.3 shard_map.159
  83.4 1.9 %collective-permute-start.3 = (bf16[64,128]{1,0:T(8,128)(2,1)S(1)}, bf16[64,128]{1,0:T(8,128)(2,1)S(1)}, u32[]{:S(2)}, u32[]{:S(2)}) collective-permute-start(bf16[64,128]{1,0:T(8,128)(2,1)S(1)} %get-tuple-element.25.noised_ref), channel_id=1, source_target_pairs={{8,16},{16,8},{24,32},{32,24},{40,48},{48,40},{56,64},{64,56},{72,... | collective-permute-start | bytes 49160 | tf_op jit(solution)/shard_map/ppermute | solution.py:552
  85.3 5.2 %all_gather.9.pair_ref = bf16[128,128]{1,0:T(8,128)(2,1)S(1)} all-gather(bf16[64,128]{1,0:T(8,128)(2,1)S(1)} %get-tuple-element.25.noised_ref), channel_id=1, replica_groups=mesh['group'=2,'plane'=16,'core'=2,'mp'=8] {'core'}, dimensions={0}, use_global_device_ids=true | all-gather | bytes 49152 | tf_op jit(solution)/shard_map/all_gather | solution.py:553
  90.4 0.0 all-to-all-done.2
  90.4 2.2 %all_gather.11.weights_ref = bf16[32,32,256]{2,1,0:T(8,128)(2,1)S(1)} all-gather(bf16[16,32,256]{2,1,0:T(8,128)(2,1)S(1)} %all-to-all-done.2), channel_id=1, replica_groups=mesh['group'=2,'plane'=16,'core'=2,'mp'=8] {'core'}, dimensions={0}, use_global_device_ids=true | all-gather | bytes 786432 | tf_op jit(solution)/shard_map/all_gather | solution.py:543
  92.6 0.0 collective-permute-done.3.cross_noised_ref
  92.6 1.3 shard_map.162
  93.9 19.4 %all_to_all.30.parts_ref = bf16[8,32,512]{2,1,0:T(8,128)(2,1)S(1)} all-to-all(bf16[8,32,512]{2,1,0:T(8,128)(2,1)S(1)} %get-tuple-element.28), channel_id=1, replica_groups=mesh['group'=2,'plane'=16,'core'=2,'mp'=8] {'mp'}, dimensions={0} | all-to-all | bytes 524288 | tf_op jit(solution)/shard_map/all_to_all | solution.py:62
  113.3 0.7 shard_map.163
  114.0 11.2 %all_to_all.31.pay_ref = bf16[8,48,128]{2,1,0:T(8,128)(2,1)S(1)} all-to-all(bf16[8,48,128]{2,1,0:T(8,128)(2,1)S(1)} %get-tuple-element.31), channel_id=1, replica_groups=mesh['group'=2,'plane'=16,'core'=2,'mp'=8] {'mp'}, dimensions={0} | all-to-all | bytes 196608 | tf_op jit(solution)/shard_map/all_to_all | solution.py:62
  125.2 1.2 shard_map.164
  126.4 11.5 %all_to_all.32.parts_ref = bf16[8,64,128]{2,1,0:T(8,128)(2,1)S(1)} all-to-all(bf16[8,64,128]{2,1,0:T(8,128)(2,1)S(1)} %get-tuple-element.37), channel_id=1, replica_groups=mesh['group'=2,'plane'=16,'core'=2,'mp'=8] {'mp'}, dimensions={0} | all-to-all | bytes 262144 | tf_op jit(solution)/shard_map/all_to_all | solution.py:62
  137.9 0.6 shard_map.165
  (6 shorter events, 0.1 us)
Async XLA Ops:
  0.6 1.0 copy-start
  0.6 1.3 copy-start.1
  1.9 13.0 %copy-start.5 = (bf16[96,768]{1,0:T(8,128)(2,1)S(1)}, bf16[96,768]{1,0:T(8,128)(2,1)}, u32[]{:S(2)}) copy-start(bf16[96,768]{1,0:T(8,128)(2,1)} %param.22) | copy-start | bytes 442372
  1.9 13.0 %copy-start.6 = (bf16[768,96]{0,1:T(8,128)(2,1)S(1)}, bf16[768,96]{0,1:T(8,128)(2,1)}, u32[]{:S(2)}) copy-start(bf16[768,96]{0,1:T(8,128)(2,1)} %param.23) | copy-start | bytes 442372
  3.8 17.6 %all-to-all-start = ((bf16[64,3,128]{2,1,0:T(4,128)(2,1)}), bf16[64,3,128]{2,1,0:T(4,128)(2,1)S(1)}, u32[]{:S(2)}, u32[]{:S(2)}) async-start(bf16[64,3,128]{2,1,0:T(4,128)(2,1)} %get-tuple-element.23), calls=%async_computation | async-start | bytes 131072 | tf_op jit(solution)/shard_map/all_to_all | solution.py:62
  14.3 7.1 %collective-permute-start.4 = (bf16[192,384]{1,0:T(8,128)(2,1)S(1)}, bf16[192,384]{1,0:T(8,128)(2,1)S(1)}, u32[]{:S(2)}, u32[]{:S(2)}) collective-permute-start(bf16[192,384]{1,0:T(8,128)(2,1)S(1)} %get-tuple-element.26), channel_id=1, source_target_pairs={{0,0},{1,32},{2,64},{3,96},{4,128},{5,160},{6,192},{7,224},{8,8},{... | collective-permute-start | bytes 442376 | tf_op jit(solution)/shard_map/ppermute | solution.py:516
  22.5 24.0 %copy-start.2 = (bf16[64,384]{1,0:T(8,128)(2,1)S(1)}, bf16[64,384]{1,0:T(8,128)(2,1)}, u32[]{:S(2)}) copy-start(bf16[64,384]{1,0:T(8,128)(2,1)} %embed_ref.3) | copy-start | bytes 147460
  22.5 24.0 %copy-start.3 = (bf16[1,128,384]{2,1,0:T(8,128)(2,1)S(1)}, bf16[1,128,384]{2,1,0:T(8,128)(2,1)}, u32[]{:S(2)}) copy-start(bf16[1,128,384]{2,1,0:T(8,128)(2,1)} %param.14) | copy-start | bytes 294916
  22.5 24.0 %copy-start.4 = (bf16[384,64]{0,1:T(8,128)(2,1)S(1)}, bf16[384,64]{0,1:T(8,128)(2,1)}, u32[]{:S(2)}) copy-start(bf16[384,64]{0,1:T(8,128)(2,1)} %param.17) | copy-start | bytes 147460
  22.5 37.5 %all-to-all-start.1 = ((bf16[16,32,256]{2,1,0:T(8,128)(2,1)}), bf16[16,32,256]{2,1,0:T(8,128)(2,1)S(1)}, u32[]{:S(2)}, u32[]{:S(2)}) async-start(bf16[16,32,256]{2,1,0:T(8,128)(2,1)} %shard_map.160), calls=%async_computation.1 | async-start | bytes 524288 | tf_op jit(solution)/shard_map/all_to_all | solution.py:62
  47.0 6.0 %collective-permute-start = (f32[104,128]{1,0:T(8,128)S(1)}, f32[104,128]{1,0:T(8,128)S(1)}, u32[]{:S(2)}, u32[]{:S(2)}) collective-permute-start(f32[104,128]{1,0:T(8,128)S(1)} %shard_map.158), channel_id=1, source_target_pairs={{0,1},{1,0},{2,3},{3,2},{4,5},{5,4},{6,7},{7,6},{8,9},{9,8},{10,11... | collective-permute-start | bytes 159752 | tf_op jit(solution)/shard_map/ppermute | solution.py:537
  53.0 7.0 %collective-permute-start.1 = (f32[104,128]{1,0:T(8,128)S(1)}, f32[104,128]{1,0:T(8,128)S(1)}, u32[]{:S(2)}, u32[]{:S(2)}) collective-permute-start(f32[104,128]{1,0:T(8,128)S(1)} %add.9), channel_id=1, source_target_pairs={{0,2},{1,3},{2,0},{3,1},{4,6},{5,7},{6,4},{7,5},{8,10},{9,11},{10,... | collective-permute-start | bytes 159752 | tf_op jit(solution)/shard_map/ppermute | solution.py:537
  60.8 29.6 %all-to-all-start.2 = ((bf16[16,32,256]{2,1,0:T(8,128)(2,1)}), bf16[16,32,256]{2,1,0:T(8,128)(2,1)S(1)}, u32[]{:S(2)}, u32[]{:S(2)}) async-start(bf16[16,32,256]{2,1,0:T(8,128)(2,1)} %shard_map.161), calls=%async_computation.2 | async-start | bytes 524288 | tf_op jit(solution)/shard_map/all_to_all | solution.py:62
  70.4 12.6 %collective-permute-start.2 = (f32[104,128]{1,0:T(8,128)S(1)}, f32[104,128]{1,0:T(8,128)S(1)}, u32[]{:S(2)}, u32[]{:S(2)}) collective-permute-start(f32[104,128]{1,0:T(8,128)S(1)} %add.10.order_ref), channel_id=1, source_target_pairs={{0,4},{1,5},{2,6},{3,7},{4,0},{5,1},{6,2},{7,3},{8,12},{9,13},{10,... | collective-permute-start | bytes 159752 | tf_op jit(solution)/shard_map/ppermute | solution.py:537
  83.4 9.3 %collective-permute-start.3 = (bf16[64,128]{1,0:T(8,128)(2,1)S(1)}, bf16[64,128]{1,0:T(8,128)(2,1)S(1)}, u32[]{:S(2)}, u32[]{:S(2)}) collective-permute-start(bf16[64,128]{1,0:T(8,128)(2,1)S(1)} %get-tuple-element.25.noised_ref), channel_id=1, source_target_pairs={{8,16},{16,8},{24,32},{32,24},{40,48},{48,40},{56,64},{64,56},{72,... | collective-permute-start | bytes 49160 | tf_op jit(solution)/shard_map/ppermute | solution.py:552

commit v6 on v5

--- a/solution.py
+++ b/solution.py
@@ -532,10 +532,10 @@
         [student_hidden[0], student_out.T, teacher_embed, mods],
     )
     stages = [sums]
-    step = 1
-    while step < mps:
-        sums = sums + lax.ppermute(sums, "mp", [(i, i ^ step) for i in range(mps)])
-        step *= 2
+    hops = [1 << bit for bit in range(mps.bit_length() - 1)]
+    hops[:2] = hops[:2][::-1]
+    for hop in hops:
+        sums = sums + lax.ppermute(sums, "mp", [(i, i ^ hop) for i in range(mps)])
         stages.append(sums)
     halfway = stages[-2]
     (terms,) = call(gather_body, [((planes, units // seqs + 8, 2 * channels), BF16)], [], [terms, halfway])

time: 139 us -> 139 us (level)
  no operation moved by 1% of the time
where the time goes in v6:
time: 139 us
  starting transfers between devices  63.9 us (46%)
  blocking collectives  51.6 us (37%)
  waiting for transfers between devices  12.5 us (9%)
  Pallas kernels  8.27 us (6%)
  between operations  1.54 us (1%)
    all_to_all x3, starting transfers between devices, exchange(): return lax.all_to_all(value, axes, 0, 0, tiled=False)  44.1 us
    all_to_all x3, blocking collectives, exchange(): return lax.all_to_all(value, axes, 0, 0, tiled=False)  42.1 us
    ppermute x3, starting transfers between devices, per_device(): sums = sums + lax.ppermute(sums, 'mp', [(i, i ^ hop) for i in range(mps)])  17.3 us
    ppermute x3, waiting for transfers between devices, per_device(): sums = sums + lax.ppermute(sums, 'mp', [(i, i ^ hop) for i in range(mps)])  8.3 us
    pallas_call x9, Pallas kernels, call(): pl.pallas_call(body, in_specs=[smem] * len(scalars) + [vmem] * len(arrays...  8.27 us
    all_gather x1, blocking collectives, per_device(): pair = lax.all_gather(noised, 'core', axis=0, tiled=True)  5.16 us
    all_to_all x3, waiting for transfers between devices, exchange(): return lax.all_to_all(value, axes, 0, 0, tiled=False)  4.16 us
  transfers between devices with their start and end apart: 8, of which 4 were waited for; matrix products, arithmetic and copies ran while one was open for 0% of the time, Pallas kernels for 1%

profile of v6, /device:TPU:24, one launch (start us, length us, event | category | flops | bytes accessed | tf_op | source)
XLA Modules:
  0.0 138.5 jit_solution(10029609730525998855)
XLA Ops:
  0.6 0.0 copy-start
  0.6 0.0 copy-start.1
  1.4 0.1 fusion.4
  1.4 0.2 copy-done
  1.6 0.3 fusion
  1.9 0.0 copy-done.1
  1.9 0.0 copy-start.5
  1.9 0.0 copy-start.6
  2.0 1.9 %shard_map.157 = (bf16[192,384]{1,0:T(8,128)(2,1)S(1)}, bf16[64,3,128]{2,1,0:T(4,128)(2,1)}, bf16[8,32,128]{2,1,0:T(8,128)(2,1)S(1)}, f32[64,16]{1,0:T(8,128)S(1)}, bf16[64,128]{1,0:T(8,128)(2,1)S(1)}) custom-call(s32[1,4]{1,0:T(1,128)} %disc_ref.3, f32[2,96]{1,0:T(2,128)} %cond_ref.1, bf16[96,384]{1,0:T(8,128)(2,1)} %bitcast.30, f32[2,384]{1,0:T(2,128)S(1)} %bitcast.28, ...), custom_call_target="tpu_custom_call" | custom-call | tf_op jit(solution)/shard_map/pallas_call | solution.py:79
  3.8 10.5 %all-to-all-start = ((bf16[64,3,128]{2,1,0:T(4,128)(2,1)}), bf16[64,3,128]{2,1,0:T(4,128)(2,1)S(1)}, u32[]{:S(2)}, u32[]{:S(2)}) async-start(bf16[64,3,128]{2,1,0:T(4,128)(2,1)} %get-tuple-element.23), calls=%async_computation | async-start | bytes 131072 | tf_op jit(solution)/shard_map/all_to_all | solution.py:62
  14.3 0.7 collective-permute-start.4
  15.0 0.0 copy-done.5
  15.0 0.0 copy-done.6
  15.0 2.2 %all_gather.10.pair_ref = bf16[384,768]{1,0:T(8,128)(2,1)S(1)} all-gather(bf16[192,768]{1,0:T(8,128)(2,1)S(1)} %pad_maximum_fusion), channel_id=1, replica_groups=mesh['group'=2,'plane'=16,'core'=2,'mp'=8] {'core'}, dimensions={0}, use_global_device_ids=true | all-gather | bytes 884736 | tf_op jit(solution)/shard_map/all_gather | solution.py:520
  17.2 4.2 %all-to-all-done.mod_ref.order_ref = bf16[64,3,128]{2,1,0:T(4,128)(2,1)S(1)} async-done(((bf16[64,3,128]{2,1,0:T(4,128)(2,1)}), bf16[64,3,128]{2,1,0:T(4,128)(2,1)S(1)}, u32[]{:S(2)}, u32[]{:S(2)}) %all-to-all-start) | async-done | bytes 49184 | tf_op jit(solution)/shard_map/all_to_all | solution.py:62
  21.4 0.0 collective-permute-done.4.got_ref
  21.4 1.1 shard_map.160
  22.5 0.0 copy-start.2
  22.5 0.0 copy-start.3
  22.5 0.0 copy-start.4
  22.5 24.0 %all-to-all-start.1 = ((bf16[16,32,256]{2,1,0:T(8,128)(2,1)}), bf16[16,32,256]{2,1,0:T(8,128)(2,1)S(1)}, u32[]{:S(2)}, u32[]{:S(2)}) async-start(bf16[16,32,256]{2,1,0:T(8,128)(2,1)} %shard_map.160), calls=%async_computation.1 | async-start | bytes 524288 | tf_op jit(solution)/shard_map/all_to_all | solution.py:62
  46.5 0.0 copy-done.2
  46.5 0.0 copy-done.3
  46.5 0.0 copy-done.4
  46.5 0.5 shard_map.158
  47.0 4.9 %collective-permute-start = (f32[104,128]{1,0:T(8,128)S(1)}, f32[104,128]{1,0:T(8,128)S(1)}, u32[]{:S(2)}, u32[]{:S(2)}) collective-permute-start(f32[104,128]{1,0:T(8,128)S(1)} %shard_map.158), channel_id=1, source_target_pairs={{0,2},{1,3},{2,0},{3,1},{4,6},{5,7},{6,4},{7,5},{8,10},{9,11},{10,... | collective-permute-start | bytes 159752 | tf_op jit(solution)/shard_map/ppermute | solution.py:538
  51.9 2.1 %collective-permute-done = f32[104,128]{1,0:T(8,128)S(1)} collective-permute-done((f32[104,128]{1,0:T(8,128)S(1)}, f32[104,128]{1,0:T(8,128)S(1)}, u32[]{:S(2)}, u32[]{:S(2)}) %collective-permute-start) | collective-permute-done | bytes 53280 | tf_op jit(solution)/shard_map/ppermute | solution.py:538
  54.0 1.9 %collective-permute-start.1 = (f32[104,128]{1,0:T(8,128)S(1)}, f32[104,128]{1,0:T(8,128)S(1)}, u32[]{:S(2)}, u32[]{:S(2)}) collective-permute-start(f32[104,128]{1,0:T(8,128)S(1)} %add.9), channel_id=1, source_target_pairs={{0,1},{1,0},{2,3},{3,2},{4,5},{5,4},{6,7},{7,6},{8,9},{9,8},{10,11... | collective-permute-start | bytes 159752 | tf_op jit(solution)/shard_map/ppermute | solution.py:538
  55.9 4.1 %collective-permute-done.1 = f32[104,128]{1,0:T(8,128)S(1)} collective-permute-done((f32[104,128]{1,0:T(8,128)S(1)}, f32[104,128]{1,0:T(8,128)S(1)}, u32[]{:S(2)}, u32[]{:S(2)}) %collective-permute-start.1) | collective-permute-done | bytes 53280 | tf_op jit(solution)/shard_map/ppermute | solution.py:538
  60.0 0.0 all-to-all-done.1.parts_ref
  60.0 0.8 shard_map.161
  60.8 9.6 %all-to-all-start.2 = ((bf16[16,32,256]{2,1,0:T(8,128)(2,1)}), bf16[16,32,256]{2,1,0:T(8,128)(2,1)S(1)}, u32[]{:S(2)}, u32[]{:S(2)}) async-start(bf16[16,32,256]{2,1,0:T(8,128)(2,1)} %shard_map.161), calls=%async_computation.2 | async-start | bytes 524288 | tf_op jit(solution)/shard_map/all_to_all | solution.py:62
  70.4 10.5 %collective-permute-start.2 = (f32[104,128]{1,0:T(8,128)S(1)}, f32[104,128]{1,0:T(8,128)S(1)}, u32[]{:S(2)}, u32[]{:S(2)}) collective-permute-start(f32[104,128]{1,0:T(8,128)S(1)} %add.10.order_ref), channel_id=1, source_target_pairs={{0,4},{1,5},{2,6},{3,7},{4,0},{5,1},{6,2},{7,3},{8,12},{9,13},{10,... | collective-permute-start | bytes 159752 | tf_op jit(solution)/shard_map/ppermute | solution.py:538
  80.9 2.1 %collective-permute-done.2 = f32[104,128]{1,0:T(8,128)S(1)} collective-permute-done((f32[104,128]{1,0:T(8,128)S(1)}, f32[104,128]{1,0:T(8,128)S(1)}, u32[]{:S(2)}, u32[]{:S(2)}) %collective-permute-start.2) | collective-permute-done | bytes 53280 | tf_op jit(solution)/shard_map/ppermute | solution.py:538
  83.0 0.3 shard_map.159
  83.3 1.9 %collective-permute-start.3 = (bf16[64,128]{1,0:T(8,128)(2,1)S(1)}, bf16[64,128]{1,0:T(8,128)(2,1)S(1)}, u32[]{:S(2)}, u32[]{:S(2)}) collective-permute-start(bf16[64,128]{1,0:T(8,128)(2,1)S(1)} %get-tuple-element.25.noised_ref), channel_id=1, source_target_pairs={{8,16},{16,8},{24,32},{32,24},{40,48},{48,40},{56,64},{64,56},{72,... | collective-permute-start | bytes 49160 | tf_op jit(solution)/shard_map/ppermute | solution.py:552
  85.3 5.2 %all_gather.9.pair_ref = bf16[128,128]{1,0:T(8,128)(2,1)S(1)} all-gather(bf16[64,128]{1,0:T(8,128)(2,1)S(1)} %get-tuple-element.25.noised_ref), channel_id=1, replica_groups=mesh['group'=2,'plane'=16,'core'=2,'mp'=8] {'core'}, dimensions={0}, use_global_device_ids=true | all-gather | bytes 49152 | tf_op jit(solution)/shard_map/all_gather | solution.py:553
  90.4 0.0 all-to-all-done.2
  90.4 2.2 %all_gather.11.weights_ref = bf16[32,32,256]{2,1,0:T(8,128)(2,1)S(1)} all-gather(bf16[16,32,256]{2,1,0:T(8,128)(2,1)S(1)} %all-to-all-done.2), channel_id=1, replica_groups=mesh['group'=2,'plane'=16,'core'=2,'mp'=8] {'core'}, dimensions={0}, use_global_device_ids=true | all-gather | bytes 786432 | tf_op jit(solution)/shard_map/all_gather | solution.py:543
  92.6 0.0 collective-permute-done.3.cross_noised_ref
  92.6 1.3 shard_map.162
  93.9 19.4 %all_to_all.30.parts_ref = bf16[8,32,512]{2,1,0:T(8,128)(2,1)S(1)} all-to-all(bf16[8,32,512]{2,1,0:T(8,128)(2,1)S(1)} %get-tuple-element.28), channel_id=1, replica_groups=mesh['group'=2,'plane'=16,'core'=2,'mp'=8] {'mp'}, dimensions={0} | all-to-all | bytes 524288 | tf_op jit(solution)/shard_map/all_to_all | solution.py:62
  113.3 0.7 shard_map.163
  114.0 11.2 %all_to_all.31.pay_ref = bf16[8,48,128]{2,1,0:T(8,128)(2,1)S(1)} all-to-all(bf16[8,48,128]{2,1,0:T(8,128)(2,1)S(1)} %get-tuple-element.31), channel_id=1, replica_groups=mesh['group'=2,'plane'=16,'core'=2,'mp'=8] {'mp'}, dimensions={0} | all-to-all | bytes 196608 | tf_op jit(solution)/shard_map/all_to_all | solution.py:62
  125.2 1.2 shard_map.164
  126.4 11.5 %all_to_all.32.parts_ref = bf16[8,64,128]{2,1,0:T(8,128)(2,1)S(1)} all-to-all(bf16[8,64,128]{2,1,0:T(8,128)(2,1)S(1)} %get-tuple-element.37), channel_id=1, replica_groups=mesh['group'=2,'plane'=16,'core'=2,'mp'=8] {'mp'}, dimensions={0} | all-to-all | bytes 262144 | tf_op jit(solution)/shard_map/all_to_all | solution.py:62
  137.9 0.6 shard_map.165
  (6 shorter events, 0.1 us)
Async XLA Ops:
  0.6 1.0 copy-start
  0.6 1.3 copy-start.1
  1.9 13.0 %copy-start.5 = (bf16[96,768]{1,0:T(8,128)(2,1)S(1)}, bf16[96,768]{1,0:T(8,128)(2,1)}, u32[]{:S(2)}) copy-start(bf16[96,768]{1,0:T(8,128)(2,1)} %param.22) | copy-start | bytes 442372
  1.9 13.0 %copy-start.6 = (bf16[768,96]{0,1:T(8,128)(2,1)S(1)}, bf16[768,96]{0,1:T(8,128)(2,1)}, u32[]{:S(2)}) copy-start(bf16[768,96]{0,1:T(8,128)(2,1)} %param.23) | copy-start | bytes 442372
  3.8 17.6 %all-to-all-start = ((bf16[64,3,128]{2,1,0:T(4,128)(2,1)}), bf16[64,3,128]{2,1,0:T(4,128)(2,1)S(1)}, u32[]{:S(2)}, u32[]{:S(2)}) async-start(bf16[64,3,128]{2,1,0:T(4,128)(2,1)} %get-tuple-element.23), calls=%async_computation | async-start | bytes 131072 | tf_op jit(solution)/shard_map/all_to_all | solution.py:62
  14.3 7.1 %collective-permute-start.4 = (bf16[192,384]{1,0:T(8,128)(2,1)S(1)}, bf16[192,384]{1,0:T(8,128)(2,1)S(1)}, u32[]{:S(2)}, u32[]{:S(2)}) collective-permute-start(bf16[192,384]{1,0:T(8,128)(2,1)S(1)} %get-tuple-element.26), channel_id=1, source_target_pairs={{0,0},{1,32},{2,64},{3,96},{4,128},{5,160},{6,192},{7,224},{8,8},{... | collective-permute-start | bytes 442376 | tf_op jit(solution)/shard_map/ppermute | solution.py:516
  22.5 24.0 %copy-start.2 = (bf16[64,384]{1,0:T(8,128)(2,1)S(1)}, bf16[64,384]{1,0:T(8,128)(2,1)}, u32[]{:S(2)}) copy-start(bf16[64,384]{1,0:T(8,128)(2,1)} %embed_ref.3) | copy-start | bytes 147460
  22.5 24.0 %copy-start.3 = (bf16[1,128,384]{2,1,0:T(8,128)(2,1)S(1)}, bf16[1,128,384]{2,1,0:T(8,128)(2,1)}, u32[]{:S(2)}) copy-start(bf16[1,128,384]{2,1,0:T(8,128)(2,1)} %param.14) | copy-start | bytes 294916
  22.5 24.0 %copy-start.4 = (bf16[384,64]{0,1:T(8,128)(2,1)S(1)}, bf16[384,64]{0,1:T(8,128)(2,1)}, u32[]{:S(2)}) copy-start(bf16[384,64]{0,1:T(8,128)(2,1)} %param.17) | copy-start | bytes 147460
  22.5 37.5 %all-to-all-start.1 = ((bf16[16,32,256]{2,1,0:T(8,128)(2,1)}), bf16[16,32,256]{2,1,0:T(8,128)(2,1)S(1)}, u32[]{:S(2)}, u32[]{:S(2)}) async-start(bf16[16,32,256]{2,1,0:T(8,128)(2,1)} %shard_map.160), calls=%async_computation.1 | async-start | bytes 524288 | tf_op jit(solution)/shard_map/all_to_all | solution.py:62
  47.0 7.0 %collective-permute-start = (f32[104,128]{1,0:T(8,128)S(1)}, f32[104,128]{1,0:T(8,128)S(1)}, u32[]{:S(2)}, u32[]{:S(2)}) collective-permute-start(f32[104,128]{1,0:T(8,128)S(1)} %shard_map.158), channel_id=1, source_target_pairs={{0,2},{1,3},{2,0},{3,1},{4,6},{5,7},{6,4},{7,5},{8,10},{9,11},{10,... | collective-permute-start | bytes 159752 | tf_op jit(solution)/shard_map/ppermute | solution.py:538
  54.0 6.0 %collective-permute-start.1 = (f32[104,128]{1,0:T(8,128)S(1)}, f32[104,128]{1,0:T(8,128)S(1)}, u32[]{:S(2)}, u32[]{:S(2)}) collective-permute-start(f32[104,128]{1,0:T(8,128)S(1)} %add.9), channel_id=1, source_target_pairs={{0,1},{1,0},{2,3},{3,2},{4,5},{5,4},{6,7},{7,6},{8,9},{9,8},{10,11... | collective-permute-start | bytes 159752 | tf_op jit(solution)/shard_map/ppermute | solution.py:538
  60.8 29.6 %all-to-all-start.2 = ((bf16[16,32,256]{2,1,0:T(8,128)(2,1)}), bf16[16,32,256]{2,1,0:T(8,128)(2,1)S(1)}, u32[]{:S(2)}, u32[]{:S(2)}) async-start(bf16[16,32,256]{2,1,0:T(8,128)(2,1)} %shard_map.161), calls=%async_computation.2 | async-start | bytes 524288 | tf_op jit(solution)/shard_map/all_to_all | solution.py:62
  70.4 12.6 %collective-permute-start.2 = (f32[104,128]{1,0:T(8,128)S(1)}, f32[104,128]{1,0:T(8,128)S(1)}, u32[]{:S(2)}, u32[]{:S(2)}) collective-permute-start(f32[104,128]{1,0:T(8,128)S(1)} %add.10.order_ref), channel_id=1, source_target_pairs={{0,4},{1,5},{2,6},{3,7},{4,0},{5,1},{6,2},{7,3},{8,12},{9,13},{10,... | collective-permute-start | bytes 159752 | tf_op jit(solution)/shard_map/ppermute | solution.py:538
  83.3 9.3 %collective-permute-start.3 = (bf16[64,128]{1,0:T(8,128)(2,1)S(1)}, bf16[64,128]{1,0:T(8,128)(2,1)S(1)}, u32[]{:S(2)}, u32[]{:S(2)}) collective-permute-start(bf16[64,128]{1,0:T(8,128)(2,1)S(1)} %get-tuple-element.25.noised_ref), channel_id=1, source_target_pairs={{8,16},{16,8},{24,32},{32,24},{40,48},{48,40},{56,64},{64,56},{72,... | collective-permute-start | bytes 49160 | tf_op jit(solution)/shard_map/ppermute | solution.py:552

commit v7 on v6

--- a/solution.py
+++ b/solution.py
@@ -47,7 +47,7 @@
     half_width = width // 2
     index = jnp.arange(half_width, dtype=F32)
     freqs = jnp.exp(-math.log(10000.0) * index / half_width)
-    angles = timestep.astype(F32)[:, None] * freqs[None, :]
+    angles = timestep.astype(F32) * freqs[None, :]
     return jnp.concatenate([jnp.cos(angles), jnp.sin(angles)], axis=-1)
 
 
@@ -469,13 +469,15 @@
     lanes = 2 * channels + 128
     extent = 3 * tokens
 
+    half_freqs = teacher_mod.shape[0] // 2
+    time = lax.optimization_barrier(jnp.broadcast_to(timestep[:, None], (1, half_freqs)))
     tmod = jnp.einsum(
         "sf,fjd->sjd",
-        time_features(timestep, teacher_mod.shape[0]),
+        time_features(time, 2 * half_freqs),
         teacher_mod.astype(F32),
         precision=HIGHEST,
     )[0]
-    time_row = jnp.broadcast_to(timestep.astype(F32)[:, None], (8, tokens))
+    time_row = jnp.broadcast_to(time[:, :tokens].astype(F32), (8, tokens))
     ratio = seqs // mps
     rows = 2 * local_width // ratio
     pieces = local_width // 128

time: 139 us -> 139 us (level)
  no operation moved by 1% of the time
where the time goes in v7:
time: 139 us; the launch traced here: 138 us
  starting transfers between devices  63.9 us (46%)
  blocking collectives  51.6 us (37%)
  waiting for transfers between devices  12.5 us (9%)
  Pallas kernels  8.28 us (6%)
  between operations  1.55 us (1%)
    all_to_all x3, starting transfers between devices, exchange(): return lax.all_to_all(value, axes, 0, 0, tiled=False)  44.1 us
    all_to_all x3, blocking collectives, exchange(): return lax.all_to_all(value, axes, 0, 0, tiled=False)  42.1 us
    ppermute x3, starting transfers between devices, per_device(): sums = sums + lax.ppermute(sums, 'mp', [(i, i ^ hop) for i in range(mps)])  17.3 us
    ppermute x3, waiting for transfers between devices, per_device(): sums = sums + lax.ppermute(sums, 'mp', [(i, i ^ hop) for i in range(mps)])  8.28 us
    pallas_call x9, Pallas kernels, call(): pl.pallas_call(body, in_specs=[smem] * len(scalars) + [vmem] * len(arrays...  8.28 us
    all_gather x1, blocking collectives, per_device(): pair = lax.all_gather(noised, 'core', axis=0, tiled=True)  5.16 us
    all_to_all x3, waiting for transfers between devices, exchange(): return lax.all_to_all(value, axes, 0, 0, tiled=False)  4.16 us
  transfers between devices with their start and end apart: 8, of which 4 were waited for; matrix products, arithmetic and copies ran while one was open for 0% of the time, Pallas kernels for 1%

profile of v7, /device:TPU:24, one launch (start us, length us, event | category | flops | bytes accessed | tf_op | source)
XLA Modules:
  0.0 138.5 jit_solution(10553492191765126354)
XLA Ops:
  0.6 0.0 copy-start
  0.6 0.0 copy-start.1
  1.4 0.1 fusion.6
  1.4 0.2 copy-done
  1.6 0.3 fusion
  1.9 0.0 copy-done.1
  1.9 0.0 copy-start.5
  1.9 0.0 copy-start.6
  2.0 1.9 %shard_map.157 = (bf16[192,384]{1,0:T(8,128)(2,1)S(1)}, bf16[64,3,128]{2,1,0:T(4,128)(2,1)}, bf16[8,32,128]{2,1,0:T(8,128)(2,1)S(1)}, f32[64,16]{1,0:T(8,128)S(1)}, bf16[64,128]{1,0:T(8,128)(2,1)S(1)}) custom-call(s32[1,4]{1,0:T(1,128)} %disc_ref.3, f32[2,96]{1,0:T(2,128)} %cond_ref.1, bf16[96,384]{1,0:T(8,128)(2,1)} %bitcast.33, f32[2,384]{1,0:T(2,128)S(1)} %bitcast.31, ...), custom_call_target="tpu_custom_call" | custom-call | tf_op jit(solution)/shard_map/pallas_call | solution.py:79
  3.8 10.5 %all-to-all-start = ((bf16[64,3,128]{2,1,0:T(4,128)(2,1)}), bf16[64,3,128]{2,1,0:T(4,128)(2,1)S(1)}, u32[]{:S(2)}, u32[]{:S(2)}) async-start(bf16[64,3,128]{2,1,0:T(4,128)(2,1)} %get-tuple-element.23), calls=%async_computation | async-start | bytes 131072 | tf_op jit(solution)/shard_map/all_to_all | solution.py:62
  14.3 0.7 collective-permute-start.4
  15.0 0.0 copy-done.5
  15.0 0.0 copy-done.6
  15.0 2.2 %all_gather.10.pair_ref = bf16[384,768]{1,0:T(8,128)(2,1)S(1)} all-gather(bf16[192,768]{1,0:T(8,128)(2,1)S(1)} %pad_maximum_fusion), channel_id=1, replica_groups=mesh['group'=2,'plane'=16,'core'=2,'mp'=8] {'core'}, dimensions={0}, use_global_device_ids=true | all-gather | bytes 884736 | tf_op jit(solution)/shard_map/all_gather | solution.py:522
  17.2 4.2 %all-to-all-done.mod_ref.order_ref = bf16[64,3,128]{2,1,0:T(4,128)(2,1)S(1)} async-done(((bf16[64,3,128]{2,1,0:T(4,128)(2,1)}), bf16[64,3,128]{2,1,0:T(4,128)(2,1)S(1)}, u32[]{:S(2)}, u32[]{:S(2)}) %all-to-all-start) | async-done | bytes 49184 | tf_op jit(solution)/shard_map/all_to_all | solution.py:62
  21.4 0.0 collective-permute-done.4.got_ref
  21.4 1.1 shard_map.160
  22.5 0.0 copy-start.2
  22.5 0.0 copy-start.3
  22.5 0.0 copy-start.4
  22.5 24.0 %all-to-all-start.1 = ((bf16[16,32,256]{2,1,0:T(8,128)(2,1)}), bf16[16,32,256]{2,1,0:T(8,128)(2,1)S(1)}, u32[]{:S(2)}, u32[]{:S(2)}) async-start(bf16[16,32,256]{2,1,0:T(8,128)(2,1)} %shard_map.160), calls=%async_computation.1 | async-start | bytes 524288 | tf_op jit(solution)/shard_map/all_to_all | solution.py:62
  46.5 0.0 copy-done.2
  46.5 0.0 copy-done.3
  46.5 0.0 copy-done.4
  46.5 0.4 shard_map.158
  47.0 4.9 %collective-permute-start = (f32[104,128]{1,0:T(8,128)S(1)}, f32[104,128]{1,0:T(8,128)S(1)}, u32[]{:S(2)}, u32[]{:S(2)}) collective-permute-start(f32[104,128]{1,0:T(8,128)S(1)} %shard_map.158), channel_id=1, source_target_pairs={{0,2},{1,3},{2,0},{3,1},{4,6},{5,7},{6,4},{7,5},{8,10},{9,11},{10,... | collective-permute-start | bytes 159752 | tf_op jit(solution)/shard_map/ppermute | solution.py:540
  51.9 2.1 %collective-permute-done = f32[104,128]{1,0:T(8,128)S(1)} collective-permute-done((f32[104,128]{1,0:T(8,128)S(1)}, f32[104,128]{1,0:T(8,128)S(1)}, u32[]{:S(2)}, u32[]{:S(2)}) %collective-permute-start) | collective-permute-done | bytes 53280 | tf_op jit(solution)/shard_map/ppermute | solution.py:540
  54.0 1.9 %collective-permute-start.1 = (f32[104,128]{1,0:T(8,128)S(1)}, f32[104,128]{1,0:T(8,128)S(1)}, u32[]{:S(2)}, u32[]{:S(2)}) collective-permute-start(f32[104,128]{1,0:T(8,128)S(1)} %add.9), channel_id=1, source_target_pairs={{0,1},{1,0},{2,3},{3,2},{4,5},{5,4},{6,7},{7,6},{8,9},{9,8},{10,11... | collective-permute-start | bytes 159752 | tf_op jit(solution)/shard_map/ppermute | solution.py:540
  55.9 4.1 %collective-permute-done.1 = f32[104,128]{1,0:T(8,128)S(1)} collective-permute-done((f32[104,128]{1,0:T(8,128)S(1)}, f32[104,128]{1,0:T(8,128)S(1)}, u32[]{:S(2)}, u32[]{:S(2)}) %collective-permute-start.1) | collective-permute-done | bytes 53280 | tf_op jit(solution)/shard_map/ppermute | solution.py:540
  60.0 0.0 all-to-all-done.1.parts_ref
  60.0 0.8 shard_map.161
  60.8 9.6 %all-to-all-start.2 = ((bf16[16,32,256]{2,1,0:T(8,128)(2,1)}), bf16[16,32,256]{2,1,0:T(8,128)(2,1)S(1)}, u32[]{:S(2)}, u32[]{:S(2)}) async-start(bf16[16,32,256]{2,1,0:T(8,128)(2,1)} %shard_map.161), calls=%async_computation.2 | async-start | bytes 524288 | tf_op jit(solution)/shard_map/all_to_all | solution.py:62
  70.4 10.5 %collective-permute-start.2 = (f32[104,128]{1,0:T(8,128)S(1)}, f32[104,128]{1,0:T(8,128)S(1)}, u32[]{:S(2)}, u32[]{:S(2)}) collective-permute-start(f32[104,128]{1,0:T(8,128)S(1)} %add.10.order_ref), channel_id=1, source_target_pairs={{0,4},{1,5},{2,6},{3,7},{4,0},{5,1},{6,2},{7,3},{8,12},{9,13},{10,... | collective-permute-start | bytes 159752 | tf_op jit(solution)/shard_map/ppermute | solution.py:540
  80.9 2.1 %collective-permute-done.2 = f32[104,128]{1,0:T(8,128)S(1)} collective-permute-done((f32[104,128]{1,0:T(8,128)S(1)}, f32[104,128]{1,0:T(8,128)S(1)}, u32[]{:S(2)}, u32[]{:S(2)}) %collective-permute-start.2) | collective-permute-done | bytes 53280 | tf_op jit(solution)/shard_map/ppermute | solution.py:540
  83.0 0.3 shard_map.159
  83.3 1.9 %collective-permute-start.3 = (bf16[64,128]{1,0:T(8,128)(2,1)S(1)}, bf16[64,128]{1,0:T(8,128)(2,1)S(1)}, u32[]{:S(2)}, u32[]{:S(2)}) collective-permute-start(bf16[64,128]{1,0:T(8,128)(2,1)S(1)} %get-tuple-element.25.noised_ref), channel_id=1, source_target_pairs={{8,16},{16,8},{24,32},{32,24},{40,48},{48,40},{56,64},{64,56},{72,... | collective-permute-start | bytes 49160 | tf_op jit(solution)/shard_map/ppermute | solution.py:554
  85.3 5.2 %all_gather.9.pair_ref = bf16[128,128]{1,0:T(8,128)(2,1)S(1)} all-gather(bf16[64,128]{1,0:T(8,128)(2,1)S(1)} %get-tuple-element.25.noised_ref), channel_id=1, replica_groups=mesh['group'=2,'plane'=16,'core'=2,'mp'=8] {'core'}, dimensions={0}, use_global_device_ids=true | all-gather | bytes 49152 | tf_op jit(solution)/shard_map/all_gather | solution.py:555
  90.4 0.0 all-to-all-done.2
  90.4 2.2 %all_gather.11.weights_ref = bf16[32,32,256]{2,1,0:T(8,128)(2,1)S(1)} all-gather(bf16[16,32,256]{2,1,0:T(8,128)(2,1)S(1)} %all-to-all-done.2), channel_id=1, replica_groups=mesh['group'=2,'plane'=16,'core'=2,'mp'=8] {'core'}, dimensions={0}, use_global_device_ids=true | all-gather | bytes 786432 | tf_op jit(solution)/shard_map/all_gather | solution.py:545
  92.6 0.0 collective-permute-done.3.cross_noised_ref
  92.6 1.3 shard_map.162
  93.9 19.4 %all_to_all.30.parts_ref = bf16[8,32,512]{2,1,0:T(8,128)(2,1)S(1)} all-to-all(bf16[8,32,512]{2,1,0:T(8,128)(2,1)S(1)} %get-tuple-element.28), channel_id=1, replica_groups=mesh['group'=2,'plane'=16,'core'=2,'mp'=8] {'mp'}, dimensions={0} | all-to-all | bytes 524288 | tf_op jit(solution)/shard_map/all_to_all | solution.py:62
  113.3 0.7 shard_map.163
  114.0 11.2 %all_to_all.31.pay_ref = bf16[8,48,128]{2,1,0:T(8,128)(2,1)S(1)} all-to-all(bf16[8,48,128]{2,1,0:T(8,128)(2,1)S(1)} %get-tuple-element.31), channel_id=1, replica_groups=mesh['group'=2,'plane'=16,'core'=2,'mp'=8] {'mp'}, dimensions={0} | all-to-all | bytes 196608 | tf_op jit(solution)/shard_map/all_to_all | solution.py:62
  125.2 1.2 shard_map.164
  126.4 11.5 %all_to_all.32.parts_ref = bf16[8,64,128]{2,1,0:T(8,128)(2,1)S(1)} all-to-all(bf16[8,64,128]{2,1,0:T(8,128)(2,1)S(1)} %get-tuple-element.37), channel_id=1, replica_groups=mesh['group'=2,'plane'=16,'core'=2,'mp'=8] {'mp'}, dimensions={0} | all-to-all | bytes 262144 | tf_op jit(solution)/shard_map/all_to_all | solution.py:62
  137.9 0.6 shard_map.165
  (8 shorter events, 0.1 us)
Async XLA Ops:
  0.6 1.0 copy-start
  0.6 1.3 copy-start.1
  1.9 13.0 %copy-start.5 = (bf16[96,768]{1,0:T(8,128)(2,1)S(1)}, bf16[96,768]{1,0:T(8,128)(2,1)}, u32[]{:S(2)}) copy-start(bf16[96,768]{1,0:T(8,128)(2,1)} %param.22) | copy-start | bytes 442372
  1.9 13.0 %copy-start.6 = (bf16[768,96]{0,1:T(8,128)(2,1)S(1)}, bf16[768,96]{0,1:T(8,128)(2,1)}, u32[]{:S(2)}) copy-start(bf16[768,96]{0,1:T(8,128)(2,1)} %param.23) | copy-start | bytes 442372
  3.8 17.6 %all-to-all-start = ((bf16[64,3,128]{2,1,0:T(4,128)(2,1)}), bf16[64,3,128]{2,1,0:T(4,128)(2,1)S(1)}, u32[]{:S(2)}, u32[]{:S(2)}) async-start(bf16[64,3,128]{2,1,0:T(4,128)(2,1)} %get-tuple-element.23), calls=%async_computation | async-start | bytes 131072 | tf_op jit(solution)/shard_map/all_to_all | solution.py:62
  14.3 7.1 %collective-permute-start.4 = (bf16[192,384]{1,0:T(8,128)(2,1)S(1)}, bf16[192,384]{1,0:T(8,128)(2,1)S(1)}, u32[]{:S(2)}, u32[]{:S(2)}) collective-permute-start(bf16[192,384]{1,0:T(8,128)(2,1)S(1)} %get-tuple-element.26), channel_id=1, source_target_pairs={{0,0},{1,32},{2,64},{3,96},{4,128},{5,160},{6,192},{7,224},{8,8},{... | collective-permute-start | bytes 442376 | tf_op jit(solution)/shard_map/ppermute | solution.py:518
  22.5 24.0 %copy-start.2 = (bf16[64,384]{1,0:T(8,128)(2,1)S(1)}, bf16[64,384]{1,0:T(8,128)(2,1)}, u32[]{:S(2)}) copy-start(bf16[64,384]{1,0:T(8,128)(2,1)} %embed_ref.3) | copy-start | bytes 147460
  22.5 24.0 %copy-start.3 = (bf16[1,128,384]{2,1,0:T(8,128)(2,1)S(1)}, bf16[1,128,384]{2,1,0:T(8,128)(2,1)}, u32[]{:S(2)}) copy-start(bf16[1,128,384]{2,1,0:T(8,128)(2,1)} %param.14) | copy-start | bytes 294916
  22.5 24.0 %copy-start.4 = (bf16[384,64]{0,1:T(8,128)(2,1)S(1)}, bf16[384,64]{0,1:T(8,128)(2,1)}, u32[]{:S(2)}) copy-start(bf16[384,64]{0,1:T(8,128)(2,1)} %param.17) | copy-start | bytes 147460
  22.5 37.5 %all-to-all-start.1 = ((bf16[16,32,256]{2,1,0:T(8,128)(2,1)}), bf16[16,32,256]{2,1,0:T(8,128)(2,1)S(1)}, u32[]{:S(2)}, u32[]{:S(2)}) async-start(bf16[16,32,256]{2,1,0:T(8,128)(2,1)} %shard_map.160), calls=%async_computation.1 | async-start | bytes 524288 | tf_op jit(solution)/shard_map/all_to_all | solution.py:62
  47.0 7.0 %collective-permute-start = (f32[104,128]{1,0:T(8,128)S(1)}, f32[104,128]{1,0:T(8,128)S(1)}, u32[]{:S(2)}, u32[]{:S(2)}) collective-permute-start(f32[104,128]{1,0:T(8,128)S(1)} %shard_map.158), channel_id=1, source_target_pairs={{0,2},{1,3},{2,0},{3,1},{4,6},{5,7},{6,4},{7,5},{8,10},{9,11},{10,... | collective-permute-start | bytes 159752 | tf_op jit(solution)/shard_map/ppermute | solution.py:540
  54.0 6.0 %collective-permute-start.1 = (f32[104,128]{1,0:T(8,128)S(1)}, f32[104,128]{1,0:T(8,128)S(1)}, u32[]{:S(2)}, u32[]{:S(2)}) collective-permute-start(f32[104,128]{1,0:T(8,128)S(1)} %add.9), channel_id=1, source_target_pairs={{0,1},{1,0},{2,3},{3,2},{4,5},{5,4},{6,7},{7,6},{8,9},{9,8},{10,11... | collective-permute-start | bytes 159752 | tf_op jit(solution)/shard_map/ppermute | solution.py:540
  60.8 29.6 %all-to-all-start.2 = ((bf16[16,32,256]{2,1,0:T(8,128)(2,1)}), bf16[16,32,256]{2,1,0:T(8,128)(2,1)S(1)}, u32[]{:S(2)}, u32[]{:S(2)}) async-start(bf16[16,32,256]{2,1,0:T(8,128)(2,1)} %shard_map.161), calls=%async_computation.2 | async-start | bytes 524288 | tf_op jit(solution)/shard_map/all_to_all | solution.py:62
  70.4 12.6 %collective-permute-start.2 = (f32[104,128]{1,0:T(8,128)S(1)}, f32[104,128]{1,0:T(8,128)S(1)}, u32[]{:S(2)}, u32[]{:S(2)}) collective-permute-start(f32[104,128]{1,0:T(8,128)S(1)} %add.10.order_ref), channel_id=1, source_target_pairs={{0,4},{1,5},{2,6},{3,7},{4,0},{5,1},{6,2},{7,3},{8,12},{9,13},{10,... | collective-permute-start | bytes 159752 | tf_op jit(solution)/shard_map/ppermute | solution.py:540
  83.3 9.3 %collective-permute-start.3 = (bf16[64,128]{1,0:T(8,128)(2,1)S(1)}, bf16[64,128]{1,0:T(8,128)(2,1)S(1)}, u32[]{:S(2)}, u32[]{:S(2)}) collective-permute-start(bf16[64,128]{1,0:T(8,128)(2,1)S(1)} %get-tuple-element.25.noised_ref), channel_id=1, source_target_pairs={{8,16},{16,8},{24,32},{32,24},{40,48},{48,40},{56,64},{64,56},{72,... | collective-permute-start | bytes 49160 | tf_op jit(solution)/shard_map/ppermute | solution.py:554
